TPU v7x, 32 devices: a whole 2x2x4 slice. The times are simulated.
32 devices in a mesh: site: 4 (over y, x), sector: 8 (over z, core).
Axes of the slice: x: 2, y: 2, z: 4, core: 2. Of those that a mesh axis runs over, the one named last changes fastest.
Arguments:
- env_in: bfloat16 [2, 8, 512, 512], P(None, 'sector'), may hold values from -6 to 6
- bra: bfloat16 [4, 4, 8, 512, 512], P('site', None, 'sector'), may hold values from -0.25 to 0.25
- ket: bfloat16 [4, 2, 4, 8, 512, 512], P('site', None, None, 'sector'), may hold values from -0.125 to 0.125
- sector_dims: int32 [5, 8], replicated, may hold values from 384 to 512, as said below
- flags: int32 [4, 4, 8], P('site', None, 'sector'), may hold values 0 or 1
Outputs:
- env_after: bfloat16 [4, 2, 8, 512, 512], P('site', None, 'sector')
Inputs may be any that keep to these rules, and one draw needn't show every extreme that they name: `sector_dims`: every bond has some sector whose used size is exactly 512.
All inputs are finite; a program needn't handle non-finite values. No bound on the sum of `flags` on one device may be relied on, other than what follows from the above.
Results may differ from a plain program's by a relative error of at most 0.013.
Values may be sent and summed in bfloat16 or wider, within the bound.
No kernel may reach another device: no remote copies, remote signals or barrier semaphores. Data moves between devices by JAX's collectives and lax.ppermute only.
A program may use at most 64 MiB of HBM per device.

v0:
```python
import jax
import jax.numpy as jnp
from jax import lax
from jax.sharding import PartitionSpec as P


def shifted(array, axis, by):
    count = lax.axis_size(axis)
    pairs = [(i, i + by) for i in range(count) if 0 <= i + by < count]
    return lax.ppermute(array, axis, pairs)


def per_device(env_in, bra, ket, sector_dims, flags):
    sections = lax.axis_size("site")
    section = lax.axis_index("site")
    sector = lax.axis_index("sector")
    pairs = ket.shape[1]
    width = ket.shape[-1]
    lanes = jnp.arange(width)
    dims_here = lax.dynamic_index_in_dim(sector_dims, sector, 1, keepdims=False)
    keep_first = (lanes < dims_here[0]).astype(jnp.float32)
    first_window = keep_first[:, None] * keep_first[None, :]
    dim_next = lax.dynamic_index_in_dim(dims_here, section + 1, 0, keepdims=False)
    keep_next = (lanes < dim_next).astype(jnp.float32)
    next_window = keep_next[:, None] * keep_next[None, :]
    bra_here = bra[0, :, 0]
    ket_here = ket[0, :, :, 0]
    flag_here = flags[0, :, 0].astype(jnp.float32)

    def advance(step, carry):
        held, result = carry
        pair = step - section
        valid = jnp.logical_and(pair >= 0, pair < pairs)
        chosen = jnp.clip(pair, 0, pairs - 1)
        entering = lax.dynamic_index_in_dim(
            env_in, jnp.minimum(step, pairs - 1), 0, keepdims=False
        )[0]
        entering = (entering.astype(jnp.float32) * first_window).astype(jnp.bfloat16)
        current = jnp.where(section == 0, entering, held)
        kets = lax.dynamic_index_in_dim(ket_here, chosen, 0, keepdims=False)
        moved = jnp.einsum("ab,sbc->sac", current, kets, preferred_element_type=jnp.float32).astype(
            jnp.bfloat16
        )
        parts = (
            jnp.einsum("sba,sbc->sac", bra_here, moved, preferred_element_type=jnp.float32)
            * flag_here[:, None, None]
        )
        single = shifted(parts[1] + parts[2], "sector", 1)
        double = shifted(parts[3], "sector", 2)
        total = (parts[0] + single + double) * next_window
        fresh = total.astype(jnp.bfloat16)
        updated = lax.dynamic_update_index_in_dim(result, fresh[None], chosen, 0)
        result = jnp.where(valid, updated, result)
        held = shifted(fresh, "site", 1)
        return (held, result)

    held_start = jnp.zeros((width, width), jnp.bfloat16)
    result_start = jnp.zeros((pairs, 1, width, width), jnp.bfloat16)
    held_end, result_end = lax.fori_loop(
        0, pairs + sections - 1, advance, (held_start, result_start)
    )
    return result_end[None]


def solution(mesh):
    in_specs = (
        P(None, "sector", None, None),
        P("site", None, "sector", None, None),
        P("site", None, None, "sector", None, None),
        P(),
        P("site", None, "sector"),
    )
    out_specs = P("site", None, "sector", None, None)
    return jax.shard_map(
        per_device, mesh=mesh, in_specs=in_specs, out_specs=out_specs, check_vma=False
    )
```

profile of v0, /device:TPU:14, one launch (start us, length us, event | category | flops | bytes accessed | tf_op | source)
XLA Modules:
  0.0 324.0 jit_solution(1189235261089442128)
XLA Ops:
  6.5 317.5 %while.17 = (s32[]{:T(128)}, bf16[512,512]{0,1:T(8,128)(2,1)}, bf16[2,1,512,512]{3,2,0,1:T(8,128)(2,1)}, s32[]{:T(128)}, bf16[2,4,512,512]{3,2,1,0:T(8,128)(2,1)...) while((s32[]{:T(128)}, bf16[512,512]{0,1:T(8,128)(2,1)}, ...), condition=%wide.region_1.2_spmd.clone, body=%wide.region_0.1_spmd.clone.sunk | while | flops 2152726528 | bytes 36185460 | solution.py:59
  7.8 6.8 %multiply_bitcast_fusion.2 = f32[4,512,512]{1,2,0:T(8,128)} fusion(bf16[4,512,512]{2,1,0:T(8,128)(2,1)} %get-tuple-element.396, f32[4]{0:T(128)S(1)} %get-tuple-element.397, bf16[2,4,512,512]{3,2,1,0:T(8,128)(2,1)} %get-tuple-element.393, s32[]{:T(128)S(6)} %min.21, bf16[512,512]{0,1:T(8,128)(2,1)} %get-tuple-element.376, ...), kind=kOutput, calls=%fused_computation.2.clone.1 | convolution fusion | flops 2150891520 | bytes 9442308 | tf_op jit(solution)/shard_map/while/body/eval_jaxpr/sba,sbc->sac/dot_general | solution.py:45
  16.8 3.5 %collective-permute-start = (f32[512,512]{0,1:T(8,128)S(1)}, f32[512,512]{0,1:T(8,128)}, u32[]{:S(2)}, u32[]{:S(2)}) collective-permute-start(f32[512,512]{0,1:T(8,128)S(1)} %get-tuple-element.357), channel_id=1, source_target_pairs={{0,2},{1,3},{2,4},{3,5},{4,6},{5,7},{8,10},{9,11},{10,12},{11,13},... | collective-permute-start | bytes 3145736 | tf_op jit(solution)/shard_map/while/body/eval_jaxpr/ppermute | solution.py:10
  23.6 21.3 %collective-permute-done = f32[512,512]{0,1:T(8,128)} collective-permute-done((f32[512,512]{0,1:T(8,128)S(1)}, f32[512,512]{0,1:T(8,128)}, u32[]{:S(2)}, u32[]{:S(2)}) %collective-permute-start) | collective-permute-done | bytes 1048608 | tf_op jit(solution)/shard_map/while/body/eval_jaxpr/ppermute | solution.py:10
  44.9 10.1 %collective-permute-done.1 = f32[512,512]{0,1:T(8,128)} collective-permute-done((f32[512,512]{0,1:T(8,128)S(1)}, f32[512,512]{0,1:T(8,128)}, u32[]{:S(2)}, u32[]{:S(2)}) %collective-permute-start.1) | collective-permute-done | bytes 1048608 | tf_op jit(solution)/shard_map/while/body/eval_jaxpr/ppermute | solution.py:10
  59.5 12.6 %collective-permute-done.2 = bf16[512,512]{0,1:T(8,128)(2,1)} collective-permute-done((bf16[512,512]{0,1:T(8,128)(2,1)S(1)}, bf16[512,512]{0,1:T(8,128)(2,1)}, u32[]{:S(2)}, u32[]{:S(2)}) %collective-permute-start.2) | collective-permute-done | bytes 524320 | tf_op jit(solution)/shard_map/while/body/eval_jaxpr/ppermute | solution.py:10
  73.4 6.8 %multiply_bitcast_fusion.2 = f32[4,512,512]{1,2,0:T(8,128)} fusion(bf16[4,512,512]{2,1,0:T(8,128)(2,1)} %get-tuple-element.396, f32[4]{0:T(128)S(1)} %get-tuple-element.397, bf16[2,4,512,512]{3,2,1,0:T(8,128)(2,1)} %get-tuple-element.393, s32[]{:T(128)S(6)} %min.21, bf16[512,512]{0,1:T(8,128)(2,1)} %get-tuple-element.376, ...), kind=kOutput, calls=%fused_computation.2.clone.1 | convolution fusion | flops 2150891520 | bytes 9442308 | tf_op jit(solution)/shard_map/while/body/eval_jaxpr/sba,sbc->sac/dot_general | solution.py:45
  82.4 3.5 %collective-permute-start = (f32[512,512]{0,1:T(8,128)S(1)}, f32[512,512]{0,1:T(8,128)}, u32[]{:S(2)}, u32[]{:S(2)}) collective-permute-start(f32[512,512]{0,1:T(8,128)S(1)} %get-tuple-element.357), channel_id=1, source_target_pairs={{0,2},{1,3},{2,4},{3,5},{4,6},{5,7},{8,10},{9,11},{10,12},{11,13},... | collective-permute-start | bytes 3145736 | tf_op jit(solution)/shard_map/while/body/eval_jaxpr/ppermute | solution.py:10
  89.1 21.3 %collective-permute-done = f32[512,512]{0,1:T(8,128)} collective-permute-done((f32[512,512]{0,1:T(8,128)S(1)}, f32[512,512]{0,1:T(8,128)}, u32[]{:S(2)}, u32[]{:S(2)}) %collective-permute-start) | collective-permute-done | bytes 1048608 | tf_op jit(solution)/shard_map/while/body/eval_jaxpr/ppermute | solution.py:10
  110.4 8.5 %collective-permute-done.1 = f32[512,512]{0,1:T(8,128)} collective-permute-done((f32[512,512]{0,1:T(8,128)S(1)}, f32[512,512]{0,1:T(8,128)}, u32[]{:S(2)}, u32[]{:S(2)}) %collective-permute-start.1) | collective-permute-done | bytes 1048608 | tf_op jit(solution)/shard_map/while/body/eval_jaxpr/ppermute | solution.py:10
  123.5 12.6 %collective-permute-done.2 = bf16[512,512]{0,1:T(8,128)(2,1)} collective-permute-done((bf16[512,512]{0,1:T(8,128)(2,1)S(1)}, bf16[512,512]{0,1:T(8,128)(2,1)}, u32[]{:S(2)}, u32[]{:S(2)}) %collective-permute-start.2) | collective-permute-done | bytes 524320 | tf_op jit(solution)/shard_map/while/body/eval_jaxpr/ppermute | solution.py:10
  137.4 6.8 %multiply_bitcast_fusion.2 = f32[4,512,512]{1,2,0:T(8,128)} fusion(bf16[4,512,512]{2,1,0:T(8,128)(2,1)} %get-tuple-element.396, f32[4]{0:T(128)S(1)} %get-tuple-element.397, bf16[2,4,512,512]{3,2,1,0:T(8,128)(2,1)} %get-tuple-element.393, s32[]{:T(128)S(6)} %min.21, bf16[512,512]{0,1:T(8,128)(2,1)} %get-tuple-element.376, ...), kind=kOutput, calls=%fused_computation.2.clone.1 | convolution fusion | flops 2150891520 | bytes 9442308 | tf_op jit(solution)/shard_map/while/body/eval_jaxpr/sba,sbc->sac/dot_general | solution.py:45
  146.4 2.2 collective-permute-start
  151.9 22.6 %collective-permute-done = f32[512,512]{0,1:T(8,128)} collective-permute-done((f32[512,512]{0,1:T(8,128)S(1)}, f32[512,512]{0,1:T(8,128)}, u32[]{:S(2)}, u32[]{:S(2)}) %collective-permute-start) | collective-permute-done | bytes 1048608 | tf_op jit(solution)/shard_map/while/body/eval_jaxpr/ppermute | solution.py:10
  174.4 8.5 %collective-permute-done.1 = f32[512,512]{0,1:T(8,128)} collective-permute-done((f32[512,512]{0,1:T(8,128)S(1)}, f32[512,512]{0,1:T(8,128)}, u32[]{:S(2)}, u32[]{:S(2)}) %collective-permute-start.1) | collective-permute-done | bytes 1048608 | tf_op jit(solution)/shard_map/while/body/eval_jaxpr/ppermute | solution.py:10
  187.5 11.9 %collective-permute-done.2 = bf16[512,512]{0,1:T(8,128)(2,1)} collective-permute-done((bf16[512,512]{0,1:T(8,128)(2,1)S(1)}, bf16[512,512]{0,1:T(8,128)(2,1)}, u32[]{:S(2)}, u32[]{:S(2)}) %collective-permute-start.2) | collective-permute-done | bytes 524320 | tf_op jit(solution)/shard_map/while/body/eval_jaxpr/ppermute | solution.py:10
  200.7 6.8 %multiply_bitcast_fusion.2 = f32[4,512,512]{1,2,0:T(8,128)} fusion(bf16[4,512,512]{2,1,0:T(8,128)(2,1)} %get-tuple-element.396, f32[4]{0:T(128)S(1)} %get-tuple-element.397, bf16[2,4,512,512]{3,2,1,0:T(8,128)(2,1)} %get-tuple-element.393, s32[]{:T(128)S(6)} %min.21, bf16[512,512]{0,1:T(8,128)(2,1)} %get-tuple-element.376, ...), kind=kOutput, calls=%fused_computation.2.clone.1 | convolution fusion | flops 2150891520 | bytes 9442308 | tf_op jit(solution)/shard_map/while/body/eval_jaxpr/sba,sbc->sac/dot_general | solution.py:45
  214.9 22.9 %collective-permute-done = f32[512,512]{0,1:T(8,128)} collective-permute-done((f32[512,512]{0,1:T(8,128)S(1)}, f32[512,512]{0,1:T(8,128)}, u32[]{:S(2)}, u32[]{:S(2)}) %collective-permute-start) | collective-permute-done | bytes 1048608 | tf_op jit(solution)/shard_map/while/body/eval_jaxpr/ppermute | solution.py:10
  237.7 7.5 %collective-permute-done.1 = f32[512,512]{0,1:T(8,128)} collective-permute-done((f32[512,512]{0,1:T(8,128)S(1)}, f32[512,512]{0,1:T(8,128)}, u32[]{:S(2)}, u32[]{:S(2)}) %collective-permute-start.1) | collective-permute-done | bytes 1048608 | tf_op jit(solution)/shard_map/while/body/eval_jaxpr/ppermute | solution.py:10
  249.8 11.9 %collective-permute-done.2 = bf16[512,512]{0,1:T(8,128)(2,1)} collective-permute-done((bf16[512,512]{0,1:T(8,128)(2,1)S(1)}, bf16[512,512]{0,1:T(8,128)(2,1)}, u32[]{:S(2)}, u32[]{:S(2)}) %collective-permute-start.2) | collective-permute-done | bytes 524320 | tf_op jit(solution)/shard_map/while/body/eval_jaxpr/ppermute | solution.py:10
  263.0 6.8 %multiply_bitcast_fusion.2 = f32[4,512,512]{1,2,0:T(8,128)} fusion(bf16[4,512,512]{2,1,0:T(8,128)(2,1)} %get-tuple-element.396, f32[4]{0:T(128)S(1)} %get-tuple-element.397, bf16[2,4,512,512]{3,2,1,0:T(8,128)(2,1)} %get-tuple-element.393, s32[]{:T(128)S(6)} %min.21, bf16[512,512]{0,1:T(8,128)(2,1)} %get-tuple-element.376, ...), kind=kOutput, calls=%fused_computation.2.clone.1 | convolution fusion | flops 2150891520 | bytes 9442308 | tf_op jit(solution)/shard_map/while/body/eval_jaxpr/sba,sbc->sac/dot_general | solution.py:45
  277.2 22.9 %collective-permute-done = f32[512,512]{0,1:T(8,128)} collective-permute-done((f32[512,512]{0,1:T(8,128)S(1)}, f32[512,512]{0,1:T(8,128)}, u32[]{:S(2)}, u32[]{:S(2)}) %collective-permute-start) | collective-permute-done | bytes 1048608 | tf_op jit(solution)/shard_map/while/body/eval_jaxpr/ppermute | solution.py:10
  300.1 7.5 %collective-permute-done.1 = f32[512,512]{0,1:T(8,128)} collective-permute-done((f32[512,512]{0,1:T(8,128)S(1)}, f32[512,512]{0,1:T(8,128)}, u32[]{:S(2)}, u32[]{:S(2)}) %collective-permute-start.1) | collective-permute-done | bytes 1048608 | tf_op jit(solution)/shard_map/while/body/eval_jaxpr/ppermute | solution.py:10
  312.1 11.9 %collective-permute-done.2 = bf16[512,512]{0,1:T(8,128)(2,1)} collective-permute-done((bf16[512,512]{0,1:T(8,128)(2,1)S(1)}, bf16[512,512]{0,1:T(8,128)(2,1)}, u32[]{:S(2)}, u32[]{:S(2)}) %collective-permute-start.2) | collective-permute-done | bytes 524320 | tf_op jit(solution)/shard_map/while/body/eval_jaxpr/ppermute | solution.py:10
  (59 shorter events, 66.4 us)
Async XLA Ops:
  16.8 28.0 %collective-permute-start = (f32[512,512]{0,1:T(8,128)S(1)}, f32[512,512]{0,1:T(8,128)}, u32[]{:S(2)}, u32[]{:S(2)}) collective-permute-start(f32[512,512]{0,1:T(8,128)S(1)} %get-tuple-element.357), channel_id=1, source_target_pairs={{0,2},{1,3},{2,4},{3,5},{4,6},{5,7},{8,10},{9,11},{10,12},{11,13},... | collective-permute-start | bytes 3145736 | tf_op jit(solution)/shard_map/while/body/eval_jaxpr/ppermute | solution.py:10
  20.3 34.6 %collective-permute-start.1 = (f32[512,512]{0,1:T(8,128)S(1)}, f32[512,512]{0,1:T(8,128)}, u32[]{:S(2)}, u32[]{:S(2)}) collective-permute-start(f32[512,512]{0,1:T(8,128)S(1)} %get-tuple-element.358), channel_id=1, source_target_pairs={{0,1},{1,2},{2,3},{3,4},{4,5},{5,6},{6,7},{8,9},{9,10},{10,11},{11... | collective-permute-start | bytes 3145736 | tf_op jit(solution)/shard_map/while/body/eval_jaxpr/ppermute | solution.py:10
  57.2 14.9 %collective-permute-start.2 = (bf16[512,512]{0,1:T(8,128)(2,1)S(1)}, bf16[512,512]{0,1:T(8,128)(2,1)}, u32[]{:S(2)}, u32[]{:S(2)}) collective-permute-start(bf16[512,512]{0,1:T(8,128)(2,1)S(1)} %get-tuple-element.359), channel_id=1, source_target_pairs={{0,8},{8,16},{16,24},{1,9},{9,17},{17,25},{2,10},{10,18},{18,26},{... | collective-permute-start | bytes 1572872 | tf_op jit(solution)/shard_map/while/body/eval_jaxpr/ppermute | solution.py:10
  82.4 28.0 %collective-permute-start = (f32[512,512]{0,1:T(8,128)S(1)}, f32[512,512]{0,1:T(8,128)}, u32[]{:S(2)}, u32[]{:S(2)}) collective-permute-start(f32[512,512]{0,1:T(8,128)S(1)} %get-tuple-element.357), channel_id=1, source_target_pairs={{0,2},{1,3},{2,4},{3,5},{4,6},{5,7},{8,10},{9,11},{10,12},{11,13},... | collective-permute-start | bytes 3145736 | tf_op jit(solution)/shard_map/while/body/eval_jaxpr/ppermute | solution.py:10
  85.9 33.0 %collective-permute-start.1 = (f32[512,512]{0,1:T(8,128)S(1)}, f32[512,512]{0,1:T(8,128)}, u32[]{:S(2)}, u32[]{:S(2)}) collective-permute-start(f32[512,512]{0,1:T(8,128)S(1)} %get-tuple-element.358), channel_id=1, source_target_pairs={{0,1},{1,2},{2,3},{3,4},{4,5},{5,6},{6,7},{8,9},{9,10},{10,11},{11... | collective-permute-start | bytes 3145736 | tf_op jit(solution)/shard_map/while/body/eval_jaxpr/ppermute | solution.py:10
  121.1 14.9 %collective-permute-start.2 = (bf16[512,512]{0,1:T(8,128)(2,1)S(1)}, bf16[512,512]{0,1:T(8,128)(2,1)}, u32[]{:S(2)}, u32[]{:S(2)}) collective-permute-start(bf16[512,512]{0,1:T(8,128)(2,1)S(1)} %get-tuple-element.359), channel_id=1, source_target_pairs={{0,8},{8,16},{16,24},{1,9},{9,17},{17,25},{2,10},{10,18},{18,26},{... | collective-permute-start | bytes 1572872 | tf_op jit(solution)/shard_map/while/body/eval_jaxpr/ppermute | solution.py:10
  146.4 28.0 %collective-permute-start = (f32[512,512]{0,1:T(8,128)S(1)}, f32[512,512]{0,1:T(8,128)}, u32[]{:S(2)}, u32[]{:S(2)}) collective-permute-start(f32[512,512]{0,1:T(8,128)S(1)} %get-tuple-element.357), channel_id=1, source_target_pairs={{0,2},{1,3},{2,4},{3,5},{4,6},{5,7},{8,10},{9,11},{10,12},{11,13},... | collective-permute-start | bytes 3145736 | tf_op jit(solution)/shard_map/while/body/eval_jaxpr/ppermute | solution.py:10
  148.6 34.3 %collective-permute-start.1 = (f32[512,512]{0,1:T(8,128)S(1)}, f32[512,512]{0,1:T(8,128)}, u32[]{:S(2)}, u32[]{:S(2)}) collective-permute-start(f32[512,512]{0,1:T(8,128)S(1)} %get-tuple-element.358), channel_id=1, source_target_pairs={{0,1},{1,2},{2,3},{3,4},{4,5},{5,6},{6,7},{8,9},{9,10},{10,11},{11... | collective-permute-start | bytes 3145736 | tf_op jit(solution)/shard_map/while/body/eval_jaxpr/ppermute | solution.py:10
  185.1 14.2 %collective-permute-start.2 = (bf16[512,512]{0,1:T(8,128)(2,1)S(1)}, bf16[512,512]{0,1:T(8,128)(2,1)}, u32[]{:S(2)}, u32[]{:S(2)}) collective-permute-start(bf16[512,512]{0,1:T(8,128)(2,1)S(1)} %get-tuple-element.359), channel_id=1, source_target_pairs={{0,8},{8,16},{16,24},{1,9},{9,17},{17,25},{2,10},{10,18},{18,26},{... | collective-permute-start | bytes 1572872 | tf_op jit(solution)/shard_map/while/body/eval_jaxpr/ppermute | solution.py:10
  209.7 28.0 %collective-permute-start = (f32[512,512]{0,1:T(8,128)S(1)}, f32[512,512]{0,1:T(8,128)}, u32[]{:S(2)}, u32[]{:S(2)}) collective-permute-start(f32[512,512]{0,1:T(8,128)S(1)} %get-tuple-element.357), channel_id=1, source_target_pairs={{0,2},{1,3},{2,4},{3,5},{4,6},{5,7},{8,10},{9,11},{10,12},{11,13},... | collective-permute-start | bytes 3145736 | tf_op jit(solution)/shard_map/while/body/eval_jaxpr/ppermute | solution.py:10
  211.6 33.6 %collective-permute-start.1 = (f32[512,512]{0,1:T(8,128)S(1)}, f32[512,512]{0,1:T(8,128)}, u32[]{:S(2)}, u32[]{:S(2)}) collective-permute-start(f32[512,512]{0,1:T(8,128)S(1)} %get-tuple-element.358), channel_id=1, source_target_pairs={{0,1},{1,2},{2,3},{3,4},{4,5},{5,6},{6,7},{8,9},{9,10},{10,11},{11... | collective-permute-start | bytes 3145736 | tf_op jit(solution)/shard_map/while/body/eval_jaxpr/ppermute | solution.py:10
  247.4 14.3 %collective-permute-start.2 = (bf16[512,512]{0,1:T(8,128)(2,1)S(1)}, bf16[512,512]{0,1:T(8,128)(2,1)}, u32[]{:S(2)}, u32[]{:S(2)}) collective-permute-start(bf16[512,512]{0,1:T(8,128)(2,1)S(1)} %get-tuple-element.359), channel_id=1, source_target_pairs={{0,8},{8,16},{16,24},{1,9},{9,17},{17,25},{2,10},{10,18},{18,26},{... | collective-permute-start | bytes 1572872 | tf_op jit(solution)/shard_map/while/body/eval_jaxpr/ppermute | solution.py:10
  272.0 28.0 %collective-permute-start = (f32[512,512]{0,1:T(8,128)S(1)}, f32[512,512]{0,1:T(8,128)}, u32[]{:S(2)}, u32[]{:S(2)}) collective-permute-start(f32[512,512]{0,1:T(8,128)S(1)} %get-tuple-element.357), channel_id=1, source_target_pairs={{0,2},{1,3},{2,4},{3,5},{4,6},{5,7},{8,10},{9,11},{10,12},{11,13},... | collective-permute-start | bytes 3145736 | tf_op jit(solution)/shard_map/while/body/eval_jaxpr/ppermute | solution.py:10
  274.0 33.6 %collective-permute-start.1 = (f32[512,512]{0,1:T(8,128)S(1)}, f32[512,512]{0,1:T(8,128)}, u32[]{:S(2)}, u32[]{:S(2)}) collective-permute-start(f32[512,512]{0,1:T(8,128)S(1)} %get-tuple-element.358), channel_id=1, source_target_pairs={{0,1},{1,2},{2,3},{3,4},{4,5},{5,6},{6,7},{8,9},{9,10},{10,11},{11... | collective-permute-start | bytes 3145736 | tf_op jit(solution)/shard_map/while/body/eval_jaxpr/ppermute | solution.py:10
  309.8 14.3 %collective-permute-start.2 = (bf16[512,512]{0,1:T(8,128)(2,1)S(1)}, bf16[512,512]{0,1:T(8,128)(2,1)}, u32[]{:S(2)}, u32[]{:S(2)}) collective-permute-start(bf16[512,512]{0,1:T(8,128)(2,1)S(1)} %get-tuple-element.359), channel_id=1, source_target_pairs={{0,8},{8,16},{16,24},{1,9},{9,17},{17,25},{2,10},{10,18},{18,26},{... | collective-permute-start | bytes 1572872 | tf_op jit(solution)/shard_map/while/body/eval_jaxpr/ppermute | solution.py:10
where the time goes:
time: 327 us; the launch traced here: 324 us
  waiting for transfers between devices  214 us (65%)
  matrix products  34.2 us (10%)
  starting transfers between devices  29.1 us (9%)
  other arithmetic  23.8 us (7%)
  local copies, waits for them, and re-layouts  22.6 us (7%)
    ppermute x15, waiting for transfers between devices, shifted(): return lax.ppermute(array, axis, pairs)  214 us
    dot_general x5, matrix products, advance(): jnp.einsum('sba,sbc->sac', bra_here, moved, preferred_element_type=jnp.fl...  34.2 us
    ppermute x15, starting transfers between devices, shifted(): return lax.ppermute(array, axis, pairs)  29.1 us
    select_n x20, local copies, waits for them, and re-layouts, advance(): result = jnp.where(valid, updated, result)  11.7 us
    add x5, other arithmetic, advance(): single = shifted(parts[1] + parts[2], 'sector', 1)  10.9 us
    select_n x5, other arithmetic, advance(): result = jnp.where(valid, updated, result)  10.9 us
  transfers between devices with their start and end apart: 15, of which 15 were waited for; matrix products, arithmetic and copies ran while one was open for 4% of the time, Pallas kernels for 0%

commit v1 on v0

v1 whole, which is shorter than its diff:
```python
import functools

import jax
import jax.numpy as jnp
from jax import lax
from jax.experimental import pallas as pl
from jax.experimental.pallas import tpu as pltpu
from jax.sharding import PartitionSpec as P

CHUNKS = 2
AXES = ("site", "sector")
LIMIT = 20 << 20
SMEM = pl.BlockSpec(memory_space=pltpu.SMEM)
VMEM = pl.BlockSpec(memory_space=pltpu.VMEM)
ANY = pl.BlockSpec(memory_space=pl.ANY)


def bounds(width):
    tile = 16
    return [width * k // CHUNKS // tile * tile for k in range(CHUNKS + 1)]


def across(a, b):
    return lax.dot_general(a, b, (((1,), (0,)), ((), ())), preferred_element_type=jnp.float32)


def down(a, b):
    return lax.dot_general(a, b, (((0,), (0,)), ((), ())), preferred_element_type=jnp.float32)


def inside(shape, row, used):
    rows = lax.broadcasted_iota(jnp.int32, shape, 0) + row
    lanes = lax.broadcasted_iota(jnp.int32, shape, 1)
    return jnp.logical_and(rows < used, lanes < used)


def pair_of(step, pairs):
    return jnp.clip(step - lax.axis_index("site"), 0, pairs - 1)


def cut(block, row, dims):
    used = dims[0, lax.axis_index("sector")]
    return jnp.where(inside(block.shape, row, used), block.astype(jnp.float32), 0.0).astype(jnp.bfloat16)


def product(e, ket_block, bra_rows, flag):
    moved = across(e, ket_block) * flag.astype(jnp.float32)
    return down(bra_rows, moved.astype(jnp.bfloat16))


def group(states, e, row, ket, bra, flags, pair, total):
    rows = slice(row, row + e.shape[0])
    for s in states:
        part = product(e, ket[0, pair, s, 0], bra[0, s, 0, rows], flags[0, s, 0])
        total = part if total is None else total + part
    return total


def open_kernel(step, groups, dims, flags, env, ket, bra, *refs):
    outs = refs[: len(groups)]
    env_buf, ket_buf, bra_buf, sems = refs[len(groups) :]
    pairs = ket.shape[1]
    states = [s for states in groups for s in states]
    pair = pair_of(step, pairs)
    first = pltpu.make_async_copy(env.at[step, 0], env_buf, sems.at[0])
    first.start()
    copies = []
    for i, s in enumerate(states):
        copies.append(
            (
                pltpu.make_async_copy(ket.at[0, pair, s, 0], ket_buf.at[i], sems.at[1 + 2 * i]),
                pltpu.make_async_copy(bra.at[0, s, 0], bra_buf.at[i], sems.at[2 + 2 * i]),
            )
        )
        for copy in copies[-1]:
            copy.start()
    first.wait()
    e = cut(env_buf[...], 0, dims)
    i = 0
    for states, out in zip(groups, outs):
        total = None
        for s in states:
            for copy in copies[i]:
                copy.wait()
            part = product(e, ket_buf[i], bra_buf[i], flags[0, s, 0])
            total = part if total is None else total + part
            i += 1
        out[...] = total.astype(jnp.bfloat16)


def step_kernel(step, row, fresh, added, groups, dims, flags, *refs):
    refs = list(refs)
    env = refs.pop(0) if fresh else None
    held, ket, bra = refs[:3]
    before = refs[3 : 3 + len(groups)] if added else [None] * len(groups)
    outs = refs[3 + len(groups) * added :]
    pair = pair_of(step, ket.shape[1])
    e = held[...]
    if fresh:
        entering = cut(env[step, 0, row : row + e.shape[0]], row, dims)
        e = jnp.where(lax.axis_index("site") == 0, entering, e)
    for states, start, out in zip(groups, before, outs):
        total = group(states, e, row, ket, bra, flags, pair, None if start is None else start[...])
        out[...] = total.astype(out.dtype)


def sum_kernel(row, bond_site, dims, none, other, came, out):
    rows = slice(row, row + came.shape[0])
    sector = lax.axis_index("sector")
    used = dims[lax.axis_index("site") + 1, sector]
    total = none[rows].astype(jnp.float32)
    total = total + jnp.where(sector % 2 == 1, other[rows].astype(jnp.float32), 0.0)
    total = total + jnp.where(sector >= 2, came[...].astype(jnp.float32), 0.0)
    out[...] = jnp.where(inside(total.shape, row, used), total, 0.0).astype(jnp.bfloat16)


def write_kernel(step, cuts, pairs, *refs):
    blocks = refs[: len(cuts) - 1]
    out, sems = refs[-2:]
    pair = step - lax.axis_index("site")

    @pl.when(jnp.logical_and(pair >= 0, pair < pairs))
    def _():
        copies = []
        for k, block in enumerate(blocks):
            rows = pl.ds(cuts[k], cuts[k + 1] - cuts[k])
            copies.append(pltpu.make_async_copy(block, out.at[0, pair, 0, rows], sems.at[k]))
            copies[-1].start()
        for copy in copies:
            copy.wait()


def call(kernel, in_specs, out_shape, flops=0, moved=0, **more):
    return pl.pallas_call(
        kernel,
        out_shape=out_shape,
        in_specs=in_specs,
        compiler_params=pltpu.CompilerParams(vmem_limit_bytes=LIMIT),
        cost_estimate=pl.CostEstimate(flops=flops, bytes_accessed=moved, transcendentals=0),
        **more,
    )


def per_device(env_in, bra, ket, sector_dims, flags):
    sections = lax.axis_size("site")
    sectors = lax.axis_size("sector")
    sector = lax.axis_index("sector")
    pairs = ket.shape[1]
    width = ket.shape[-1]
    steps = pairs + sections - 1
    cuts = bounds(width)
    even = sector % 2 == 0

    def at(j, q):
        return j * sectors + q

    everyone = [(j, q) for j in range(sections) for q in range(sectors)]
    swap_pairs = [(at(j, q), at(j, q ^ 1)) for j, q in everyone]
    up_pairs = [(at(j, q), at(j, (q + 2) % sectors)) for j, q in everyone]
    next_pairs = [(at(j, q), at((j + 1) % sections, q)) for j, q in everyone]

    def block(rows, dtype=jnp.bfloat16):
        return jax.ShapeDtypeStruct((rows, width), dtype)

    def opening(groups):
        count = sum(len(states) for states in groups)
        scratch = [
            pltpu.VMEM((width, width), jnp.bfloat16),
            pltpu.VMEM((count, width, width), jnp.bfloat16),
            pltpu.VMEM((count, width, width), jnp.bfloat16),
            pltpu.SemaphoreType.DMA((1 + 2 * count,)),
        ]
        return call(
            functools.partial(open_kernel, 0, groups),
            [SMEM, SMEM, ANY, ANY, ANY],
            [block(width)] * len(groups),
            4 * count * width**3,
            scratch_shapes=scratch,
            out_specs=[VMEM] * len(groups),
        )(sector_dims, flags, env_in, ket, bra)

    def chunk(step, k, groups, held, before, dtype):
        fresh = step < pairs
        operands = [sector_dims, flags] + ([env_in] if fresh else []) + [held, ket, bra] + before
        return call(
            functools.partial(step_kernel, step, cuts[k], fresh, len(before) > 0, groups),
            [SMEM, SMEM] + [VMEM] * (len(operands) - 2),
            [block(width, dtype)] * len(groups),
            4 * sum(len(states) for states in groups) * (cuts[k + 1] - cuts[k]) * width**2,
            out_specs=[VMEM] * len(groups),
        )(*operands)

    result = None
    held = None
    for step in range(steps):
        if step == 0:
            (single,) = opening([(1, 2)])
            other = lax.ppermute(single, AXES, swap_pairs)
            double, none = opening([(3,), (0,)])
        else:
            total = []
            for k in range(CHUNKS - 1):
                total = chunk(step, k, [(1, 2), (3,), (0,)], held[k], list(total), jnp.float32)
            total = list(total)
            (single,) = chunk(step, CHUNKS - 1, [(1, 2)], held[-1], total[:1], jnp.bfloat16)
            other = lax.ppermute(single, AXES, swap_pairs)
            double, none = chunk(step, CHUNKS - 1, [(3,), (0,)], held[-1], total[1:], jnp.bfloat16)
        fresh = []
        for k in range(CHUNKS):
            rows = slice(cuts[k], cuts[k + 1])
            part = jnp.where(even, other[rows].astype(jnp.float32), 0.0)
            up = (double[rows].astype(jnp.float32) + part).astype(jnp.bfloat16)
            came = lax.ppermute(up, AXES, up_pairs)
            fresh.append(
                call(
                    functools.partial(sum_kernel, cuts[k], step),
                    [SMEM] + [VMEM] * 3,
                    block(cuts[k + 1] - cuts[k]),
                    out_specs=VMEM,
                )(sector_dims, none, other, came)
            )
        if step + 1 < steps:
            held = [lax.ppermute(rows, AXES, next_pairs) for rows in fresh]
        shape = jax.ShapeDtypeStruct((1, pairs, 1, width, width), jnp.bfloat16)
        operands = fresh + ([] if result is None else [result])
        result = call(
            functools.partial(write_kernel, step, cuts, pairs),
            [VMEM] * CHUNKS + [ANY] * (len(operands) - CHUNKS),
            shape,
            out_specs=ANY,
            scratch_shapes=[pltpu.SemaphoreType.DMA((CHUNKS,))],
            input_output_aliases={} if result is None else {CHUNKS: 0},
        )(*operands)
    return result


def solution(mesh):
    in_specs = (
        P(None, "sector", None, None),
        P("site", None, "sector", None, None),
        P("site", None, None, "sector", None, None),
        P(),
        P("site", None, "sector"),
    )
    out_specs = P("site", None, "sector", None, None)
    return jax.shard_map(per_device, mesh=mesh, in_specs=in_specs, out_specs=out_specs, check_vma=False)
```

time: 327 us -> 152 us (0.46)
  the two profiles are of different devices: /device:TPU:14 before, /device:TPU:0 now
where the time goes in v1:
time: 152 us
  waiting for transfers between devices  91.2 us (60%)
  Pallas kernels  38.6 us (25%)
  starting transfers between devices  11 us (7%)
  local copies, waits for them, and re-layouts  8.63 us (6%)
  other arithmetic  1.97 us (1%)
    ppermute x10, waiting for transfers between devices, per_device(): came = lax.ppermute(up, AXES, up_pairs)  66.7 us
    ppermute x8, waiting for transfers between devices, per_device(): held = [lax.ppermute(rows, AXES, next_pairs) for rows in fresh]  23.4 us
    pallas_call x12, Pallas kernels, chunk(): call(functools.partial(step_kernel, step, cuts[k], fresh, len(before) > 0...  22.2 us
    pallas_call x10, Pallas kernels, per_device(): call(functools.partial(sum_kernel, cuts[k], step), [SMEM] + [VMEM] * 3, b...  8.83 us
    unnamed x19, local copies, waits for them, and re-layouts  8.63 us
    pallas_call x2, Pallas kernels, opening(): call(functools.partial(open_kernel, 0, groups), [SMEM, SMEM, ANY, ANY, AN...  5.84 us
    ppermute x10, starting transfers between devices, per_device(): came = lax.ppermute(up, AXES, up_pairs)  5.63 us
    ppermute x8, starting transfers between devices, per_device(): held = [lax.ppermute(rows, AXES, next_pairs) for rows in fresh]  4.57 us
  transfers between devices with their start and end apart: 23, of which 22 were waited for; matrix products, arithmetic and copies ran while one was open for 0% of the time, Pallas kernels for 18%

profile of v1, /device:TPU:0, one launch (start us, length us, event | category | flops | bytes accessed | tf_op | source)
XLA Modules:
  0.0 151.9 jit_solution(13137206131071987998)
XLA Ops:
  6.4 3.3 %shard_map.56 = bf16[512,512]{1,0:T(8,128)(2,1)} custom-call(s32[5,8]{1,0:T(8,128)S(1)} %copy-done.7, s32[1,4,1]{2,1,0:T(4,128)S(1)} %copy.22.flags, bf16[2,1,512,512]{3,2,1,0:T(8,128)(2,1)S(1)} %copy-done.5, bf16[1,2,4,1,512,512]{5,4,3,2,1,0:T(8,128)(2,1)S(1)} %copy-done, bf16[1,4,1,512,512]{4,3,2,1,0:T(8,128)(2,1)S(1)} %copy-done.3), custom_call_target="tpu_custom_call" | custom-call | flops 1073741824 | tf_op jit(solution)/shard_map/pallas_call | solution.py:173
  12.5 2.6 %shard_map.55 = (bf16[512,512]{1,0:T(8,128)(2,1)S(1)}, bf16[512,512]{1,0:T(8,128)(2,1)S(1)}) custom-call(s32[5,8]{1,0:T(8,128)S(1)} %copy-done.8, s32[1,4,1]{2,1,0:T(4,128)S(1)} %copy.22.flags, bf16[2,1,512,512]{3,2,1,0:T(8,128)(2,1)S(1)} %copy-done.6, bf16[1,2,4,1,512,512]{5,4,3,2,1,0:T(8,128)(2,1)S(1)} %copy-done.1, bf16[1,4,1,512,512]{4,3,2,1,0:T(8,128)(2,1)S(1)} %copy-done.4), custom_call_target="tpu_custom_call" | custom-call | flops 1073741824 | tf_op jit(solution)/shard_map/pallas_call | solution.py:173
  16.4 2.7 %collective-permute-start.3 = (bf16[256,512]{1,0:T(8,128)(2,1)S(1)}, bf16[256,512]{1,0:T(8,128)(2,1)S(1)}, u32[]{:S(2)}, u32[]{:S(2)}) collective-permute-start(bf16[256,512]{1,0:T(8,128)(2,1)S(1)} %get-tuple-element.57), channel_id=1, source_target_pairs={{0,2},{1,3},{2,4},{3,5},{4,6},{5,7},{6,0},{7,1},{8,10},{9,11},{10,... | collective-permute-start | bytes 786440 | tf_op jit(solution)/shard_map/ppermute | solution.py:213
  20.6 7.6 %collective-permute-done.3.came = bf16[256,512]{1,0:T(8,128)(2,1)S(1)} collective-permute-done((bf16[256,512]{1,0:T(8,128)(2,1)S(1)}, bf16[256,512]{1,0:T(8,128)(2,1)S(1)}, u32[]{:S(2)}, u32[]{:S(2)}) %collective-permute-start.3) | collective-permute-done | bytes 262176 | tf_op jit(solution)/shard_map/ppermute | solution.py:213
  31.3 2.4 %collective-permute-done.1.came = bf16[256,512]{1,0:T(8,128)(2,1)S(1)} collective-permute-done((bf16[256,512]{1,0:T(8,128)(2,1)S(1)}, bf16[256,512]{1,0:T(8,128)(2,1)S(1)}, u32[]{:S(2)}, u32[]{:S(2)}) %collective-permute-start.1) | collective-permute-done | bytes 262176 | tf_op jit(solution)/shard_map/ppermute | solution.py:213
  38.3 2.3 %shard_map.59 = (f32[512,512]{1,0:T(8,128)S(1)}, f32[512,512]{1,0:T(8,128)S(1)}, f32[512,512]{1,0:T(8,128)S(1)}) custom-call(s32[5,8]{1,0:T(8,128)S(1)} %copy-done.8, s32[1,4,1]{2,1,0:T(4,128)S(1)} %copy.22.flags, bf16[2,1,512,512]{3,2,1,0:T(8,128)(2,1)S(1)} %copy-done.6, bf16[256,512]{1,0:T(8,128)(2,1)S(1)} %collective-permute-done.4.refs_1_, ...), custom_call_target="tpu_custom_call" | custom-call | flops 1073741824 | tf_op jit(solution)/shard_map/pallas_call | solution.py:185
  40.6 3.3 %collective-permute-done.2.refs_1_ = bf16[256,512]{1,0:T(8,128)(2,1)S(1)} collective-permute-done((bf16[256,512]{1,0:T(8,128)(2,1)S(1)}, bf16[256,512]{1,0:T(8,128)(2,1)S(1)}, u32[]{:S(2)}, u32[]{:S(2)}) %collective-permute-start.2) | collective-permute-done | bytes 262176 | tf_op jit(solution)/shard_map/ppermute | solution.py:223
  48.8 10.0 %collective-permute-done.8.came = bf16[256,512]{1,0:T(8,128)(2,1)S(1)} collective-permute-done((bf16[256,512]{1,0:T(8,128)(2,1)S(1)}, bf16[256,512]{1,0:T(8,128)(2,1)S(1)}, u32[]{:S(2)}, u32[]{:S(2)}) %collective-permute-start.8) | collective-permute-done | bytes 262176 | tf_op jit(solution)/shard_map/ppermute | solution.py:213
  60.0 3.7 %collective-permute-done.6.came = bf16[256,512]{1,0:T(8,128)(2,1)S(1)} collective-permute-done((bf16[256,512]{1,0:T(8,128)(2,1)S(1)}, bf16[256,512]{1,0:T(8,128)(2,1)S(1)}, u32[]{:S(2)}, u32[]{:S(2)}) %collective-permute-start.6) | collective-permute-done | bytes 262176 | tf_op jit(solution)/shard_map/ppermute | solution.py:213
  64.9 2.5 %collective-permute-done.9.refs_0_ = bf16[256,512]{1,0:T(8,128)(2,1)S(1)} collective-permute-done((bf16[256,512]{1,0:T(8,128)(2,1)S(1)}, bf16[256,512]{1,0:T(8,128)(2,1)S(1)}, u32[]{:S(2)}, u32[]{:S(2)}) %collective-permute-start.9) | collective-permute-done | bytes 262176 | tf_op jit(solution)/shard_map/ppermute | solution.py:223
  67.4 2.3 %shard_map.64 = (f32[512,512]{1,0:T(8,128)S(1)}, f32[512,512]{1,0:T(8,128)S(1)}, f32[512,512]{1,0:T(8,128)S(1)}) custom-call(s32[5,8]{1,0:T(8,128)S(1)} %copy-done.8, s32[1,4,1]{2,1,0:T(4,128)S(1)} %copy.22.flags, bf16[256,512]{1,0:T(8,128)(2,1)S(1)} %collective-permute-done.9.refs_0_, bf16[1,2,4,1,512,512]{5,4,3,2,1,0:T(8,128)(2,1)S(1)} %copy-done.2, ...), custom_call_target="tpu_custom_call" | custom-call | flops 1073741824 | tf_op jit(solution)/shard_map/pallas_call | solution.py:185
  69.7 3.3 %collective-permute-done.7.refs_0_ = bf16[256,512]{1,0:T(8,128)(2,1)S(1)} collective-permute-done((bf16[256,512]{1,0:T(8,128)(2,1)S(1)}, bf16[256,512]{1,0:T(8,128)(2,1)S(1)}, u32[]{:S(2)}, u32[]{:S(2)}) %collective-permute-start.7) | collective-permute-done | bytes 262176 | tf_op jit(solution)/shard_map/ppermute | solution.py:223
  76.9 10.9 %collective-permute-done.13.came = bf16[256,512]{1,0:T(8,128)(2,1)S(1)} collective-permute-done((bf16[256,512]{1,0:T(8,128)(2,1)S(1)}, bf16[256,512]{1,0:T(8,128)(2,1)S(1)}, u32[]{:S(2)}, u32[]{:S(2)}) %collective-permute-start.13) | collective-permute-done | bytes 262176 | tf_op jit(solution)/shard_map/ppermute | solution.py:213
  88.7 4.0 %collective-permute-done.11.came = bf16[256,512]{1,0:T(8,128)(2,1)S(1)} collective-permute-done((bf16[256,512]{1,0:T(8,128)(2,1)S(1)}, bf16[256,512]{1,0:T(8,128)(2,1)S(1)}, u32[]{:S(2)}, u32[]{:S(2)}) %collective-permute-start.11) | collective-permute-done | bytes 262176 | tf_op jit(solution)/shard_map/ppermute | solution.py:213
  93.8 2.7 %collective-permute-done.14.refs_0_ = bf16[256,512]{1,0:T(8,128)(2,1)S(1)} collective-permute-done((bf16[256,512]{1,0:T(8,128)(2,1)S(1)}, bf16[256,512]{1,0:T(8,128)(2,1)S(1)}, u32[]{:S(2)}, u32[]{:S(2)}) %collective-permute-start.14) | collective-permute-done | bytes 262176 | tf_op jit(solution)/shard_map/ppermute | solution.py:223
  96.4 2.3 %shard_map.69 = (f32[512,512]{1,0:T(8,128)S(1)}, f32[512,512]{1,0:T(8,128)S(1)}, f32[512,512]{1,0:T(8,128)S(1)}) custom-call(s32[5,8]{1,0:T(8,128)S(1)} %copy-done.8, s32[1,4,1]{2,1,0:T(4,128)S(1)} %copy.22.flags, bf16[256,512]{1,0:T(8,128)(2,1)S(1)} %collective-permute-done.14.refs_0_, bf16[1,2,4,1,512,512]{5,4,3,2,1,0:T(8,128)(2,1)S(1)} %copy-done.2, ...), custom_call_target="tpu_custom_call" | custom-call | flops 1073741824 | tf_op jit(solution)/shard_map/pallas_call | solution.py:185
  98.7 3.5 %collective-permute-done.12.refs_0_ = bf16[256,512]{1,0:T(8,128)(2,1)S(1)} collective-permute-done((bf16[256,512]{1,0:T(8,128)(2,1)S(1)}, bf16[256,512]{1,0:T(8,128)(2,1)S(1)}, u32[]{:S(2)}, u32[]{:S(2)}) %collective-permute-start.12) | collective-permute-done | bytes 262176 | tf_op jit(solution)/shard_map/ppermute | solution.py:223
  106.1 10.9 %collective-permute-done.18.came = bf16[256,512]{1,0:T(8,128)(2,1)S(1)} collective-permute-done((bf16[256,512]{1,0:T(8,128)(2,1)S(1)}, bf16[256,512]{1,0:T(8,128)(2,1)S(1)}, u32[]{:S(2)}, u32[]{:S(2)}) %collective-permute-start.18) | collective-permute-done | bytes 262176 | tf_op jit(solution)/shard_map/ppermute | solution.py:213
  117.9 4.0 %collective-permute-done.16.came = bf16[256,512]{1,0:T(8,128)(2,1)S(1)} collective-permute-done((bf16[256,512]{1,0:T(8,128)(2,1)S(1)}, bf16[256,512]{1,0:T(8,128)(2,1)S(1)}, u32[]{:S(2)}, u32[]{:S(2)}) %collective-permute-start.16) | collective-permute-done | bytes 262176 | tf_op jit(solution)/shard_map/ppermute | solution.py:213
  122.8 2.9 %collective-permute-done.19.refs_0_ = bf16[256,512]{1,0:T(8,128)(2,1)S(1)} collective-permute-done((bf16[256,512]{1,0:T(8,128)(2,1)S(1)}, bf16[256,512]{1,0:T(8,128)(2,1)S(1)}, u32[]{:S(2)}, u32[]{:S(2)}) %collective-permute-start.19) | collective-permute-done | bytes 262176 | tf_op jit(solution)/shard_map/ppermute | solution.py:223
  125.6 2.3 %shard_map.74 = (f32[512,512]{1,0:T(8,128)S(1)}, f32[512,512]{1,0:T(8,128)S(1)}, f32[512,512]{1,0:T(8,128)S(1)}) custom-call(s32[5,8]{1,0:T(8,128)S(1)} %copy-done.8, s32[1,4,1]{2,1,0:T(4,128)S(1)} %copy.22.flags, bf16[256,512]{1,0:T(8,128)(2,1)S(1)} %collective-permute-done.19.refs_0_, bf16[1,2,4,1,512,512]{5,4,3,2,1,0:T(8,128)(2,1)S(1)} %copy-done.2, ...), custom_call_target="tpu_custom_call" | custom-call | flops 1073741824 | tf_op jit(solution)/shard_map/pallas_call | solution.py:185
  127.9 3.3 %collective-permute-done.17.refs_0_ = bf16[256,512]{1,0:T(8,128)(2,1)S(1)} collective-permute-done((bf16[256,512]{1,0:T(8,128)(2,1)S(1)}, bf16[256,512]{1,0:T(8,128)(2,1)S(1)}, u32[]{:S(2)}, u32[]{:S(2)}) %collective-permute-start.17) | collective-permute-done | bytes 262176 | tf_op jit(solution)/shard_map/ppermute | solution.py:223
  136.9 9.2 %collective-permute-done.22.came = bf16[256,512]{1,0:T(8,128)(2,1)S(1)} collective-permute-done((bf16[256,512]{1,0:T(8,128)(2,1)S(1)}, bf16[256,512]{1,0:T(8,128)(2,1)S(1)}, u32[]{:S(2)}, u32[]{:S(2)}) %collective-permute-start.22) | collective-permute-done | bytes 262176 | tf_op jit(solution)/shard_map/ppermute | solution.py:213
  146.8 4.1 %collective-permute-done.21.came = bf16[256,512]{1,0:T(8,128)(2,1)S(1)} collective-permute-done((bf16[256,512]{1,0:T(8,128)(2,1)S(1)}, bf16[256,512]{1,0:T(8,128)(2,1)S(1)}, u32[]{:S(2)}, u32[]{:S(2)}) %collective-permute-start.21) | collective-permute-done | bytes 262176 | tf_op jit(solution)/shard_map/ppermute | solution.py:213
  (75 shorter events, 45.5 us)
Async XLA Ops:
  9.7 5.3 %collective-permute-start = (bf16[512,512]{1,0:T(8,128)(2,1)}, bf16[512,512]{1,0:T(8,128)(2,1)}, u32[]{:S(2)}, u32[]{:S(2)}) collective-permute-start(bf16[512,512]{1,0:T(8,128)(2,1)} %shard_map.56), channel_id=1, source_target_pairs={{0,1},{1,0},{2,3},{3,2},{4,5},{5,4},{6,7},{7,6},{8,9},{9,8},{10,11... | collective-permute-start | bytes 1572872 | tf_op jit(solution)/shard_map/ppermute | solution.py:198
  15.0 23.3 %copy-start.2 = (bf16[1,2,4,1,512,512]{5,4,3,2,1,0:T(8,128)(2,1)S(1)}, bf16[1,2,4,1,512,512]{5,4,3,2,1,0:T(8,128)(2,1)}, u32[]{:S(2)}) copy-start(bf16[1,2,4,1,512,512]{5,4,3,2,1,0:T(8,128)(2,1)} %refs_1_.17) | copy-start | bytes 12582916
  16.4 11.8 %collective-permute-start.3 = (bf16[256,512]{1,0:T(8,128)(2,1)S(1)}, bf16[256,512]{1,0:T(8,128)(2,1)S(1)}, u32[]{:S(2)}, u32[]{:S(2)}) collective-permute-start(bf16[256,512]{1,0:T(8,128)(2,1)S(1)} %get-tuple-element.57), channel_id=1, source_target_pairs={{0,2},{1,3},{2,4},{3,5},{4,6},{5,7},{6,0},{7,1},{8,10},{9,11},{10,... | collective-permute-start | bytes 786440 | tf_op jit(solution)/shard_map/ppermute | solution.py:213
  19.1 14.6 %collective-permute-start.1 = (bf16[256,512]{1,0:T(8,128)(2,1)S(1)}, bf16[256,512]{1,0:T(8,128)(2,1)S(1)}, u32[]{:S(2)}, u32[]{:S(2)}) collective-permute-start(bf16[256,512]{1,0:T(8,128)(2,1)S(1)} %get-tuple-element.58), channel_id=1, source_target_pairs={{0,2},{1,3},{2,4},{3,5},{4,6},{5,7},{6,0},{7,1},{8,10},{9,11},{10,... | collective-permute-start | bytes 786440 | tf_op jit(solution)/shard_map/ppermute | solution.py:213
  29.5 8.8 %collective-permute-start.4 = (bf16[256,512]{1,0:T(8,128)(2,1)S(1)}, bf16[256,512]{1,0:T(8,128)(2,1)S(1)}, u32[]{:S(2)}, u32[]{:S(2)}) collective-permute-start(bf16[256,512]{1,0:T(8,128)(2,1)S(1)} %shard_map.58.refs_0_), channel_id=1, source_target_pairs={{0,8},{1,9},{2,10},{3,11},{4,12},{5,13},{6,14},{7,15},{8,16},{9,17... | collective-permute-start | bytes 786440 | tf_op jit(solution)/shard_map/ppermute | solution.py:223
  34.9 9.0 %collective-permute-start.2 = (bf16[256,512]{1,0:T(8,128)(2,1)S(1)}, bf16[256,512]{1,0:T(8,128)(2,1)S(1)}, u32[]{:S(2)}, u32[]{:S(2)}) collective-permute-start(bf16[256,512]{1,0:T(8,128)(2,1)S(1)} %shard_map.57.refs_1_), channel_id=1, source_target_pairs={{0,8},{1,9},{2,10},{3,11},{4,12},{5,13},{6,14},{7,15},{8,16},{9,17... | collective-permute-start | bytes 786440 | tf_op jit(solution)/shard_map/ppermute | solution.py:223
  45.6 2.0 %collective-permute-start.5 = (bf16[512,512]{1,0:T(8,128)(2,1)S(1)}, bf16[512,512]{1,0:T(8,128)(2,1)S(1)}, u32[]{:S(2)}, u32[]{:S(2)}) collective-permute-start(bf16[512,512]{1,0:T(8,128)(2,1)S(1)} %shard_map.61), channel_id=1, source_target_pairs={{0,1},{1,0},{2,3},{3,2},{4,5},{5,4},{6,7},{7,6},{8,9},{9,8},{10,11... | collective-permute-start | bytes 1572872 | tf_op jit(solution)/shard_map/ppermute | solution.py:206
  47.7 11.0 %collective-permute-start.8 = (bf16[256,512]{1,0:T(8,128)(2,1)S(1)}, bf16[256,512]{1,0:T(8,128)(2,1)S(1)}, u32[]{:S(2)}, u32[]{:S(2)}) collective-permute-start(bf16[256,512]{1,0:T(8,128)(2,1)S(1)} %get-tuple-element.55), channel_id=1, source_target_pairs={{0,2},{1,3},{2,4},{3,5},{4,6},{5,7},{6,0},{7,1},{8,10},{9,11},{10,... | collective-permute-start | bytes 786440 | tf_op jit(solution)/shard_map/ppermute | solution.py:213
  47.8 15.9 %collective-permute-start.6 = (bf16[256,512]{1,0:T(8,128)(2,1)S(1)}, bf16[256,512]{1,0:T(8,128)(2,1)S(1)}, u32[]{:S(2)}, u32[]{:S(2)}) collective-permute-start(bf16[256,512]{1,0:T(8,128)(2,1)S(1)} %get-tuple-element.56), channel_id=1, source_target_pairs={{0,2},{1,3},{2,4},{3,5},{4,6},{5,7},{6,0},{7,1},{8,10},{9,11},{10,... | collective-permute-start | bytes 786440 | tf_op jit(solution)/shard_map/ppermute | solution.py:213
  59.5 7.9 %collective-permute-start.9 = (bf16[256,512]{1,0:T(8,128)(2,1)S(1)}, bf16[256,512]{1,0:T(8,128)(2,1)S(1)}, u32[]{:S(2)}, u32[]{:S(2)}) collective-permute-start(bf16[256,512]{1,0:T(8,128)(2,1)S(1)} %shard_map.63.refs_0_), channel_id=1, source_target_pairs={{0,8},{1,9},{2,10},{3,11},{4,12},{5,13},{6,14},{7,15},{8,16},{9,17... | collective-permute-start | bytes 786440 | tf_op jit(solution)/shard_map/ppermute | solution.py:223
  64.5 8.6 %collective-permute-start.7 = (bf16[256,512]{1,0:T(8,128)(2,1)S(1)}, bf16[256,512]{1,0:T(8,128)(2,1)S(1)}, u32[]{:S(2)}, u32[]{:S(2)}) collective-permute-start(bf16[256,512]{1,0:T(8,128)(2,1)S(1)} %shard_map.62.refs_1_), channel_id=1, source_target_pairs={{0,8},{1,9},{2,10},{3,11},{4,12},{5,13},{6,14},{7,15},{8,16},{9,17... | collective-permute-start | bytes 786440 | tf_op jit(solution)/shard_map/ppermute | solution.py:223
  74.6 2.0 %collective-permute-start.10 = (bf16[512,512]{1,0:T(8,128)(2,1)S(1)}, bf16[512,512]{1,0:T(8,128)(2,1)S(1)}, u32[]{:S(2)}, u32[]{:S(2)}) collective-permute-start(bf16[512,512]{1,0:T(8,128)(2,1)S(1)} %shard_map.66), channel_id=1, source_target_pairs={{0,1},{1,0},{2,3},{3,2},{4,5},{5,4},{6,7},{7,6},{8,9},{9,8},{10,11... | collective-permute-start | bytes 1572872 | tf_op jit(solution)/shard_map/ppermute | solution.py:206
  76.8 11.0 %collective-permute-start.13 = (bf16[256,512]{1,0:T(8,128)(2,1)S(1)}, bf16[256,512]{1,0:T(8,128)(2,1)S(1)}, u32[]{:S(2)}, u32[]{:S(2)}) collective-permute-start(bf16[256,512]{1,0:T(8,128)(2,1)S(1)} %get-tuple-element.53), channel_id=1, source_target_pairs={{0,2},{1,3},{2,4},{3,5},{4,6},{5,7},{6,0},{7,1},{8,10},{9,11},{10,... | collective-permute-start | bytes 786440 | tf_op jit(solution)/shard_map/ppermute | solution.py:213
  76.8 15.9 %collective-permute-start.11 = (bf16[256,512]{1,0:T(8,128)(2,1)S(1)}, bf16[256,512]{1,0:T(8,128)(2,1)S(1)}, u32[]{:S(2)}, u32[]{:S(2)}) collective-permute-start(bf16[256,512]{1,0:T(8,128)(2,1)S(1)} %get-tuple-element.54), channel_id=1, source_target_pairs={{0,2},{1,3},{2,4},{3,5},{4,6},{5,7},{6,0},{7,1},{8,10},{9,11},{10,... | collective-permute-start | bytes 786440 | tf_op jit(solution)/shard_map/ppermute | solution.py:213
  88.6 7.8 %collective-permute-start.14 = (bf16[256,512]{1,0:T(8,128)(2,1)S(1)}, bf16[256,512]{1,0:T(8,128)(2,1)S(1)}, u32[]{:S(2)}, u32[]{:S(2)}) collective-permute-start(bf16[256,512]{1,0:T(8,128)(2,1)S(1)} %shard_map.68.refs_0_), channel_id=1, source_target_pairs={{0,8},{1,9},{2,10},{3,11},{4,12},{5,13},{6,14},{7,15},{8,16},{9,17... | collective-permute-start | bytes 786440 | tf_op jit(solution)/shard_map/ppermute | solution.py:223
  93.5 8.7 %collective-permute-start.12 = (bf16[256,512]{1,0:T(8,128)(2,1)S(1)}, bf16[256,512]{1,0:T(8,128)(2,1)S(1)}, u32[]{:S(2)}, u32[]{:S(2)}) collective-permute-start(bf16[256,512]{1,0:T(8,128)(2,1)S(1)} %shard_map.67.refs_1_), channel_id=1, source_target_pairs={{0,8},{1,9},{2,10},{3,11},{4,12},{5,13},{6,14},{7,15},{8,16},{9,17... | collective-permute-start | bytes 786440 | tf_op jit(solution)/shard_map/ppermute | solution.py:223
  103.9 2.0 %collective-permute-start.15 = (bf16[512,512]{1,0:T(8,128)(2,1)S(1)}, bf16[512,512]{1,0:T(8,128)(2,1)S(1)}, u32[]{:S(2)}, u32[]{:S(2)}) collective-permute-start(bf16[512,512]{1,0:T(8,128)(2,1)S(1)} %shard_map.71), channel_id=1, source_target_pairs={{0,1},{1,0},{2,3},{3,2},{4,5},{5,4},{6,7},{7,6},{8,9},{9,8},{10,11... | collective-permute-start | bytes 1572872 | tf_op jit(solution)/shard_map/ppermute | solution.py:206
  106.0 11.0 %collective-permute-start.18 = (bf16[256,512]{1,0:T(8,128)(2,1)S(1)}, bf16[256,512]{1,0:T(8,128)(2,1)S(1)}, u32[]{:S(2)}, u32[]{:S(2)}) collective-permute-start(bf16[256,512]{1,0:T(8,128)(2,1)S(1)} %get-tuple-element.51), channel_id=1, source_target_pairs={{0,2},{1,3},{2,4},{3,5},{4,6},{5,7},{6,0},{7,1},{8,10},{9,11},{10,... | collective-permute-start | bytes 786440 | tf_op jit(solution)/shard_map/ppermute | solution.py:213
  106.1 15.9 %collective-permute-start.16 = (bf16[256,512]{1,0:T(8,128)(2,1)S(1)}, bf16[256,512]{1,0:T(8,128)(2,1)S(1)}, u32[]{:S(2)}, u32[]{:S(2)}) collective-permute-start(bf16[256,512]{1,0:T(8,128)(2,1)S(1)} %get-tuple-element.52), channel_id=1, source_target_pairs={{0,2},{1,3},{2,4},{3,5},{4,6},{5,7},{6,0},{7,1},{8,10},{9,11},{10,... | collective-permute-start | bytes 786440 | tf_op jit(solution)/shard_map/ppermute | solution.py:213
  117.8 7.8 %collective-permute-start.19 = (bf16[256,512]{1,0:T(8,128)(2,1)S(1)}, bf16[256,512]{1,0:T(8,128)(2,1)S(1)}, u32[]{:S(2)}, u32[]{:S(2)}) collective-permute-start(bf16[256,512]{1,0:T(8,128)(2,1)S(1)} %shard_map.73.refs_0_), channel_id=1, source_target_pairs={{0,8},{1,9},{2,10},{3,11},{4,12},{5,13},{6,14},{7,15},{8,16},{9,17... | collective-permute-start | bytes 786440 | tf_op jit(solution)/shard_map/ppermute | solution.py:223
  122.7 8.5 %collective-permute-start.17 = (bf16[256,512]{1,0:T(8,128)(2,1)S(1)}, bf16[256,512]{1,0:T(8,128)(2,1)S(1)}, u32[]{:S(2)}, u32[]{:S(2)}) collective-permute-start(bf16[256,512]{1,0:T(8,128)(2,1)S(1)} %shard_map.72.refs_1_), channel_id=1, source_target_pairs={{0,8},{1,9},{2,10},{3,11},{4,12},{5,13},{6,14},{7,15},{8,16},{9,17... | collective-permute-start | bytes 786440 | tf_op jit(solution)/shard_map/ppermute | solution.py:223
  132.9 2.0 %collective-permute-start.20 = (bf16[512,512]{1,0:T(8,128)(2,1)S(1)}, bf16[512,512]{1,0:T(8,128)(2,1)S(1)}, u32[]{:S(2)}, u32[]{:S(2)}) collective-permute-start(bf16[512,512]{1,0:T(8,128)(2,1)S(1)} %shard_map.76), channel_id=1, source_target_pairs={{0,1},{1,0},{2,3},{3,2},{4,5},{5,4},{6,7},{7,6},{8,9},{9,8},{10,11... | collective-permute-start | bytes 1572872 | tf_op jit(solution)/shard_map/ppermute | solution.py:206
  135.0 11.0 %collective-permute-start.22 = (bf16[256,512]{1,0:T(8,128)(2,1)S(1)}, bf16[256,512]{1,0:T(8,128)(2,1)S(1)}, u32[]{:S(2)}, u32[]{:S(2)}) collective-permute-start(bf16[256,512]{1,0:T(8,128)(2,1)S(1)} %get-tuple-element.49), channel_id=1, source_target_pairs={{0,2},{1,3},{2,4},{3,5},{4,6},{5,7},{6,0},{7,1},{8,10},{9,11},{10,... | collective-permute-start | bytes 786440 | tf_op jit(solution)/shard_map/ppermute | solution.py:213
  135.1 15.8 %collective-permute-start.21 = (bf16[256,512]{1,0:T(8,128)(2,1)S(1)}, bf16[256,512]{1,0:T(8,128)(2,1)S(1)}, u32[]{:S(2)}, u32[]{:S(2)}) collective-permute-start(bf16[256,512]{1,0:T(8,128)(2,1)S(1)} %get-tuple-element.50), channel_id=1, source_target_pairs={{0,2},{1,3},{2,4},{3,5},{4,6},{5,7},{6,0},{7,1},{8,10},{9,11},{10,... | collective-permute-start | bytes 786440 | tf_op jit(solution)/shard_map/ppermute | solution.py:213
  (8 other events, 19.4 us)

commit v2 on v1

--- a/solution.py
+++ b/solution.py
@@ -7,9 +7,10 @@
 from jax.experimental.pallas import tpu as pltpu
 from jax.sharding import PartitionSpec as P
 
-CHUNKS = 2
+CHUNKS = 3
 AXES = ("site", "sector")
 LIMIT = 20 << 20
+OPEN_LIMIT = 60 << 20
 SMEM = pl.BlockSpec(memory_space=pltpu.SMEM)
 VMEM = pl.BlockSpec(memory_space=pltpu.VMEM)
 ANY = pl.BlockSpec(memory_space=pl.ANY)
@@ -44,14 +45,14 @@
 
 
 def product(e, ket_block, bra_rows, flag):
-    moved = across(e, ket_block) * flag.astype(jnp.float32)
+    moved = across(e, ket_block) * flag
     return down(bra_rows, moved.astype(jnp.bfloat16))
 
 
 def group(states, e, row, ket, bra, flags, pair, total):
     rows = slice(row, row + e.shape[0])
     for s in states:
-        part = product(e, ket[0, pair, s, 0], bra[0, s, 0, rows], flags[0, s, 0])
+        part = product(e, ket[0, pair, s, 0], bra[0, s, 0, rows], flags[s, :1])
         total = part if total is None else total + part
     return total
 
@@ -82,36 +83,56 @@
         for s in states:
             for copy in copies[i]:
                 copy.wait()
-            part = product(e, ket_buf[i], bra_buf[i], flags[0, s, 0])
+            part = product(e, ket_buf[i], bra_buf[i], flags[0, s, 0].astype(jnp.float32))
             total = part if total is None else total + part
             i += 1
         out[...] = total.astype(jnp.bfloat16)
 
 
-def step_kernel(step, row, fresh, added, groups, dims, flags, *refs):
+def setup_kernel(dims, flags, env, after, window, flag_rows, entering):
+    del after
+    used = dims[lax.axis_index("site") + 1, lax.axis_index("sector")]
+    window[...] = jnp.where(inside(window.shape, 0, used), 1.0, 0.0).astype(window.dtype)
+    for s in range(flag_rows.shape[0]):
+        flag_rows[s] = jnp.zeros(flag_rows.shape[1:], jnp.float32) + flags[0, s, 0].astype(jnp.float32)
+    for p in range(entering.shape[0]):
+        entering[p] = cut(env[p + 1, 0], 0, dims)
+
+
+def step_kernel(step, row, fresh, added, groups, flags, *refs):
     refs = list(refs)
-    env = refs.pop(0) if fresh else None
+    entering = refs.pop(0) if fresh else None
     held, ket, bra = refs[:3]
     before = refs[3 : 3 + len(groups)] if added else [None] * len(groups)
     outs = refs[3 + len(groups) * added :]
     pair = pair_of(step, ket.shape[1])
     e = held[...]
     if fresh:
-        entering = cut(env[step, 0, row : row + e.shape[0]], row, dims)
-        e = jnp.where(lax.axis_index("site") == 0, entering, e)
+        e = jnp.where(lax.axis_index("site") == 0, entering[step - 1, row : row + e.shape[0]], e)
     for states, start, out in zip(groups, before, outs):
         total = group(states, e, row, ket, bra, flags, pair, None if start is None else start[...])
         out[...] = total.astype(out.dtype)
 
 
-def sum_kernel(row, bond_site, dims, none, other, came, out):
+def summed(row, window, none, other, came):
     rows = slice(row, row + came.shape[0])
     sector = lax.axis_index("sector")
-    used = dims[lax.axis_index("site") + 1, sector]
     total = none[rows].astype(jnp.float32)
     total = total + jnp.where(sector % 2 == 1, other[rows].astype(jnp.float32), 0.0)
     total = total + jnp.where(sector >= 2, came[...].astype(jnp.float32), 0.0)
-    out[...] = jnp.where(inside(total.shape, row, used), total, 0.0).astype(jnp.bfloat16)
+    return (total * window[rows].astype(jnp.float32)).astype(jnp.bfloat16)
+
+
+def sum_kernel(row, window, none, other, came, out):
+    out[...] = summed(row, window, none, other, came)
+
+
+def written(pair, pairs, row, block, out, sem):
+    @pl.when(jnp.logical_and(pair >= 0, pair < pairs))
+    def _():
+        copy = pltpu.make_async_copy(block, out.at[0, pair, 0, pl.ds(row, block.shape[0])], sem)
+        copy.start()
+        copy.wait()
 
 
 def write_kernel(step, cuts, pairs, *refs):
@@ -130,12 +151,18 @@
             copy.wait()
 
 
-def call(kernel, in_specs, out_shape, flops=0, moved=0, **more):
+def last_kernel(step, pairs, row, window, none, other, came, before, out, block, sem):
+    del before
+    block[...] = summed(row, window, none, other, came)
+    written(step - lax.axis_index("site"), pairs, row, block, out, sem)
+
+
+def call(kernel, in_specs, out_shape, flops=0, moved=0, limit=LIMIT, **more):
     return pl.pallas_call(
         kernel,
         out_shape=out_shape,
         in_specs=in_specs,
-        compiler_params=pltpu.CompilerParams(vmem_limit_bytes=LIMIT),
+        compiler_params=pltpu.CompilerParams(vmem_limit_bytes=limit),
         cost_estimate=pl.CostEstimate(flops=flops, bytes_accessed=moved, transcendentals=0),
         **more,
     )
@@ -175,21 +202,23 @@
             [SMEM, SMEM, ANY, ANY, ANY],
             [block(width)] * len(groups),
             4 * count * width**3,
+            limit=OPEN_LIMIT,
             scratch_shapes=scratch,
             out_specs=[VMEM] * len(groups),
         )(sector_dims, flags, env_in, ket, bra)
 
     def chunk(step, k, groups, held, before, dtype):
         fresh = step < pairs
-        operands = [sector_dims, flags] + ([env_in] if fresh else []) + [held, ket, bra] + before
+        operands = [flag_rows] + ([entering] if fresh else []) + [held, ket, bra] + before
         return call(
             functools.partial(step_kernel, step, cuts[k], fresh, len(before) > 0, groups),
-            [SMEM, SMEM] + [VMEM] * (len(operands) - 2),
+            [VMEM] * len(operands),
             [block(width, dtype)] * len(groups),
             4 * sum(len(states) for states in groups) * (cuts[k + 1] - cuts[k]) * width**2,
             out_specs=[VMEM] * len(groups),
         )(*operands)
 
+    whole = jax.ShapeDtypeStruct((1, pairs, 1, width, width), jnp.bfloat16)
     result = None
     held = None
     for step in range(steps):
@@ -197,6 +226,16 @@
             (single,) = opening([(1, 2)])
             other = lax.ppermute(single, AXES, swap_pairs)
             double, none = opening([(3,), (0,)])
+            window, flag_rows, entering = call(
+                setup_kernel,
+                [SMEM, SMEM, VMEM, ANY],
+                [
+                    block(width),
+                    jax.ShapeDtypeStruct((ket.shape[2], 8, width), jnp.float32),
+                    jax.ShapeDtypeStruct((max(pairs - 1, 1), width, width), jnp.bfloat16),
+                ],
+                out_specs=[VMEM] * 3,
+            )(sector_dims, flags, env_in, double)
         else:
             total = []
             for k in range(CHUNKS - 1):
@@ -211,22 +250,33 @@
             part = jnp.where(even, other[rows].astype(jnp.float32), 0.0)
             up = (double[rows].astype(jnp.float32) + part).astype(jnp.bfloat16)
             came = lax.ppermute(up, AXES, up_pairs)
-            fresh.append(
-                call(
-                    functools.partial(sum_kernel, cuts[k], step),
-                    [SMEM] + [VMEM] * 3,
-                    block(cuts[k + 1] - cuts[k]),
-                    out_specs=VMEM,
-                )(sector_dims, none, other, came)
-            )
-        if step + 1 < steps:
-            held = [lax.ppermute(rows, AXES, next_pairs) for rows in fresh]
-        shape = jax.ShapeDtypeStruct((1, pairs, 1, width, width), jnp.bfloat16)
+            operands = (window, none, other, came)
+            if step + 1 < steps:
+                fresh.append(
+                    call(
+                        functools.partial(sum_kernel, cuts[k]),
+                        [VMEM] * 4,
+                        block(cuts[k + 1] - cuts[k]),
+                        out_specs=VMEM,
+                    )(*operands)
+                )
+            else:
+                result = call(
+                    functools.partial(last_kernel, step, pairs, cuts[k]),
+                    [VMEM] * 4 + [ANY],
+                    whole,
+                    out_specs=ANY,
+                    scratch_shapes=[pltpu.VMEM((cuts[k + 1] - cuts[k], width), jnp.bfloat16), pltpu.SemaphoreType.DMA],
+                    input_output_aliases={4: 0},
+                )(*operands, result)
+        if step + 1 == steps:
+            break
+        held = [lax.ppermute(rows, AXES, next_pairs) for rows in fresh]
         operands = fresh + ([] if result is None else [result])
         result = call(
             functools.partial(write_kernel, step, cuts, pairs),
             [VMEM] * CHUNKS + [ANY] * (len(operands) - CHUNKS),
-            shape,
+            whole,
             out_specs=ANY,
             scratch_shapes=[pltpu.SemaphoreType.DMA((CHUNKS,))],
             input_output_aliases={} if result is None else {CHUNKS: 0},

time: 152 us -> 136 us (0.89)
  waiting for transfers between devices: 91.2 us -> 75.6 us
  starting transfers between devices: 11 us -> 19.7 us
  Pallas kernels: 38.6 us -> 33.2 us
  local copies, waits for them, and re-layouts: 8.63 us -> 3.41 us
    ppermute x10 -> x15, waiting for transfers between devices: 66.7 us -> 56.5 us  [per_device(): came = lax.ppermute(up, AXES, up_pairs)]
    ppermute x8 -> x12, waiting for transfers between devices: 23.4 us -> 15.2 us  [per_device(): held = [lax.ppermute(rows, AXES, next_pairs) for rows in fresh]]
    ppermute x10 -> x15, starting transfers between devices: 5.63 us -> 12 us  [per_device(): came = lax.ppermute(up, AXES, up_pairs)]
    pallas_call x10 -> x16, Pallas kernels: 8.83 us -> 2.66 us  [the longest x12 1.43 us: per_device(): call(functools.partial(sum_kernel, cuts[k]), [VMEM] * 4, block(cuts[k + 1...]
    unnamed x19 -> x15, local copies, waits for them, and re-layouts: 8.63 us -> 3.41 us
    pallas_call x2, Pallas kernels: 5.84 us -> 9.17 us  [opening(): call(functools.partial(open_kernel, 0, groups), [SMEM, SMEM, ANY, ANY, AN...]
    ppermute x5, waiting for transfers between devices: 1.05 us -> 3.94 us  [per_device(): other = lax.ppermute(single, AXES, swap_pairs)]
    pallas_call x12 -> x16, Pallas kernels: 22.2 us -> 19.7 us  [chunk(): call(functools.partial(step_kernel, step, cuts[k], fresh, len(before) > 0...]
  transfers between devices with their start and end apart: 23 -> 32, of which waited for: 22 -> 26; matrix products, arithmetic and copies ran while one was open for 0% -> 1% of each run, Pallas kernels for 18% -> 18%
where the time goes in v2:
time: 136 us; the launch traced here: 135 us
  waiting for transfers between devices  75.6 us (56%)
  Pallas kernels  33.2 us (24%)
  starting transfers between devices  19.7 us (14%)
  local copies, waits for them, and re-layouts  3.41 us (3%)
  other arithmetic  2.73 us (2%)
    ppermute x15, waiting for transfers between devices, per_device(): came = lax.ppermute(up, AXES, up_pairs)  56.5 us
    pallas_call x16, Pallas kernels, chunk(): call(functools.partial(step_kernel, step, cuts[k], fresh, len(before) > 0...  19.7 us
    ppermute x12, waiting for transfers between devices, per_device(): held = [lax.ppermute(rows, AXES, next_pairs) for rows in fresh]  15.2 us
    ppermute x15, starting transfers between devices, per_device(): came = lax.ppermute(up, AXES, up_pairs)  12 us
    pallas_call x2, Pallas kernels, opening(): call(functools.partial(open_kernel, 0, groups), [SMEM, SMEM, ANY, ANY, AN...  9.17 us
    ppermute x12, starting transfers between devices, per_device(): held = [lax.ppermute(rows, AXES, next_pairs) for rows in fresh]  6.87 us
    ppermute x5, waiting for transfers between devices, per_device(): other = lax.ppermute(single, AXES, swap_pairs)  3.94 us
    unnamed x15, local copies, waits for them, and re-layouts  3.41 us
  transfers between devices with their start and end apart: 32, of which 26 were waited for; matrix products, arithmetic and copies ran while one was open for 1% of the time, Pallas kernels for 18%

profile of v2, /device:TPU:0, one launch (start us, length us, event | category | flops | bytes accessed | tf_op | source)
XLA Modules:
  0.0 135.3 jit_solution(7516064461514159959)
XLA Ops:
  1.3 4.5 %shard_map.57 = bf16[512,512]{1,0:T(8,128)(2,1)} custom-call(s32[5,8]{1,0:T(8,128)} %dims.5, s32[1,4,1]{2,1,0:T(4,128)} %copy.13.flags, bf16[2,1,512,512]{3,2,1,0:T(8,128)(2,1)} %env.5, bf16[1,2,4,1,512,512]{5,4,3,2,1,0:T(8,128)(2,1)} %refs_1_.23, bf16[1,4,1,512,512]{4,3,2,1,0:T(8,128)(2,1)} %refs_2_.31), custom_call_target="tpu_custom_call" | custom-call | flops 1073741824 | tf_op jit(solution)/shard_map/pallas_call | solution.py:200
  6.4 4.7 %shard_map.55 = (bf16[512,512]{1,0:T(8,128)(2,1)}, bf16[512,512]{1,0:T(8,128)(2,1)}) custom-call(s32[5,8]{1,0:T(8,128)} %dims.5, s32[1,4,1]{2,1,0:T(4,128)} %copy.13.flags, bf16[2,1,512,512]{3,2,1,0:T(8,128)(2,1)} %env.5, bf16[1,2,4,1,512,512]{5,4,3,2,1,0:T(8,128)(2,1)} %refs_1_.23, bf16[1,4,1,512,512]{4,3,2,1,0:T(8,128)(2,1)} %refs_2_.31), custom_call_target="tpu_custom_call" | custom-call | flops 1073741824 | tf_op jit(solution)/shard_map/pallas_call | solution.py:200
  12.1 2.6 %collective-permute-start.5 = (bf16[160,512]{1,0:T(8,128)(2,1)S(1)}, bf16[160,512]{1,0:T(8,128)(2,1)S(1)}, u32[]{:S(2)}, u32[]{:S(2)}) collective-permute-start(bf16[160,512]{1,0:T(8,128)(2,1)S(1)} %add_convert_fusion.14), channel_id=1, source_target_pairs={{0,2},{1,3},{2,4},{3,5},{4,6},{5,7},{6,0},{7,1},{8,10},{9,11},{10,... | collective-permute-start | bytes 491528 | tf_op jit(solution)/shard_map/ppermute | solution.py:252
  15.8 1.8 %collective-permute-start.3 = (bf16[176,512]{1,0:T(8,128)(2,1)S(1)}, bf16[176,512]{1,0:T(8,128)(2,1)S(1)}, u32[]{:S(2)}, u32[]{:S(2)}) collective-permute-start(bf16[176,512]{1,0:T(8,128)(2,1)S(1)} %get-tuple-element.87), channel_id=1, source_target_pairs={{0,2},{1,3},{2,4},{3,5},{4,6},{5,7},{6,0},{7,1},{8,10},{9,11},{10,... | collective-permute-start | bytes 540680 | tf_op jit(solution)/shard_map/ppermute | solution.py:252
  23.0 1.7 %collective-permute-start.6 = (bf16[160,512]{1,0:T(8,128)(2,1)S(1)}, bf16[160,512]{1,0:T(8,128)(2,1)S(1)}, u32[]{:S(2)}, u32[]{:S(2)}) collective-permute-start(bf16[160,512]{1,0:T(8,128)(2,1)S(1)} %shard_map.60.refs_0_), channel_id=1, source_target_pairs={{0,8},{1,9},{2,10},{3,11},{4,12},{5,13},{6,14},{7,15},{8,16},{9,17... | collective-permute-start | bytes 491528 | tf_op jit(solution)/shard_map/ppermute | solution.py:274
  25.8 1.7 %collective-permute-start.4 = (bf16[176,512]{1,0:T(8,128)(2,1)S(1)}, bf16[176,512]{1,0:T(8,128)(2,1)S(1)}, u32[]{:S(2)}, u32[]{:S(2)}) collective-permute-start(bf16[176,512]{1,0:T(8,128)(2,1)S(1)} %shard_map.59.refs_1_), channel_id=1, source_target_pairs={{0,8},{1,9},{2,10},{3,11},{4,12},{5,13},{6,14},{7,15},{8,16},{9,17... | collective-permute-start | bytes 540680 | tf_op jit(solution)/shard_map/ppermute | solution.py:274
  27.5 1.8 %collective-permute-done.1.came = bf16[176,512]{1,0:T(8,128)(2,1)S(1)} collective-permute-done((bf16[176,512]{1,0:T(8,128)(2,1)S(1)}, bf16[176,512]{1,0:T(8,128)(2,1)S(1)}, u32[]{:S(2)}, u32[]{:S(2)}) %collective-permute-start.1) | collective-permute-done | bytes 180256 | tf_op jit(solution)/shard_map/ppermute | solution.py:252
  32.5 1.7 %collective-permute-done.4.refs_1_ = bf16[176,512]{1,0:T(8,128)(2,1)S(1)} collective-permute-done((bf16[176,512]{1,0:T(8,128)(2,1)S(1)}, bf16[176,512]{1,0:T(8,128)(2,1)S(1)}, u32[]{:S(2)}, u32[]{:S(2)}) %collective-permute-start.4) | collective-permute-done | bytes 180256 | tf_op jit(solution)/shard_map/ppermute | solution.py:274
  34.2 1.6 %shard_map.62 = (f32[512,512]{1,0:T(8,128)S(1)}, f32[512,512]{1,0:T(8,128)S(1)}, f32[512,512]{1,0:T(8,128)S(1)}) custom-call(f32[4,8,512]{2,1,0:T(8,128)S(1)} %get-tuple-element.44.flags, bf16[1,512,512]{2,1,0:T(8,128)(2,1)S(1)} %get-tuple-element.45.refs_0_, bf16[176,512]{1,0:T(8,128)(2,1)S(1)} %collective-permute-done.4.refs_1_, ...), custom_call_target="tpu_custom_call" | custom-call | flops 738197504 | tf_op jit(solution)/shard_map/pallas_call | solution.py:213
  41.8 1.8 %collective-permute-start.8 = (bf16[176,512]{1,0:T(8,128)(2,1)S(1)}, bf16[176,512]{1,0:T(8,128)(2,1)S(1)}, u32[]{:S(2)}, u32[]{:S(2)}) collective-permute-start(bf16[176,512]{1,0:T(8,128)(2,1)S(1)} %get-tuple-element.86), channel_id=1, source_target_pairs={{0,2},{1,3},{2,4},{3,5},{4,6},{5,7},{6,0},{7,1},{8,10},{9,11},{10,... | collective-permute-start | bytes 540680 | tf_op jit(solution)/shard_map/ppermute | solution.py:252
  43.6 5.7 %collective-permute-done.12.came = bf16[160,512]{1,0:T(8,128)(2,1)S(1)} collective-permute-done((bf16[160,512]{1,0:T(8,128)(2,1)S(1)}, bf16[160,512]{1,0:T(8,128)(2,1)S(1)}, u32[]{:S(2)}, u32[]{:S(2)}) %collective-permute-start.12) | collective-permute-done | bytes 163872 | tf_op jit(solution)/shard_map/ppermute | solution.py:252
  49.8 3.3 %collective-permute-done.10.came = bf16[176,512]{1,0:T(8,128)(2,1)S(1)} collective-permute-done((bf16[176,512]{1,0:T(8,128)(2,1)S(1)}, bf16[176,512]{1,0:T(8,128)(2,1)S(1)}, u32[]{:S(2)}, u32[]{:S(2)}) %collective-permute-start.10) | collective-permute-done | bytes 180256 | tf_op jit(solution)/shard_map/ppermute | solution.py:252
  53.7 2.5 %collective-permute-done.8.came = bf16[176,512]{1,0:T(8,128)(2,1)S(1)} collective-permute-done((bf16[176,512]{1,0:T(8,128)(2,1)S(1)}, bf16[176,512]{1,0:T(8,128)(2,1)S(1)}, u32[]{:S(2)}, u32[]{:S(2)}) %collective-permute-start.8) | collective-permute-done | bytes 180256 | tf_op jit(solution)/shard_map/ppermute | solution.py:252
  58.2 2.1 %collective-permute-done.11.refs_0_ = bf16[176,512]{1,0:T(8,128)(2,1)S(1)} collective-permute-done((bf16[176,512]{1,0:T(8,128)(2,1)S(1)}, bf16[176,512]{1,0:T(8,128)(2,1)S(1)}, u32[]{:S(2)}, u32[]{:S(2)}) %collective-permute-start.11) | collective-permute-done | bytes 180256 | tf_op jit(solution)/shard_map/ppermute | solution.py:274
  61.9 1.6 %collective-permute-done.9.refs_0_ = bf16[176,512]{1,0:T(8,128)(2,1)S(1)} collective-permute-done((bf16[176,512]{1,0:T(8,128)(2,1)S(1)}, bf16[176,512]{1,0:T(8,128)(2,1)S(1)}, u32[]{:S(2)}, u32[]{:S(2)}) %collective-permute-start.9) | collective-permute-done | bytes 180256 | tf_op jit(solution)/shard_map/ppermute | solution.py:274
  67.9 7.5 %collective-permute-done.19.came = bf16[160,512]{1,0:T(8,128)(2,1)S(1)} collective-permute-done((bf16[160,512]{1,0:T(8,128)(2,1)S(1)}, bf16[160,512]{1,0:T(8,128)(2,1)S(1)}, u32[]{:S(2)}, u32[]{:S(2)}) %collective-permute-start.19) | collective-permute-done | bytes 163872 | tf_op jit(solution)/shard_map/ppermute | solution.py:252
  75.8 3.5 %collective-permute-done.17.came = bf16[176,512]{1,0:T(8,128)(2,1)S(1)} collective-permute-done((bf16[176,512]{1,0:T(8,128)(2,1)S(1)}, bf16[176,512]{1,0:T(8,128)(2,1)S(1)}, u32[]{:S(2)}, u32[]{:S(2)}) %collective-permute-start.17) | collective-permute-done | bytes 180256 | tf_op jit(solution)/shard_map/ppermute | solution.py:252
  79.5 2.8 %collective-permute-done.15.came = bf16[176,512]{1,0:T(8,128)(2,1)S(1)} collective-permute-done((bf16[176,512]{1,0:T(8,128)(2,1)S(1)}, bf16[176,512]{1,0:T(8,128)(2,1)S(1)}, u32[]{:S(2)}, u32[]{:S(2)}) %collective-permute-start.15) | collective-permute-done | bytes 180256 | tf_op jit(solution)/shard_map/ppermute | solution.py:252
  84.0 2.4 %collective-permute-done.18.refs_0_ = bf16[176,512]{1,0:T(8,128)(2,1)S(1)} collective-permute-done((bf16[176,512]{1,0:T(8,128)(2,1)S(1)}, bf16[176,512]{1,0:T(8,128)(2,1)S(1)}, u32[]{:S(2)}, u32[]{:S(2)}) %collective-permute-start.18) | collective-permute-done | bytes 180256 | tf_op jit(solution)/shard_map/ppermute | solution.py:274
  93.5 8.0 %collective-permute-done.26.came = bf16[160,512]{1,0:T(8,128)(2,1)S(1)} collective-permute-done((bf16[160,512]{1,0:T(8,128)(2,1)S(1)}, bf16[160,512]{1,0:T(8,128)(2,1)S(1)}, u32[]{:S(2)}, u32[]{:S(2)}) %collective-permute-start.26) | collective-permute-done | bytes 163872 | tf_op jit(solution)/shard_map/ppermute | solution.py:252
  101.7 3.7 %collective-permute-done.24.came = bf16[176,512]{1,0:T(8,128)(2,1)S(1)} collective-permute-done((bf16[176,512]{1,0:T(8,128)(2,1)S(1)}, bf16[176,512]{1,0:T(8,128)(2,1)S(1)}, u32[]{:S(2)}, u32[]{:S(2)}) %collective-permute-start.24) | collective-permute-done | bytes 180256 | tf_op jit(solution)/shard_map/ppermute | solution.py:252
  105.6 2.8 %collective-permute-done.22.came = bf16[176,512]{1,0:T(8,128)(2,1)S(1)} collective-permute-done((bf16[176,512]{1,0:T(8,128)(2,1)S(1)}, bf16[176,512]{1,0:T(8,128)(2,1)S(1)}, u32[]{:S(2)}, u32[]{:S(2)}) %collective-permute-start.22) | collective-permute-done | bytes 180256 | tf_op jit(solution)/shard_map/ppermute | solution.py:252
  110.1 2.4 %collective-permute-done.25.refs_0_ = bf16[176,512]{1,0:T(8,128)(2,1)S(1)} collective-permute-done((bf16[176,512]{1,0:T(8,128)(2,1)S(1)}, bf16[176,512]{1,0:T(8,128)(2,1)S(1)}, u32[]{:S(2)}, u32[]{:S(2)}) %collective-permute-start.25) | collective-permute-done | bytes 180256 | tf_op jit(solution)/shard_map/ppermute | solution.py:274
  121.4 13.2 %collective-permute-done.31.came = bf16[160,512]{1,0:T(8,128)(2,1)S(1)} collective-permute-done((bf16[160,512]{1,0:T(8,128)(2,1)S(1)}, bf16[160,512]{1,0:T(8,128)(2,1)S(1)}, u32[]{:S(2)}, u32[]{:S(2)}) %collective-permute-start.31) | collective-permute-done | bytes 163872 | tf_op jit(solution)/shard_map/ppermute | solution.py:252
  (103 shorter events, 48.9 us)
Async XLA Ops:
  12.1 9.7 %collective-permute-start.5 = (bf16[160,512]{1,0:T(8,128)(2,1)S(1)}, bf16[160,512]{1,0:T(8,128)(2,1)S(1)}, u32[]{:S(2)}, u32[]{:S(2)}) collective-permute-start(bf16[160,512]{1,0:T(8,128)(2,1)S(1)} %add_convert_fusion.14), channel_id=1, source_target_pairs={{0,2},{1,3},{2,4},{3,5},{4,6},{5,7},{6,0},{7,1},{8,10},{9,11},{10,... | collective-permute-start | bytes 491528 | tf_op jit(solution)/shard_map/ppermute | solution.py:252
  15.8 9.8 %collective-permute-start.3 = (bf16[176,512]{1,0:T(8,128)(2,1)S(1)}, bf16[176,512]{1,0:T(8,128)(2,1)S(1)}, u32[]{:S(2)}, u32[]{:S(2)}) collective-permute-start(bf16[176,512]{1,0:T(8,128)(2,1)S(1)} %get-tuple-element.87), channel_id=1, source_target_pairs={{0,2},{1,3},{2,4},{3,5},{4,6},{5,7},{6,0},{7,1},{8,10},{9,11},{10,... | collective-permute-start | bytes 540680 | tf_op jit(solution)/shard_map/ppermute | solution.py:252
  17.7 11.6 %collective-permute-start.1 = (bf16[176,512]{1,0:T(8,128)(2,1)S(1)}, bf16[176,512]{1,0:T(8,128)(2,1)S(1)}, u32[]{:S(2)}, u32[]{:S(2)}) collective-permute-start(bf16[176,512]{1,0:T(8,128)(2,1)S(1)} %get-tuple-element.88), channel_id=1, source_target_pairs={{0,2},{1,3},{2,4},{3,5},{4,6},{5,7},{6,0},{7,1},{8,10},{9,11},{10,... | collective-permute-start | bytes 540680 | tf_op jit(solution)/shard_map/ppermute | solution.py:252
  23.0 8.0 %collective-permute-start.6 = (bf16[160,512]{1,0:T(8,128)(2,1)S(1)}, bf16[160,512]{1,0:T(8,128)(2,1)S(1)}, u32[]{:S(2)}, u32[]{:S(2)}) collective-permute-start(bf16[160,512]{1,0:T(8,128)(2,1)S(1)} %shard_map.60.refs_0_), channel_id=1, source_target_pairs={{0,8},{1,9},{2,10},{3,11},{4,12},{5,13},{6,14},{7,15},{8,16},{9,17... | collective-permute-start | bytes 491528 | tf_op jit(solution)/shard_map/ppermute | solution.py:274
  25.8 8.4 %collective-permute-start.4 = (bf16[176,512]{1,0:T(8,128)(2,1)S(1)}, bf16[176,512]{1,0:T(8,128)(2,1)S(1)}, u32[]{:S(2)}, u32[]{:S(2)}) collective-permute-start(bf16[176,512]{1,0:T(8,128)(2,1)S(1)} %shard_map.59.refs_1_), channel_id=1, source_target_pairs={{0,8},{1,9},{2,10},{3,11},{4,12},{5,13},{6,14},{7,15},{8,16},{9,17... | collective-permute-start | bytes 540680 | tf_op jit(solution)/shard_map/ppermute | solution.py:274
  29.4 8.0 %collective-permute-start.2 = (bf16[176,512]{1,0:T(8,128)(2,1)S(1)}, bf16[176,512]{1,0:T(8,128)(2,1)S(1)}, u32[]{:S(2)}, u32[]{:S(2)}) collective-permute-start(bf16[176,512]{1,0:T(8,128)(2,1)S(1)} %shard_map.58.refs_2_), channel_id=1, source_target_pairs={{0,8},{1,9},{2,10},{3,11},{4,12},{5,13},{6,14},{7,15},{8,16},{9,17... | collective-permute-start | bytes 540680 | tf_op jit(solution)/shard_map/ppermute | solution.py:274
  40.3 8.9 %collective-permute-start.12 = (bf16[160,512]{1,0:T(8,128)(2,1)S(1)}, bf16[160,512]{1,0:T(8,128)(2,1)S(1)}, u32[]{:S(2)}, u32[]{:S(2)}) collective-permute-start(bf16[160,512]{1,0:T(8,128)(2,1)S(1)} %add_convert_fusion.13), channel_id=1, source_target_pairs={{0,2},{1,3},{2,4},{3,5},{4,6},{5,7},{6,0},{7,1},{8,10},{9,11},{10,... | collective-permute-start | bytes 491528 | tf_op jit(solution)/shard_map/ppermute | solution.py:252
  40.5 12.6 %collective-permute-start.10 = (bf16[176,512]{1,0:T(8,128)(2,1)S(1)}, bf16[176,512]{1,0:T(8,128)(2,1)S(1)}, u32[]{:S(2)}, u32[]{:S(2)}) collective-permute-start(bf16[176,512]{1,0:T(8,128)(2,1)S(1)} %get-tuple-element.85), channel_id=1, source_target_pairs={{0,2},{1,3},{2,4},{3,5},{4,6},{5,7},{6,0},{7,1},{8,10},{9,11},{10,... | collective-permute-start | bytes 540680 | tf_op jit(solution)/shard_map/ppermute | solution.py:252
  41.8 14.4 %collective-permute-start.8 = (bf16[176,512]{1,0:T(8,128)(2,1)S(1)}, bf16[176,512]{1,0:T(8,128)(2,1)S(1)}, u32[]{:S(2)}, u32[]{:S(2)}) collective-permute-start(bf16[176,512]{1,0:T(8,128)(2,1)S(1)} %get-tuple-element.86), channel_id=1, source_target_pairs={{0,2},{1,3},{2,4},{3,5},{4,6},{5,7},{6,0},{7,1},{8,10},{9,11},{10,... | collective-permute-start | bytes 540680 | tf_op jit(solution)/shard_map/ppermute | solution.py:252
  49.4 7.3 %collective-permute-start.13 = (bf16[160,512]{1,0:T(8,128)(2,1)S(1)}, bf16[160,512]{1,0:T(8,128)(2,1)S(1)}, u32[]{:S(2)}, u32[]{:S(2)}) collective-permute-start(bf16[160,512]{1,0:T(8,128)(2,1)S(1)} %shard_map.67.refs_0_), channel_id=1, source_target_pairs={{0,8},{1,9},{2,10},{3,11},{4,12},{5,13},{6,14},{7,15},{8,16},{9,17... | collective-permute-start | bytes 491528 | tf_op jit(solution)/shard_map/ppermute | solution.py:274
  53.2 7.0 %collective-permute-start.11 = (bf16[176,512]{1,0:T(8,128)(2,1)S(1)}, bf16[176,512]{1,0:T(8,128)(2,1)S(1)}, u32[]{:S(2)}, u32[]{:S(2)}) collective-permute-start(bf16[176,512]{1,0:T(8,128)(2,1)S(1)} %shard_map.66.refs_1_), channel_id=1, source_target_pairs={{0,8},{1,9},{2,10},{3,11},{4,12},{5,13},{6,14},{7,15},{8,16},{9,17... | collective-permute-start | bytes 540680 | tf_op jit(solution)/shard_map/ppermute | solution.py:274
  56.3 7.3 %collective-permute-start.9 = (bf16[176,512]{1,0:T(8,128)(2,1)S(1)}, bf16[176,512]{1,0:T(8,128)(2,1)S(1)}, u32[]{:S(2)}, u32[]{:S(2)}) collective-permute-start(bf16[176,512]{1,0:T(8,128)(2,1)S(1)} %shard_map.65.refs_2_), channel_id=1, source_target_pairs={{0,8},{1,9},{2,10},{3,11},{4,12},{5,13},{6,14},{7,15},{8,16},{9,17... | collective-permute-start | bytes 540680 | tf_op jit(solution)/shard_map/ppermute | solution.py:274
  66.5 8.9 %collective-permute-start.19 = (bf16[160,512]{1,0:T(8,128)(2,1)S(1)}, bf16[160,512]{1,0:T(8,128)(2,1)S(1)}, u32[]{:S(2)}, u32[]{:S(2)}) collective-permute-start(bf16[160,512]{1,0:T(8,128)(2,1)S(1)} %add_convert_fusion.12), channel_id=1, source_target_pairs={{0,2},{1,3},{2,4},{3,5},{4,6},{5,7},{6,0},{7,1},{8,10},{9,11},{10,... | collective-permute-start | bytes 491528 | tf_op jit(solution)/shard_map/ppermute | solution.py:252
  66.7 12.6 %collective-permute-start.17 = (bf16[176,512]{1,0:T(8,128)(2,1)S(1)}, bf16[176,512]{1,0:T(8,128)(2,1)S(1)}, u32[]{:S(2)}, u32[]{:S(2)}) collective-permute-start(bf16[176,512]{1,0:T(8,128)(2,1)S(1)} %get-tuple-element.83), channel_id=1, source_target_pairs={{0,2},{1,3},{2,4},{3,5},{4,6},{5,7},{6,0},{7,1},{8,10},{9,11},{10,... | collective-permute-start | bytes 540680 | tf_op jit(solution)/shard_map/ppermute | solution.py:252
  66.7 15.6 %collective-permute-start.15 = (bf16[176,512]{1,0:T(8,128)(2,1)S(1)}, bf16[176,512]{1,0:T(8,128)(2,1)S(1)}, u32[]{:S(2)}, u32[]{:S(2)}) collective-permute-start(bf16[176,512]{1,0:T(8,128)(2,1)S(1)} %get-tuple-element.84), channel_id=1, source_target_pairs={{0,2},{1,3},{2,4},{3,5},{4,6},{5,7},{6,0},{7,1},{8,10},{9,11},{10,... | collective-permute-start | bytes 540680 | tf_op jit(solution)/shard_map/ppermute | solution.py:252
  79.4 7.0 %collective-permute-start.18 = (bf16[176,512]{1,0:T(8,128)(2,1)S(1)}, bf16[176,512]{1,0:T(8,128)(2,1)S(1)}, u32[]{:S(2)}, u32[]{:S(2)}) collective-permute-start(bf16[176,512]{1,0:T(8,128)(2,1)S(1)} %shard_map.73.refs_1_), channel_id=1, source_target_pairs={{0,8},{1,9},{2,10},{3,11},{4,12},{5,13},{6,14},{7,15},{8,16},{9,17... | collective-permute-start | bytes 540680 | tf_op jit(solution)/shard_map/ppermute | solution.py:274
  82.4 7.3 %collective-permute-start.16 = (bf16[176,512]{1,0:T(8,128)(2,1)S(1)}, bf16[176,512]{1,0:T(8,128)(2,1)S(1)}, u32[]{:S(2)}, u32[]{:S(2)}) collective-permute-start(bf16[176,512]{1,0:T(8,128)(2,1)S(1)} %shard_map.72.refs_2_), channel_id=1, source_target_pairs={{0,8},{1,9},{2,10},{3,11},{4,12},{5,13},{6,14},{7,15},{8,16},{9,17... | collective-permute-start | bytes 540680 | tf_op jit(solution)/shard_map/ppermute | solution.py:274
  92.6 8.9 %collective-permute-start.26 = (bf16[160,512]{1,0:T(8,128)(2,1)S(1)}, bf16[160,512]{1,0:T(8,128)(2,1)S(1)}, u32[]{:S(2)}, u32[]{:S(2)}) collective-permute-start(bf16[160,512]{1,0:T(8,128)(2,1)S(1)} %add_convert_fusion.11), channel_id=1, source_target_pairs={{0,2},{1,3},{2,4},{3,5},{4,6},{5,7},{6,0},{7,1},{8,10},{9,11},{10,... | collective-permute-start | bytes 491528 | tf_op jit(solution)/shard_map/ppermute | solution.py:252
  92.8 12.6 %collective-permute-start.24 = (bf16[176,512]{1,0:T(8,128)(2,1)S(1)}, bf16[176,512]{1,0:T(8,128)(2,1)S(1)}, u32[]{:S(2)}, u32[]{:S(2)}) collective-permute-start(bf16[176,512]{1,0:T(8,128)(2,1)S(1)} %get-tuple-element.81), channel_id=1, source_target_pairs={{0,2},{1,3},{2,4},{3,5},{4,6},{5,7},{6,0},{7,1},{8,10},{9,11},{10,... | collective-permute-start | bytes 540680 | tf_op jit(solution)/shard_map/ppermute | solution.py:252
  92.9 15.6 %collective-permute-start.22 = (bf16[176,512]{1,0:T(8,128)(2,1)S(1)}, bf16[176,512]{1,0:T(8,128)(2,1)S(1)}, u32[]{:S(2)}, u32[]{:S(2)}) collective-permute-start(bf16[176,512]{1,0:T(8,128)(2,1)S(1)} %get-tuple-element.82), channel_id=1, source_target_pairs={{0,2},{1,3},{2,4},{3,5},{4,6},{5,7},{6,0},{7,1},{8,10},{9,11},{10,... | collective-permute-start | bytes 540680 | tf_op jit(solution)/shard_map/ppermute | solution.py:252
  108.6 7.3 %collective-permute-start.23 = (bf16[176,512]{1,0:T(8,128)(2,1)S(1)}, bf16[176,512]{1,0:T(8,128)(2,1)S(1)}, u32[]{:S(2)}, u32[]{:S(2)}) collective-permute-start(bf16[176,512]{1,0:T(8,128)(2,1)S(1)} %shard_map.79.refs_2_), channel_id=1, source_target_pairs={{0,8},{1,9},{2,10},{3,11},{4,12},{5,13},{6,14},{7,15},{8,16},{9,17... | collective-permute-start | bytes 540680 | tf_op jit(solution)/shard_map/ppermute | solution.py:274
  118.8 15.9 %collective-permute-start.30 = (bf16[176,512]{1,0:T(8,128)(2,1)S(1)}, bf16[176,512]{1,0:T(8,128)(2,1)S(1)}, u32[]{:S(2)}, u32[]{:S(2)}) collective-permute-start(bf16[176,512]{1,0:T(8,128)(2,1)S(1)} %get-tuple-element.79), channel_id=1, source_target_pairs={{0,2},{1,3},{2,4},{3,5},{4,6},{5,7},{6,0},{7,1},{8,10},{9,11},{10,... | collective-permute-start | bytes 540680 | tf_op jit(solution)/shard_map/ppermute | solution.py:252
  118.9 16.0 %collective-permute-start.29 = (bf16[176,512]{1,0:T(8,128)(2,1)S(1)}, bf16[176,512]{1,0:T(8,128)(2,1)S(1)}, u32[]{:S(2)}, u32[]{:S(2)}) collective-permute-start(bf16[176,512]{1,0:T(8,128)(2,1)S(1)} %get-tuple-element.80), channel_id=1, source_target_pairs={{0,2},{1,3},{2,4},{3,5},{4,6},{5,7},{6,0},{7,1},{8,10},{9,11},{10,... | collective-permute-start | bytes 540680 | tf_op jit(solution)/shard_map/ppermute | solution.py:252
  119.0 15.6 %collective-permute-start.31 = (bf16[160,512]{1,0:T(8,128)(2,1)S(1)}, bf16[160,512]{1,0:T(8,128)(2,1)S(1)}, u32[]{:S(2)}, u32[]{:S(2)}) collective-permute-start(bf16[160,512]{1,0:T(8,128)(2,1)S(1)} %add_convert_fusion.10), channel_id=1, source_target_pairs={{0,2},{1,3},{2,4},{3,5},{4,6},{5,7},{6,0},{7,1},{8,10},{9,11},{10,... | collective-permute-start | bytes 491528 | tf_op jit(solution)/shard_map/ppermute | solution.py:252
  (15 other events, 112.9 us)

commit v3 on v2

--- a/solution.py
+++ b/solution.py
@@ -7,18 +7,20 @@
 from jax.experimental.pallas import tpu as pltpu
 from jax.sharding import PartitionSpec as P
 
-CHUNKS = 3
+PARTS = (11, 11, 10)
+CHUNKS = len(PARTS)
 AXES = ("site", "sector")
 LIMIT = 20 << 20
-OPEN_LIMIT = 60 << 20
+OPEN_LIMIT = 20 << 20
 SMEM = pl.BlockSpec(memory_space=pltpu.SMEM)
 VMEM = pl.BlockSpec(memory_space=pltpu.VMEM)
 ANY = pl.BlockSpec(memory_space=pl.ANY)
 
 
 def bounds(width):
-    tile = 16
-    return [width * k // CHUNKS // tile * tile for k in range(CHUNKS + 1)]
+    tiles = width // 16
+    ends = [sum(PARTS[:k]) * tiles // sum(PARTS) for k in range(len(PARTS) + 1)]
+    return [16 * end for end in ends]
 
 
 def across(a, b):
@@ -57,36 +59,32 @@
     return total
 
 
-def open_kernel(step, groups, dims, flags, env, ket, bra, *refs):
-    outs = refs[: len(groups)]
-    env_buf, ket_buf, bra_buf, sems = refs[len(groups) :]
-    pairs = ket.shape[1]
-    states = [s for states in groups for s in states]
-    pair = pair_of(step, pairs)
-    first = pltpu.make_async_copy(env.at[step, 0], env_buf, sems.at[0])
-    first.start()
-    copies = []
-    for i, s in enumerate(states):
-        copies.append(
-            (
-                pltpu.make_async_copy(ket.at[0, pair, s, 0], ket_buf.at[i], sems.at[1 + 2 * i]),
-                pltpu.make_async_copy(bra.at[0, s, 0], bra_buf.at[i], sems.at[2 + 2 * i]),
-            )
-        )
-        for copy in copies[-1]:
-            copy.start()
-    first.wait()
+def open_kernel(first, later, dims, flags, env, ket, bra, out, e_out, ket_out, bra_out, env_buf, ket_buf, bra_buf, sems):
+    pair = pair_of(0, ket.shape[1])
+    copies = [pltpu.make_async_copy(env.at[0, 0], env_buf, sems.at[0])]
+    for states, kets, bras in ((first, ket_buf, bra_buf), (later, ket_out, bra_out)):
+        for i, s in enumerate(states):
+            copies.append(pltpu.make_async_copy(ket.at[0, pair, s, 0], kets.at[i], sems.at[len(copies)]))
+            copies.append(pltpu.make_async_copy(bra.at[0, s, 0], bras.at[i], sems.at[len(copies)]))
+    for copy in copies:
+        copy.start()
+    copies[0].wait()
     e = cut(env_buf[...], 0, dims)
-    i = 0
-    for states, out in zip(groups, outs):
-        total = None
-        for s in states:
-            for copy in copies[i]:
-                copy.wait()
-            part = product(e, ket_buf[i], bra_buf[i], flags[0, s, 0].astype(jnp.float32))
-            total = part if total is None else total + part
-            i += 1
-        out[...] = total.astype(jnp.bfloat16)
+    e_out[...] = e
+    total = None
+    for i, s in enumerate(first):
+        copies[1 + 2 * i].wait()
+        copies[2 + 2 * i].wait()
+        part = product(e, ket_buf[i], bra_buf[i], flags[s].astype(jnp.float32))
+        total = part if total is None else total + part
+    out[...] = total.astype(jnp.bfloat16)
+    for copy in copies[1 + 2 * len(first) :]:
+        copy.wait()
+
+
+def follow_kernel(later, flags, e, kets, bras, *outs):
+    for i, (s, out) in enumerate(zip(later, outs)):
+        out[...] = product(e[...], kets[i], bras[i], flags[s].astype(jnp.float32)).astype(jnp.bfloat16)
 
 
 def setup_kernel(dims, flags, env, after, window, flag_rows, entering):
@@ -94,7 +92,7 @@
     used = dims[lax.axis_index("site") + 1, lax.axis_index("sector")]
     window[...] = jnp.where(inside(window.shape, 0, used), 1.0, 0.0).astype(window.dtype)
     for s in range(flag_rows.shape[0]):
-        flag_rows[s] = jnp.zeros(flag_rows.shape[1:], jnp.float32) + flags[0, s, 0].astype(jnp.float32)
+        flag_rows[s] = jnp.zeros(flag_rows.shape[1:], jnp.float32) + flags[s].astype(jnp.float32)
     for p in range(entering.shape[0]):
         entering[p] = cut(env[p + 1, 0], 0, dims)
 
@@ -118,7 +116,7 @@
     rows = slice(row, row + came.shape[0])
     sector = lax.axis_index("sector")
     total = none[rows].astype(jnp.float32)
-    total = total + jnp.where(sector % 2 == 1, other[rows].astype(jnp.float32), 0.0)
+    total = total + jnp.where(sector % 2 == 1, other[...].astype(jnp.float32), 0.0)
     total = total + jnp.where(sector >= 2, came[...].astype(jnp.float32), 0.0)
     return (total * window[rows].astype(jnp.float32)).astype(jnp.bfloat16)
 
@@ -183,29 +181,37 @@
 
     everyone = [(j, q) for j in range(sections) for q in range(sectors)]
     swap_pairs = [(at(j, q), at(j, q ^ 1)) for j, q in everyone]
-    up_pairs = [(at(j, q), at(j, (q + 2) % sectors)) for j, q in everyone]
-    next_pairs = [(at(j, q), at((j + 1) % sections, q)) for j, q in everyone]
+
+    def swapped(rows):
+        return [lax.ppermute(rows[cuts[k] : cuts[k + 1]], AXES, swap_pairs) for k in range(CHUNKS)]
+
+    def working(step):
+        return [step - p for p in range(pairs) if 0 <= step - p < sections]
+
+    def up_pairs(step):
+        work = working(step)
+        if step + 1 == steps:
+            return [(at(j, q), at(j, q + 2)) for j in work for q in range(sectors - 2)]
+        half = sections // 2
+        if sections != 4 or len({j % half for j in work}) != len(work) or 1 in work:
+            return [(at(j, q), at(j, (q + 2) % sectors)) for j, q in everyone]
+        found = []
+        for j in range(half):
+            up, back = (j + half, j) if j + half in work else (j, j + half)
+            found += [(at(up, q), at(up, q + 2)) for q in range(sectors - 2)]
+            found += [(at(back, q + 2), at(back, q)) for q in range(sectors - 2)]
+            found += [(at(up, q), at(back, q)) for q in (sectors - 2, sectors - 1)]
+            found += [(at(back, q), at(up, q)) for q in (0, 1)]
+        return found
+
+    def next_pairs(step):
+        moves = [j for j in working(step) if j + 1 < sections]
+        if sections == 4 and 1 not in moves:
+            return [(at(j, q), at(j ^ 1, q)) for j in range(sections) for q in range(sectors)]
+        return [(at(j, q), at((j + 1) % sections, q)) for j in range(sections) for q in range(sectors)]
 
     def block(rows, dtype=jnp.bfloat16):
         return jax.ShapeDtypeStruct((rows, width), dtype)
-
-    def opening(groups):
-        count = sum(len(states) for states in groups)
-        scratch = [
-            pltpu.VMEM((width, width), jnp.bfloat16),
-            pltpu.VMEM((count, width, width), jnp.bfloat16),
-            pltpu.VMEM((count, width, width), jnp.bfloat16),
-            pltpu.SemaphoreType.DMA((1 + 2 * count,)),
-        ]
-        return call(
-            functools.partial(open_kernel, 0, groups),
-            [SMEM, SMEM, ANY, ANY, ANY],
-            [block(width)] * len(groups),
-            4 * count * width**3,
-            limit=OPEN_LIMIT,
-            scratch_shapes=scratch,
-            out_specs=[VMEM] * len(groups),
-        )(sector_dims, flags, env_in, ket, bra)
 
     def chunk(step, k, groups, held, before, dtype):
         fresh = step < pairs
@@ -218,14 +224,37 @@
             out_specs=[VMEM] * len(groups),
         )(*operands)
 
+    flag_here = flags.reshape(flags.shape[1])
     whole = jax.ShapeDtypeStruct((1, pairs, 1, width, width), jnp.bfloat16)
     result = None
     held = None
     for step in range(steps):
         if step == 0:
-            (single,) = opening([(1, 2)])
-            other = lax.ppermute(single, AXES, swap_pairs)
-            double, none = opening([(3,), (0,)])
+            first, later = (1, 2), (3, 0)
+            copies = 1 + 2 * len(first) + 2 * len(later)
+            stack = lambda n: jax.ShapeDtypeStruct((n, width, width), jnp.bfloat16)
+            single, e, kets, bras = call(
+                functools.partial(open_kernel, first, later),
+                [SMEM, SMEM] + [pl.BlockSpec(memory_space=pltpu.HBM)] * 3,
+                [block(width), block(width), stack(len(later)), stack(len(later))],
+                4 * len(first) * width**3,
+                limit=OPEN_LIMIT,
+                scratch_shapes=[
+                    pltpu.VMEM((width, width), jnp.bfloat16),
+                    pltpu.VMEM((len(first), width, width), jnp.bfloat16),
+                    pltpu.VMEM((len(first), width, width), jnp.bfloat16),
+                    pltpu.SemaphoreType.DMA((copies,)),
+                ],
+                out_specs=[VMEM] * 4,
+            )(*[pltpu.with_memory_space_constraint(a, pltpu.HBM) for a in (sector_dims, flag_here, env_in, ket, bra)])
+            other = swapped(single)
+            double, none = call(
+                functools.partial(follow_kernel, later),
+                [SMEM] + [VMEM] * 3,
+                [block(width)] * 2,
+                4 * len(later) * width**3,
+                out_specs=[VMEM] * 2,
+            )(flag_here, e, kets, bras)
             window, flag_rows, entering = call(
                 setup_kernel,
                 [SMEM, SMEM, VMEM, ANY],
@@ -235,22 +264,22 @@
                     jax.ShapeDtypeStruct((max(pairs - 1, 1), width, width), jnp.bfloat16),
                 ],
                 out_specs=[VMEM] * 3,
-            )(sector_dims, flags, env_in, double)
+            )(sector_dims, flag_here, env_in, double)
         else:
             total = []
             for k in range(CHUNKS - 1):
                 total = chunk(step, k, [(1, 2), (3,), (0,)], held[k], list(total), jnp.float32)
             total = list(total)
             (single,) = chunk(step, CHUNKS - 1, [(1, 2)], held[-1], total[:1], jnp.bfloat16)
-            other = lax.ppermute(single, AXES, swap_pairs)
+            other = swapped(single)
             double, none = chunk(step, CHUNKS - 1, [(3,), (0,)], held[-1], total[1:], jnp.bfloat16)
         fresh = []
         for k in range(CHUNKS):
             rows = slice(cuts[k], cuts[k + 1])
-            part = jnp.where(even, other[rows].astype(jnp.float32), 0.0)
+            part = jnp.where(even, other[k].astype(jnp.float32), 0.0)
             up = (double[rows].astype(jnp.float32) + part).astype(jnp.bfloat16)
-            came = lax.ppermute(up, AXES, up_pairs)
-            operands = (window, none, other, came)
+            came = lax.ppermute(up, AXES, up_pairs(step))
+            operands = (window, none, other[k], came)
             if step + 1 < steps:
                 fresh.append(
                     call(
@@ -271,7 +300,7 @@
                 )(*operands, result)
         if step + 1 == steps:
             break
-        held = [lax.ppermute(rows, AXES, next_pairs) for rows in fresh]
+        held = [lax.ppermute(rows, AXES, next_pairs(step)) for rows in fresh]
         operands = fresh + ([] if result is None else [result])
         result = call(
             functools.partial(write_kernel, step, cuts, pairs),

time: 136 us -> 122 us (0.90)
  the two profiles are of different devices: /device:TPU:0 before, /device:TPU:14 now
where the time goes in v3:
time: 122 us
  waiting for transfers between devices  47.6 us (39%)
  starting transfers between devices  39.6 us (32%)
  Pallas kernels  31 us (25%)
  local copies, waits for them, and re-layouts  2.1 us (2%)
    ppermute x15, waiting for transfers between devices, per_device(): came = lax.ppermute(up, AXES, up_pairs(step))  39.3 us
    ppermute x15, starting transfers between devices, per_device(): came = lax.ppermute(up, AXES, up_pairs(step))  21 us
    pallas_call x16, Pallas kernels, chunk(): call(functools.partial(step_kernel, step, cuts[k], fresh, len(before) > 0...  19.7 us
    ppermute x12, starting transfers between devices, per_device(): held = [lax.ppermute(rows, AXES, next_pairs(step)) for rows in fresh]  15.1 us
    ppermute x12, waiting for transfers between devices, per_device(): held = [lax.ppermute(rows, AXES, next_pairs(step)) for rows in fresh]  7.79 us
    pallas_call x1, Pallas kernels, per_device(): call(functools.partial(open_kernel, first, later), [SMEM, SMEM] + [pl.Blo...  3.84 us
    ppermute x15, starting transfers between devices, swapped(): lax.ppermute(rows[cuts[k]:cuts[k + 1]], AXES, swap_pairs)  3.49 us
  transfers between devices with their start and end apart: 42, of which 26 were waited for; matrix products, arithmetic and copies ran while one was open for 1% of the time, Pallas kernels for 19%

profile of v3, /device:TPU:14, one launch (start us, length us, event | category | flops | bytes accessed | tf_op | source)
XLA Modules:
  0.0 121.8 jit_solution(18356447977536622605)
XLA Ops:
  0.0 3.8 %shard_map.55 = (bf16[512,512]{1,0:T(8,128)(2,1)S(1)}, bf16[512,512]{1,0:T(8,128)(2,1)S(1)}, bf16[2,512,512]{2,1,0:T(8,128)(2,1)S(1)}, bf16[2,512,512]{2,1,0:T(8,128)(2,1)S(1)}) custom-call(s32[5,8]{1,0:T(8,128)} %dims.3, s32[4]{0:T(128)} %bitcast.1, bf16[2,1,512,512]{3,2,1,0:T(8,128)(2,1)} %env.3, bf16[1,2,4,1,512,512]{5,4,3,2,1,0:T(8,128)(2,1)} %refs_1_.23, ...), custom_call_target="tpu_custom_call" | custom-call | flops 1073741824 | tf_op jit(solution)/shard_map/pallas_call | solution.py:236
  6.5 2.0 %shard_map.56 = (bf16[512,512]{1,0:T(8,128)(2,1)S(1)}, bf16[512,512]{1,0:T(8,128)(2,1)S(1)}) custom-call(s32[4]{0:T(128)S(1)} %bitcast.2, bf16[512,512]{1,0:T(8,128)(2,1)S(1)} %get-tuple-element.46.e, bf16[2,512,512]{2,1,0:T(8,128)(2,1)S(1)} %get-tuple-element.47.kets, bf16[2,512,512]{2,1,0:T(8,128)(2,1)S(1)} %copy-done.6), custom_call_target="tpu_custom_call" | custom-call | flops 1073741824 | tf_op jit(solution)/shard_map/pallas_call | solution.py:251
  12.1 3.9 %collective-permute-done.7.came = bf16[176,512]{1,0:T(8,128)(2,1)S(1)} collective-permute-done((bf16[176,512]{1,0:T(8,128)(2,1)S(1)}, bf16[176,512]{1,0:T(8,128)(2,1)S(1)}, u32[]{:S(2)}, u32[]{:S(2)}) %collective-permute-start.7) | collective-permute-done | bytes 180256 | tf_op jit(solution)/shard_map/ppermute | solution.py:281
  16.8 3.1 %collective-permute-done.4.came = bf16[176,512]{1,0:T(8,128)(2,1)S(1)} collective-permute-done((bf16[176,512]{1,0:T(8,128)(2,1)S(1)}, bf16[176,512]{1,0:T(8,128)(2,1)S(1)}, u32[]{:S(2)}, u32[]{:S(2)}) %collective-permute-start.4) | collective-permute-done | bytes 180256 | tf_op jit(solution)/shard_map/ppermute | solution.py:281
  20.7 2.2 %collective-permute-done.1.came = bf16[160,512]{1,0:T(8,128)(2,1)S(1)} collective-permute-done((bf16[160,512]{1,0:T(8,128)(2,1)S(1)}, bf16[160,512]{1,0:T(8,128)(2,1)S(1)}, u32[]{:S(2)}, u32[]{:S(2)}) %collective-permute-start.1) | collective-permute-done | bytes 163872 | tf_op jit(solution)/shard_map/ppermute | solution.py:281
  26.0 1.6 %shard_map.62 = (f32[512,512]{1,0:T(8,128)S(1)}, f32[512,512]{1,0:T(8,128)S(1)}, f32[512,512]{1,0:T(8,128)S(1)}) custom-call(f32[4,8,512]{2,1,0:T(8,128)S(1)} %get-tuple-element.51.flags, bf16[1,512,512]{2,1,0:T(8,128)(2,1)S(1)} %get-tuple-element.52.refs_0_, bf16[176,512]{1,0:T(8,128)(2,1)S(1)} %collective-permute-done.5.refs_1_, ...), custom_call_target="tpu_custom_call" | custom-call | flops 738197504 | tf_op jit(solution)/shard_map/pallas_call | solution.py:219
  35.5 3.9 %collective-permute-done.16.came = bf16[176,512]{1,0:T(8,128)(2,1)S(1)} collective-permute-done((bf16[176,512]{1,0:T(8,128)(2,1)S(1)}, bf16[176,512]{1,0:T(8,128)(2,1)S(1)}, u32[]{:S(2)}, u32[]{:S(2)}) %collective-permute-start.16) | collective-permute-done | bytes 180256 | tf_op jit(solution)/shard_map/ppermute | solution.py:281
  40.0 3.2 %collective-permute-done.13.came = bf16[176,512]{1,0:T(8,128)(2,1)S(1)} collective-permute-done((bf16[176,512]{1,0:T(8,128)(2,1)S(1)}, bf16[176,512]{1,0:T(8,128)(2,1)S(1)}, u32[]{:S(2)}, u32[]{:S(2)}) %collective-permute-start.13) | collective-permute-done | bytes 180256 | tf_op jit(solution)/shard_map/ppermute | solution.py:281
  43.9 2.2 %collective-permute-done.10.came = bf16[160,512]{1,0:T(8,128)(2,1)S(1)} collective-permute-done((bf16[160,512]{1,0:T(8,128)(2,1)S(1)}, bf16[160,512]{1,0:T(8,128)(2,1)S(1)}, u32[]{:S(2)}, u32[]{:S(2)}) %collective-permute-start.10) | collective-permute-done | bytes 163872 | tf_op jit(solution)/shard_map/ppermute | solution.py:281
  49.5 1.6 %shard_map.69 = (f32[512,512]{1,0:T(8,128)S(1)}, f32[512,512]{1,0:T(8,128)S(1)}, f32[512,512]{1,0:T(8,128)S(1)}) custom-call(f32[4,8,512]{2,1,0:T(8,128)S(1)} %get-tuple-element.51.flags, bf16[176,512]{1,0:T(8,128)(2,1)S(1)} %collective-permute-done.14.refs_0_, bf16[1,2,4,1,512,512]{5,4,3,2,1,0:T(8,128)(2,1)S(1)} %copy-done, ...), custom_call_target="tpu_custom_call" | custom-call | flops 738197504 | tf_op jit(solution)/shard_map/pallas_call | solution.py:219
  58.5 2.2 %collective-permute-start.19 = (bf16[160,512]{1,0:T(8,128)(2,1)S(1)}, bf16[160,512]{1,0:T(8,128)(2,1)S(1)}, u32[]{:S(2)}, u32[]{:S(2)}) collective-permute-start(bf16[160,512]{1,0:T(8,128)(2,1)S(1)} %add_convert_fusion.12), channel_id=1, source_target_pairs={{0,2},{1,3},{2,4},{3,5},{4,6},{5,7},{6,0},{7,1},{8,10},{9,11},{10,... | collective-permute-start | bytes 491528 | tf_op jit(solution)/shard_map/ppermute | solution.py:281
  60.7 2.2 %collective-permute-done.25.came = bf16[176,512]{1,0:T(8,128)(2,1)S(1)} collective-permute-done((bf16[176,512]{1,0:T(8,128)(2,1)S(1)}, bf16[176,512]{1,0:T(8,128)(2,1)S(1)}, u32[]{:S(2)}, u32[]{:S(2)}) %collective-permute-start.25) | collective-permute-done | bytes 180256 | tf_op jit(solution)/shard_map/ppermute | solution.py:281
  64.5 2.2 %collective-permute-done.22.came = bf16[176,512]{1,0:T(8,128)(2,1)S(1)} collective-permute-done((bf16[176,512]{1,0:T(8,128)(2,1)S(1)}, bf16[176,512]{1,0:T(8,128)(2,1)S(1)}, u32[]{:S(2)}, u32[]{:S(2)}) %collective-permute-start.22) | collective-permute-done | bytes 180256 | tf_op jit(solution)/shard_map/ppermute | solution.py:281
  73.2 1.6 %shard_map.76 = (f32[512,512]{1,0:T(8,128)S(1)}, f32[512,512]{1,0:T(8,128)S(1)}, f32[512,512]{1,0:T(8,128)S(1)}) custom-call(f32[4,8,512]{2,1,0:T(8,128)S(1)} %get-tuple-element.51.flags, bf16[176,512]{1,0:T(8,128)(2,1)S(1)} %collective-permute-done.23.refs_0_, bf16[1,2,4,1,512,512]{5,4,3,2,1,0:T(8,128)(2,1)S(1)} %copy-done, ...), custom_call_target="tpu_custom_call" | custom-call | flops 738197504 | tf_op jit(solution)/shard_map/pallas_call | solution.py:219
  82.3 5.7 %collective-permute-done.34.came = bf16[176,512]{1,0:T(8,128)(2,1)S(1)} collective-permute-done((bf16[176,512]{1,0:T(8,128)(2,1)S(1)}, bf16[176,512]{1,0:T(8,128)(2,1)S(1)}, u32[]{:S(2)}, u32[]{:S(2)}) %collective-permute-start.34) | collective-permute-done | bytes 180256 | tf_op jit(solution)/shard_map/ppermute | solution.py:281
  88.1 2.4 %collective-permute-start.35 = (bf16[176,512]{1,0:T(8,128)(2,1)S(1)}, bf16[176,512]{1,0:T(8,128)(2,1)S(1)}, u32[]{:S(2)}, u32[]{:S(2)}) collective-permute-start(bf16[176,512]{1,0:T(8,128)(2,1)S(1)} %shard_map.81.refs_0_), channel_id=1, source_target_pairs={{0,8},{1,9},{2,10},{3,11},{4,12},{5,13},{6,14},{7,15},{8,0},{9,1},... | collective-permute-start | bytes 540680 | tf_op jit(solution)/shard_map/ppermute | solution.py:303
  92.0 2.4 %collective-permute-start.32 = (bf16[176,512]{1,0:T(8,128)(2,1)S(1)}, bf16[176,512]{1,0:T(8,128)(2,1)S(1)}, u32[]{:S(2)}, u32[]{:S(2)}) collective-permute-start(bf16[176,512]{1,0:T(8,128)(2,1)S(1)} %shard_map.80.refs_1_), channel_id=1, source_target_pairs={{0,8},{1,9},{2,10},{3,11},{4,12},{5,13},{6,14},{7,15},{8,0},{9,1},... | collective-permute-start | bytes 540680 | tf_op jit(solution)/shard_map/ppermute | solution.py:303
  95.1 2.4 %collective-permute-start.29 = (bf16[160,512]{1,0:T(8,128)(2,1)S(1)}, bf16[160,512]{1,0:T(8,128)(2,1)S(1)}, u32[]{:S(2)}, u32[]{:S(2)}) collective-permute-start(bf16[160,512]{1,0:T(8,128)(2,1)S(1)} %shard_map.79.refs_2_), channel_id=1, source_target_pairs={{0,8},{1,9},{2,10},{3,11},{4,12},{5,13},{6,14},{7,15},{8,0},{9,1},... | collective-permute-start | bytes 491528 | tf_op jit(solution)/shard_map/ppermute | solution.py:303
  104.8 1.9 %collective-permute-start.41 = (bf16[176,512]{1,0:T(8,128)(2,1)S(1)}, bf16[176,512]{1,0:T(8,128)(2,1)S(1)}, u32[]{:S(2)}, u32[]{:S(2)}) collective-permute-start(bf16[176,512]{1,0:T(8,128)(2,1)S(1)} %get-tuple-element.87), channel_id=1, source_target_pairs={{24,26},{25,27},{26,28},{27,29},{28,30},{29,31}} | collective-permute-start | bytes 540680 | tf_op jit(solution)/shard_map/ppermute | solution.py:281
  106.7 2.5 %collective-permute-start.39 = (bf16[176,512]{1,0:T(8,128)(2,1)S(1)}, bf16[176,512]{1,0:T(8,128)(2,1)S(1)}, u32[]{:S(2)}, u32[]{:S(2)}) collective-permute-start(bf16[176,512]{1,0:T(8,128)(2,1)S(1)} %get-tuple-element.88), channel_id=1, source_target_pairs={{24,26},{25,27},{26,28},{27,29},{28,30},{29,31}} | collective-permute-start | bytes 540680 | tf_op jit(solution)/shard_map/ppermute | solution.py:281
  109.3 1.9 %collective-permute-start.37 = (bf16[160,512]{1,0:T(8,128)(2,1)S(1)}, bf16[160,512]{1,0:T(8,128)(2,1)S(1)}, u32[]{:S(2)}, u32[]{:S(2)}) collective-permute-start(bf16[160,512]{1,0:T(8,128)(2,1)S(1)} %add_convert_fusion.10), channel_id=1, source_target_pairs={{24,26},{25,27},{26,28},{27,29},{28,30},{29,31}} | collective-permute-start | bytes 491528 | tf_op jit(solution)/shard_map/ppermute | solution.py:281
  112.2 1.9 %collective-permute-done.41.came = bf16[176,512]{1,0:T(8,128)(2,1)S(1)} collective-permute-done((bf16[176,512]{1,0:T(8,128)(2,1)S(1)}, bf16[176,512]{1,0:T(8,128)(2,1)S(1)}, u32[]{:S(2)}, u32[]{:S(2)}) %collective-permute-start.41) | collective-permute-done | bytes 180256 | tf_op jit(solution)/shard_map/ppermute | solution.py:281
  114.9 3.1 %collective-permute-done.39.came = bf16[176,512]{1,0:T(8,128)(2,1)S(1)} collective-permute-done((bf16[176,512]{1,0:T(8,128)(2,1)S(1)}, bf16[176,512]{1,0:T(8,128)(2,1)S(1)}, u32[]{:S(2)}, u32[]{:S(2)}) %collective-permute-start.39) | collective-permute-done | bytes 180256 | tf_op jit(solution)/shard_map/ppermute | solution.py:281
  118.8 2.1 %collective-permute-done.37.came = bf16[160,512]{1,0:T(8,128)(2,1)S(1)} collective-permute-done((bf16[160,512]{1,0:T(8,128)(2,1)S(1)}, bf16[160,512]{1,0:T(8,128)(2,1)S(1)}, u32[]{:S(2)}, u32[]{:S(2)}) %collective-permute-start.37) | collective-permute-done | bytes 163872 | tf_op jit(solution)/shard_map/ppermute | solution.py:281
  (132 shorter events, 58.9 us)
Async XLA Ops:
  8.6 7.5 %collective-permute-start.7 = (bf16[176,512]{1,0:T(8,128)(2,1)S(1)}, bf16[176,512]{1,0:T(8,128)(2,1)S(1)}, u32[]{:S(2)}, u32[]{:S(2)}) collective-permute-start(bf16[176,512]{1,0:T(8,128)(2,1)S(1)} %get-tuple-element.103), channel_id=1, source_target_pairs={{0,2},{1,3},{2,4},{3,5},{4,6},{5,7},{18,16},{19,17},{20,18},{21,19... | collective-permute-start | bytes 540680 | tf_op jit(solution)/shard_map/ppermute | solution.py:281
  9.1 10.8 %collective-permute-start.4 = (bf16[176,512]{1,0:T(8,128)(2,1)S(1)}, bf16[176,512]{1,0:T(8,128)(2,1)S(1)}, u32[]{:S(2)}, u32[]{:S(2)}) collective-permute-start(bf16[176,512]{1,0:T(8,128)(2,1)S(1)} %get-tuple-element.104), channel_id=1, source_target_pairs={{0,2},{1,3},{2,4},{3,5},{4,6},{5,7},{18,16},{19,17},{20,18},{21,19... | collective-permute-start | bytes 540680 | tf_op jit(solution)/shard_map/ppermute | solution.py:281
  9.7 13.2 %collective-permute-start.1 = (bf16[160,512]{1,0:T(8,128)(2,1)S(1)}, bf16[160,512]{1,0:T(8,128)(2,1)S(1)}, u32[]{:S(2)}, u32[]{:S(2)}) collective-permute-start(bf16[160,512]{1,0:T(8,128)(2,1)S(1)} %add_convert_fusion.14), channel_id=1, source_target_pairs={{0,2},{1,3},{2,4},{3,5},{4,6},{5,7},{18,16},{19,17},{20,18},{21,19... | collective-permute-start | bytes 491528 | tf_op jit(solution)/shard_map/ppermute | solution.py:281
  16.2 7.4 %collective-permute-start.8 = (bf16[176,512]{1,0:T(8,128)(2,1)S(1)}, bf16[176,512]{1,0:T(8,128)(2,1)S(1)}, u32[]{:S(2)}, u32[]{:S(2)}) collective-permute-start(bf16[176,512]{1,0:T(8,128)(2,1)S(1)} %shard_map.60.refs_0_), channel_id=1, source_target_pairs={{0,8},{1,9},{2,10},{3,11},{4,12},{5,13},{6,14},{7,15},{8,0},{9,1},... | collective-permute-start | bytes 540680 | tf_op jit(solution)/shard_map/ppermute | solution.py:303
  31.9 7.5 %collective-permute-start.16 = (bf16[176,512]{1,0:T(8,128)(2,1)S(1)}, bf16[176,512]{1,0:T(8,128)(2,1)S(1)}, u32[]{:S(2)}, u32[]{:S(2)}) collective-permute-start(bf16[176,512]{1,0:T(8,128)(2,1)S(1)} %get-tuple-element.99), channel_id=1, source_target_pairs={{0,2},{1,3},{2,4},{3,5},{4,6},{5,7},{6,0},{7,1},{8,10},{9,11},{10,... | collective-permute-start | bytes 540680 | tf_op jit(solution)/shard_map/ppermute | solution.py:281
  33.5 9.7 %collective-permute-start.13 = (bf16[176,512]{1,0:T(8,128)(2,1)S(1)}, bf16[176,512]{1,0:T(8,128)(2,1)S(1)}, u32[]{:S(2)}, u32[]{:S(2)}) collective-permute-start(bf16[176,512]{1,0:T(8,128)(2,1)S(1)} %get-tuple-element.100), channel_id=1, source_target_pairs={{0,2},{1,3},{2,4},{3,5},{4,6},{5,7},{6,0},{7,1},{8,10},{9,11},{10,... | collective-permute-start | bytes 540680 | tf_op jit(solution)/shard_map/ppermute | solution.py:281
  35.2 11.0 %collective-permute-start.10 = (bf16[160,512]{1,0:T(8,128)(2,1)S(1)}, bf16[160,512]{1,0:T(8,128)(2,1)S(1)}, u32[]{:S(2)}, u32[]{:S(2)}) collective-permute-start(bf16[160,512]{1,0:T(8,128)(2,1)S(1)} %add_convert_fusion.13), channel_id=1, source_target_pairs={{0,2},{1,3},{2,4},{3,5},{4,6},{5,7},{6,0},{7,1},{8,10},{9,11},{10,... | collective-permute-start | bytes 491528 | tf_op jit(solution)/shard_map/ppermute | solution.py:281
  39.5 7.3 %collective-permute-start.17 = (bf16[176,512]{1,0:T(8,128)(2,1)S(1)}, bf16[176,512]{1,0:T(8,128)(2,1)S(1)}, u32[]{:S(2)}, u32[]{:S(2)}) collective-permute-start(bf16[176,512]{1,0:T(8,128)(2,1)S(1)} %shard_map.67.refs_0_), channel_id=1, source_target_pairs={{0,8},{1,9},{2,10},{3,11},{4,12},{5,13},{6,14},{7,15},{8,16},{9,17... | collective-permute-start | bytes 540680 | tf_op jit(solution)/shard_map/ppermute | solution.py:303
  46.3 6.2 %collective-permute-start.11 = (bf16[160,512]{1,0:T(8,128)(2,1)S(1)}, bf16[160,512]{1,0:T(8,128)(2,1)S(1)}, u32[]{:S(2)}, u32[]{:S(2)}) collective-permute-start(bf16[160,512]{1,0:T(8,128)(2,1)S(1)} %shard_map.65.refs_2_), channel_id=1, source_target_pairs={{0,8},{1,9},{2,10},{3,11},{4,12},{5,13},{6,14},{7,15},{8,16},{9,17... | collective-permute-start | bytes 491528 | tf_op jit(solution)/shard_map/ppermute | solution.py:303
  55.2 7.7 %collective-permute-start.25 = (bf16[176,512]{1,0:T(8,128)(2,1)S(1)}, bf16[176,512]{1,0:T(8,128)(2,1)S(1)}, u32[]{:S(2)}, u32[]{:S(2)}) collective-permute-start(bf16[176,512]{1,0:T(8,128)(2,1)S(1)} %get-tuple-element.95), channel_id=1, source_target_pairs={{0,2},{1,3},{2,4},{3,5},{4,6},{5,7},{6,0},{7,1},{8,10},{9,11},{10,... | collective-permute-start | bytes 540680 | tf_op jit(solution)/shard_map/ppermute | solution.py:281
  56.8 9.9 %collective-permute-start.22 = (bf16[176,512]{1,0:T(8,128)(2,1)S(1)}, bf16[176,512]{1,0:T(8,128)(2,1)S(1)}, u32[]{:S(2)}, u32[]{:S(2)}) collective-permute-start(bf16[176,512]{1,0:T(8,128)(2,1)S(1)} %get-tuple-element.96), channel_id=1, source_target_pairs={{0,2},{1,3},{2,4},{3,5},{4,6},{5,7},{6,0},{7,1},{8,10},{9,11},{10,... | collective-permute-start | bytes 540680 | tf_op jit(solution)/shard_map/ppermute | solution.py:281
  58.5 11.4 %collective-permute-start.19 = (bf16[160,512]{1,0:T(8,128)(2,1)S(1)}, bf16[160,512]{1,0:T(8,128)(2,1)S(1)}, u32[]{:S(2)}, u32[]{:S(2)}) collective-permute-start(bf16[160,512]{1,0:T(8,128)(2,1)S(1)} %add_convert_fusion.12), channel_id=1, source_target_pairs={{0,2},{1,3},{2,4},{3,5},{4,6},{5,7},{6,0},{7,1},{8,10},{9,11},{10,... | collective-permute-start | bytes 491528 | tf_op jit(solution)/shard_map/ppermute | solution.py:281
  63.0 8.5 %collective-permute-start.26 = (bf16[176,512]{1,0:T(8,128)(2,1)S(1)}, bf16[176,512]{1,0:T(8,128)(2,1)S(1)}, u32[]{:S(2)}, u32[]{:S(2)}) collective-permute-start(bf16[176,512]{1,0:T(8,128)(2,1)S(1)} %shard_map.74.refs_0_), channel_id=1, source_target_pairs={{0,8},{1,9},{2,10},{3,11},{4,12},{5,13},{6,14},{7,15},{8,16},{9,17... | collective-permute-start | bytes 540680 | tf_op jit(solution)/shard_map/ppermute | solution.py:303
  66.9 6.3 %collective-permute-start.23 = (bf16[176,512]{1,0:T(8,128)(2,1)S(1)}, bf16[176,512]{1,0:T(8,128)(2,1)S(1)}, u32[]{:S(2)}, u32[]{:S(2)}) collective-permute-start(bf16[176,512]{1,0:T(8,128)(2,1)S(1)} %shard_map.73.refs_1_), channel_id=1, source_target_pairs={{0,8},{1,9},{2,10},{3,11},{4,12},{5,13},{6,14},{7,15},{8,16},{9,17... | collective-permute-start | bytes 540680 | tf_op jit(solution)/shard_map/ppermute | solution.py:303
  70.1 6.3 %collective-permute-start.20 = (bf16[160,512]{1,0:T(8,128)(2,1)S(1)}, bf16[160,512]{1,0:T(8,128)(2,1)S(1)}, u32[]{:S(2)}, u32[]{:S(2)}) collective-permute-start(bf16[160,512]{1,0:T(8,128)(2,1)S(1)} %shard_map.72.refs_2_), channel_id=1, source_target_pairs={{0,8},{1,9},{2,10},{3,11},{4,12},{5,13},{6,14},{7,15},{8,16},{9,17... | collective-permute-start | bytes 491528 | tf_op jit(solution)/shard_map/ppermute | solution.py:303
  79.1 8.9 %collective-permute-start.34 = (bf16[176,512]{1,0:T(8,128)(2,1)S(1)}, bf16[176,512]{1,0:T(8,128)(2,1)S(1)}, u32[]{:S(2)}, u32[]{:S(2)}) collective-permute-start(bf16[176,512]{1,0:T(8,128)(2,1)S(1)} %get-tuple-element.91), channel_id=1, source_target_pairs={{16,18},{17,19},{18,20},{19,21},{20,22},{21,23},{2,0},{3,1},{4,2},... | collective-permute-start | bytes 540680 | tf_op jit(solution)/shard_map/ppermute | solution.py:281
  80.2 11.7 %collective-permute-start.31 = (bf16[176,512]{1,0:T(8,128)(2,1)S(1)}, bf16[176,512]{1,0:T(8,128)(2,1)S(1)}, u32[]{:S(2)}, u32[]{:S(2)}) collective-permute-start(bf16[176,512]{1,0:T(8,128)(2,1)S(1)} %get-tuple-element.92), channel_id=1, source_target_pairs={{16,18},{17,19},{18,20},{19,21},{20,22},{21,23},{2,0},{3,1},{4,2},... | collective-permute-start | bytes 540680 | tf_op jit(solution)/shard_map/ppermute | solution.py:281
  81.8 13.2 %collective-permute-start.28 = (bf16[160,512]{1,0:T(8,128)(2,1)S(1)}, bf16[160,512]{1,0:T(8,128)(2,1)S(1)}, u32[]{:S(2)}, u32[]{:S(2)}) collective-permute-start(bf16[160,512]{1,0:T(8,128)(2,1)S(1)} %add_convert_fusion.11), channel_id=1, source_target_pairs={{16,18},{17,19},{18,20},{19,21},{20,22},{21,23},{2,0},{3,1},{4,2},... | collective-permute-start | bytes 491528 | tf_op jit(solution)/shard_map/ppermute | solution.py:281
  88.1 9.4 %collective-permute-start.35 = (bf16[176,512]{1,0:T(8,128)(2,1)S(1)}, bf16[176,512]{1,0:T(8,128)(2,1)S(1)}, u32[]{:S(2)}, u32[]{:S(2)}) collective-permute-start(bf16[176,512]{1,0:T(8,128)(2,1)S(1)} %shard_map.81.refs_0_), channel_id=1, source_target_pairs={{0,8},{1,9},{2,10},{3,11},{4,12},{5,13},{6,14},{7,15},{8,0},{9,1},... | collective-permute-start | bytes 540680 | tf_op jit(solution)/shard_map/ppermute | solution.py:303
  92.0 7.1 %collective-permute-start.32 = (bf16[176,512]{1,0:T(8,128)(2,1)S(1)}, bf16[176,512]{1,0:T(8,128)(2,1)S(1)}, u32[]{:S(2)}, u32[]{:S(2)}) collective-permute-start(bf16[176,512]{1,0:T(8,128)(2,1)S(1)} %shard_map.80.refs_1_), channel_id=1, source_target_pairs={{0,8},{1,9},{2,10},{3,11},{4,12},{5,13},{6,14},{7,15},{8,0},{9,1},... | collective-permute-start | bytes 540680 | tf_op jit(solution)/shard_map/ppermute | solution.py:303
  95.1 6.9 %collective-permute-start.29 = (bf16[160,512]{1,0:T(8,128)(2,1)S(1)}, bf16[160,512]{1,0:T(8,128)(2,1)S(1)}, u32[]{:S(2)}, u32[]{:S(2)}) collective-permute-start(bf16[160,512]{1,0:T(8,128)(2,1)S(1)} %shard_map.79.refs_2_), channel_id=1, source_target_pairs={{0,8},{1,9},{2,10},{3,11},{4,12},{5,13},{6,14},{7,15},{8,0},{9,1},... | collective-permute-start | bytes 491528 | tf_op jit(solution)/shard_map/ppermute | solution.py:303
  104.8 9.3 %collective-permute-start.41 = (bf16[176,512]{1,0:T(8,128)(2,1)S(1)}, bf16[176,512]{1,0:T(8,128)(2,1)S(1)}, u32[]{:S(2)}, u32[]{:S(2)}) collective-permute-start(bf16[176,512]{1,0:T(8,128)(2,1)S(1)} %get-tuple-element.87), channel_id=1, source_target_pairs={{24,26},{25,27},{26,28},{27,29},{28,30},{29,31}} | collective-permute-start | bytes 540680 | tf_op jit(solution)/shard_map/ppermute | solution.py:281
  106.7 11.2 %collective-permute-start.39 = (bf16[176,512]{1,0:T(8,128)(2,1)S(1)}, bf16[176,512]{1,0:T(8,128)(2,1)S(1)}, u32[]{:S(2)}, u32[]{:S(2)}) collective-permute-start(bf16[176,512]{1,0:T(8,128)(2,1)S(1)} %get-tuple-element.88), channel_id=1, source_target_pairs={{24,26},{25,27},{26,28},{27,29},{28,30},{29,31}} | collective-permute-start | bytes 540680 | tf_op jit(solution)/shard_map/ppermute | solution.py:281
  109.3 11.6 %collective-permute-start.37 = (bf16[160,512]{1,0:T(8,128)(2,1)S(1)}, bf16[160,512]{1,0:T(8,128)(2,1)S(1)}, u32[]{:S(2)}, u32[]{:S(2)}) collective-permute-start(bf16[160,512]{1,0:T(8,128)(2,1)S(1)} %add_convert_fusion.10), channel_id=1, source_target_pairs={{24,26},{25,27},{26,28},{27,29},{28,30},{29,31}} | collective-permute-start | bytes 491528 | tf_op jit(solution)/shard_map/ppermute | solution.py:281
  (25 other events, 116.3 us)

commit v4 on v3

--- a/solution.py
+++ b/solution.py
@@ -7,8 +7,9 @@
 from jax.experimental.pallas import tpu as pltpu
 from jax.sharding import PartitionSpec as P
 
-PARTS = (11, 11, 10)
+PARTS = (10, 11, 11)
 CHUNKS = len(PARTS)
+LAST_PARTS = (21, 11)
 AXES = ("site", "sector")
 LIMIT = 20 << 20
 OPEN_LIMIT = 20 << 20
@@ -17,9 +18,9 @@
 ANY = pl.BlockSpec(memory_space=pl.ANY)
 
 
-def bounds(width):
+def bounds(width, parts):
     tiles = width // 16
-    ends = [sum(PARTS[:k]) * tiles // sum(PARTS) for k in range(len(PARTS) + 1)]
+    ends = [sum(parts[:k]) * tiles // sum(parts) for k in range(len(parts) + 1)]
     return [16 * end for end in ends]
 
 
@@ -59,45 +60,63 @@
     return total
 
 
-def open_kernel(first, later, dims, flags, env, ket, bra, out, e_out, ket_out, bra_out, env_buf, ket_buf, bra_buf, sems):
+def parted(total, cuts, outs):
+    for start, end, out in zip(cuts, cuts[1:], outs):
+        out[...] = total[start:end].astype(out.dtype)
+
+
+def open_kernel(first, later, cuts, dims_in, flags_in, env, ket, bra, *refs):
+    outs, (e_out, block_out, flag_rows, dims, flags, env_buf, ket_buf, bra_buf, small_sems, sems) = refs[: len(cuts) - 1], refs[len(cuts) - 1 :]
+    ket_out, bra_out = block_out.at[: len(later)], block_out.at[len(later) :]
     pair = pair_of(0, ket.shape[1])
     copies = [pltpu.make_async_copy(env.at[0, 0], env_buf, sems.at[0])]
     for states, kets, bras in ((first, ket_buf, bra_buf), (later, ket_out, bra_out)):
         for i, s in enumerate(states):
             copies.append(pltpu.make_async_copy(ket.at[0, pair, s, 0], kets.at[i], sems.at[len(copies)]))
             copies.append(pltpu.make_async_copy(bra.at[0, s, 0], bras.at[i], sems.at[len(copies)]))
-    for copy in copies:
+    soon = 1 + 2 * len(first)
+    small = [
+        pltpu.make_async_copy(dims_in, dims, small_sems.at[0]),
+        pltpu.make_async_copy(flags_in, flags, small_sems.at[1]),
+    ]
+    for copy in small:
         copy.start()
+    for copy in copies[:soon]:
+        copy.start()
+    for copy in small:
+        copy.wait()
     copies[0].wait()
+    for copy in copies[soon:]:
+        copy.start()
     e = cut(env_buf[...], 0, dims)
     e_out[...] = e
+    for s in range(flag_rows.shape[0]):
+        flag_rows[s] = jnp.zeros(flag_rows.shape[1:], jnp.float32) + flags[s].astype(jnp.float32)
     total = None
     for i, s in enumerate(first):
         copies[1 + 2 * i].wait()
         copies[2 + 2 * i].wait()
         part = product(e, ket_buf[i], bra_buf[i], flags[s].astype(jnp.float32))
         total = part if total is None else total + part
-    out[...] = total.astype(jnp.bfloat16)
+    parted(total, cuts, outs)
     for copy in copies[1 + 2 * len(first) :]:
         copy.wait()
 
 
-def follow_kernel(later, flags, e, kets, bras, *outs):
+def follow_kernel(later, flags, e, blocks, *outs):
     for i, (s, out) in enumerate(zip(later, outs)):
-        out[...] = product(e[...], kets[i], bras[i], flags[s].astype(jnp.float32)).astype(jnp.bfloat16)
-
-
-def setup_kernel(dims, flags, env, after, window, flag_rows, entering):
+        out[...] = product(e[...], blocks[i], blocks[len(later) + i], flags[s, :1]).astype(jnp.bfloat16)
+
+
+def setup_kernel(dims, env, after, window, entering):
     del after
     used = dims[lax.axis_index("site") + 1, lax.axis_index("sector")]
     window[...] = jnp.where(inside(window.shape, 0, used), 1.0, 0.0).astype(window.dtype)
-    for s in range(flag_rows.shape[0]):
-        flag_rows[s] = jnp.zeros(flag_rows.shape[1:], jnp.float32) + flags[s].astype(jnp.float32)
     for p in range(entering.shape[0]):
         entering[p] = cut(env[p + 1, 0], 0, dims)
 
 
-def step_kernel(step, row, fresh, added, groups, flags, *refs):
+def step_kernel(step, row, fresh, added, groups, cuts, flags, *refs):
     refs = list(refs)
     entering = refs.pop(0) if fresh else None
     held, ket, bra = refs[:3]
@@ -109,7 +128,10 @@
         e = jnp.where(lax.axis_index("site") == 0, entering[step - 1, row : row + e.shape[0]], e)
     for states, start, out in zip(groups, before, outs):
         total = group(states, e, row, ket, bra, flags, pair, None if start is None else start[...])
-        out[...] = total.astype(out.dtype)
+        if cuts is None:
+            out[...] = total.astype(out.dtype)
+        else:
+            parted(total, cuts, outs)
 
 
 def summed(row, window, none, other, came):
@@ -173,7 +195,8 @@
     pairs = ket.shape[1]
     width = ket.shape[-1]
     steps = pairs + sections - 1
-    cuts = bounds(width)
+    cuts = bounds(width, PARTS)
+    last_cuts = bounds(width, LAST_PARTS)
     even = sector % 2 == 0
 
     def at(j, q):
@@ -182,8 +205,8 @@
     everyone = [(j, q) for j in range(sections) for q in range(sectors)]
     swap_pairs = [(at(j, q), at(j, q ^ 1)) for j, q in everyone]
 
-    def swapped(rows):
-        return [lax.ppermute(rows[cuts[k] : cuts[k + 1]], AXES, swap_pairs) for k in range(CHUNKS)]
+    def swapped(parts):
+        return [lax.ppermute(part, AXES, swap_pairs) for part in parts]
 
     def working(step):
         return [step - p for p in range(pairs) if 0 <= step - p < sections]
@@ -213,15 +236,18 @@
     def block(rows, dtype=jnp.bfloat16):
         return jax.ShapeDtypeStruct((rows, width), dtype)
 
-    def chunk(step, k, groups, held, before, dtype):
+    def blocks_of(parts):
+        return [block(end - start) for start, end in zip(parts, parts[1:])]
+
+    def chunk(step, k, groups, held, before, dtype, parts=None):
         fresh = step < pairs
         operands = [flag_rows] + ([entering] if fresh else []) + [held, ket, bra] + before
         return call(
-            functools.partial(step_kernel, step, cuts[k], fresh, len(before) > 0, groups),
+            functools.partial(step_kernel, step, cuts[k], fresh, len(before) > 0, groups, parts),
             [VMEM] * len(operands),
-            [block(width, dtype)] * len(groups),
+            [block(width, dtype)] * len(groups) if parts is None else blocks_of(parts),
             4 * sum(len(states) for states in groups) * (cuts[k + 1] - cuts[k]) * width**2,
-            out_specs=[VMEM] * len(groups),
+            out_specs=[VMEM] * (len(groups) if parts is None else len(parts) - 1),
         )(*operands)
 
     flag_here = flags.reshape(flags.shape[1])
@@ -233,48 +259,58 @@
             first, later = (1, 2), (3, 0)
             copies = 1 + 2 * len(first) + 2 * len(later)
             stack = lambda n: jax.ShapeDtypeStruct((n, width, width), jnp.bfloat16)
-            single, e, kets, bras = call(
-                functools.partial(open_kernel, first, later),
-                [SMEM, SMEM] + [pl.BlockSpec(memory_space=pltpu.HBM)] * 3,
-                [block(width), block(width), stack(len(later)), stack(len(later))],
+            *single, e, blocks, flag_rows = call(
+                functools.partial(open_kernel, first, later, cuts),
+                [pl.BlockSpec(memory_space=pltpu.HBM)] * 5,
+                blocks_of(cuts)
+                + [
+                    block(width),
+                    stack(2 * len(later)),
+                    jax.ShapeDtypeStruct((ket.shape[2], 8, width), jnp.float32),
+                ],
                 4 * len(first) * width**3,
                 limit=OPEN_LIMIT,
                 scratch_shapes=[
+                    pltpu.SMEM(sector_dims.shape, jnp.int32),
+                    pltpu.SMEM(flag_here.shape, jnp.int32),
                     pltpu.VMEM((width, width), jnp.bfloat16),
                     pltpu.VMEM((len(first), width, width), jnp.bfloat16),
                     pltpu.VMEM((len(first), width, width), jnp.bfloat16),
+                    pltpu.SemaphoreType.DMA((2,)),
                     pltpu.SemaphoreType.DMA((copies,)),
                 ],
-                out_specs=[VMEM] * 4,
+                out_specs=[VMEM] * (CHUNKS + 3),
             )(*[pltpu.with_memory_space_constraint(a, pltpu.HBM) for a in (sector_dims, flag_here, env_in, ket, bra)])
             other = swapped(single)
             double, none = call(
                 functools.partial(follow_kernel, later),
-                [SMEM] + [VMEM] * 3,
+                [VMEM] * 3,
                 [block(width)] * 2,
                 4 * len(later) * width**3,
                 out_specs=[VMEM] * 2,
-            )(flag_here, e, kets, bras)
-            window, flag_rows, entering = call(
+            )(flag_rows, e, blocks)
+            window, entering = call(
                 setup_kernel,
-                [SMEM, SMEM, VMEM, ANY],
+                [SMEM, VMEM, ANY],
                 [
                     block(width),
-                    jax.ShapeDtypeStruct((ket.shape[2], 8, width), jnp.float32),
                     jax.ShapeDtypeStruct((max(pairs - 1, 1), width, width), jnp.bfloat16),
                 ],
-                out_specs=[VMEM] * 3,
-            )(sector_dims, flag_here, env_in, double)
+                out_specs=[VMEM] * 2,
+            )(sector_dims, env_in, double)
         else:
             total = []
             for k in range(CHUNKS - 1):
                 total = chunk(step, k, [(1, 2), (3,), (0,)], held[k], list(total), jnp.float32)
             total = list(total)
-            (single,) = chunk(step, CHUNKS - 1, [(1, 2)], held[-1], total[:1], jnp.bfloat16)
+            parts = cuts if step + 1 < steps else last_cuts
+            single = chunk(step, CHUNKS - 1, [(1, 2)], held[-1], total[:1], jnp.bfloat16, parts)
             other = swapped(single)
             double, none = chunk(step, CHUNKS - 1, [(3,), (0,)], held[-1], total[1:], jnp.bfloat16)
         fresh = []
-        for k in range(CHUNKS):
+        if step + 1 == steps:
+            cuts = last_cuts
+        for k in range(len(cuts) - 1):
             rows = slice(cuts[k], cuts[k + 1])
             part = jnp.where(even, other[k].astype(jnp.float32), 0.0)
             up = (double[rows].astype(jnp.float32) + part).astype(jnp.bfloat16)

time: 122 us -> 119 us (0.975)
  waiting for transfers between devices: 47.6 us -> 50.5 us
  starting transfers between devices: 39.6 us -> 36.9 us
  local copies, waits for them, and re-layouts: 2.1 us -> 0.01 us
  Pallas kernels: 31 us -> 29.7 us
    ppermute x15 -> x14, waiting for transfers between devices: 39.3 us -> 42.1 us  [per_device(): came = lax.ppermute(up, AXES, up_pairs(step))]
    ppermute x15 -> x14, starting transfers between devices: 21 us -> 18.7 us  [per_device(): came = lax.ppermute(up, AXES, up_pairs(step))]
    unnamed x14 -> x8, local copies, waits for them, and re-layouts: 1.26 us -> 0.01 us
    ppermute x15 -> x14, starting transfers between devices: 3.49 us -> 3.15 us  [swapped(): return [lax.ppermute(part, AXES, swap_pairs) for part in parts]]
  transfers between devices with their start and end apart: 42 -> 40, of which waited for: 26 -> 21; matrix products, arithmetic and copies ran while one was open for 1% -> 1% of each run, Pallas kernels for 19% -> 18%
where the time goes in v4:
time: 119 us; the launch traced here: 118 us
  waiting for transfers between devices  50.5 us (42%)
  starting transfers between devices  36.9 us (31%)
  Pallas kernels  29.7 us (25%)
    ppermute x14, waiting for transfers between devices, per_device(): came = lax.ppermute(up, AXES, up_pairs(step))  42.1 us
    pallas_call x16, Pallas kernels, chunk(): call(functools.partial(step_kernel, step, cuts[k], fresh, len(before) > 0...  19.7 us
    ppermute x14, starting transfers between devices, per_device(): came = lax.ppermute(up, AXES, up_pairs(step))  18.7 us
    ppermute x12, starting transfers between devices, per_device(): held = [lax.ppermute(rows, AXES, next_pairs(step)) for rows in fresh]  15 us
    ppermute x12, waiting for transfers between devices, per_device(): held = [lax.ppermute(rows, AXES, next_pairs(step)) for rows in fresh]  8.05 us
    pallas_call x1, Pallas kernels, per_device(): call(functools.partial(open_kernel, first, later, cuts), [pl.BlockSpec(me...  3.66 us
    ppermute x14, starting transfers between devices, swapped(): return [lax.ppermute(part, AXES, swap_pairs) for part in parts]  3.15 us
  transfers between devices with their start and end apart: 40, of which 21 were waited for; matrix products, arithmetic and copies ran while one was open for 1% of the time, Pallas kernels for 18%

profile of v4, /device:TPU:14, one launch (start us, length us, event | category | flops | bytes accessed | tf_op | source)
XLA Modules:
  0.0 118.4 jit_solution(11551963103226099822)
XLA Ops:
  0.0 3.7 %shard_map.55 = (bf16[160,512]{1,0:T(8,128)(2,1)S(1)}, bf16[176,512]{1,0:T(8,128)(2,1)S(1)}, bf16[176,512]{1,0:T(8,128)(2,1)}, bf16[512,512]{1,0:T(8,128)(2,1)S(...) custom-call(s32[5,8]{1,0:T(8,128)} %dims.1, s32[4]{0:T(128)} %bitcast.1, bf16[2,1,512,512]{3,2,1,0:T(8,128)(2,1)} %env.3, ...), custom_call_target="tpu_custom_call" | custom-call | flops 1073741824 | tf_op jit(solution)/shard_map/pallas_call | solution.py:262
  9.4 3.5 %collective-permute-done.7.came = bf16[160,512]{1,0:T(8,128)(2,1)S(1)} collective-permute-done((bf16[160,512]{1,0:T(8,128)(2,1)S(1)}, bf16[160,512]{1,0:T(8,128)(2,1)S(1)}, u32[]{:S(2)}, u32[]{:S(2)}) %collective-permute-start.7) | collective-permute-done | bytes 163872 | tf_op jit(solution)/shard_map/ppermute | solution.py:317
  13.7 3.1 %collective-permute-done.4.came = bf16[176,512]{1,0:T(8,128)(2,1)S(1)} collective-permute-done((bf16[176,512]{1,0:T(8,128)(2,1)S(1)}, bf16[176,512]{1,0:T(8,128)(2,1)S(1)}, u32[]{:S(2)}, u32[]{:S(2)}) %collective-permute-start.4) | collective-permute-done | bytes 180256 | tf_op jit(solution)/shard_map/ppermute | solution.py:317
  17.5 2.6 %collective-permute-done.1.came = bf16[176,512]{1,0:T(8,128)(2,1)S(1)} collective-permute-done((bf16[176,512]{1,0:T(8,128)(2,1)S(1)}, bf16[176,512]{1,0:T(8,128)(2,1)S(1)}, u32[]{:S(2)}, u32[]{:S(2)}) %collective-permute-start.1) | collective-permute-done | bytes 180256 | tf_op jit(solution)/shard_map/ppermute | solution.py:317
  22.5 1.6 %shard_map.62 = (f32[512,512]{1,0:T(8,128)S(1)}, f32[512,512]{1,0:T(8,128)S(1)}, f32[512,512]{1,0:T(8,128)S(1)}) custom-call(f32[4,8,512]{2,1,0:T(8,128)S(1)} %get-tuple-element.58.flags, bf16[1,512,512]{2,1,0:T(8,128)(2,1)S(1)} %get-tuple-element.63.refs_0_, bf16[176,512]{1,0:T(8,128)(2,1)S(1)} %collective-permute-done.5.refs_1_, ...), custom_call_target="tpu_custom_call" | custom-call | flops 738197504 | tf_op jit(solution)/shard_map/pallas_call | solution.py:245
  24.1 2.2 %collective-permute-done.2.refs_1_ = bf16[176,512]{1,0:T(8,128)(2,1)S(1)} collective-permute-done((bf16[176,512]{1,0:T(8,128)(2,1)S(1)}, bf16[176,512]{1,0:T(8,128)(2,1)S(1)}, u32[]{:S(2)}, u32[]{:S(2)}) %collective-permute-start.2) | collective-permute-done | bytes 180256 | tf_op jit(solution)/shard_map/ppermute | solution.py:339
  32.6 3.5 %collective-permute-done.16.came = bf16[160,512]{1,0:T(8,128)(2,1)S(1)} collective-permute-done((bf16[160,512]{1,0:T(8,128)(2,1)S(1)}, bf16[160,512]{1,0:T(8,128)(2,1)S(1)}, u32[]{:S(2)}, u32[]{:S(2)}) %collective-permute-start.16) | collective-permute-done | bytes 163872 | tf_op jit(solution)/shard_map/ppermute | solution.py:317
  36.7 3.2 %collective-permute-done.13.came = bf16[176,512]{1,0:T(8,128)(2,1)S(1)} collective-permute-done((bf16[176,512]{1,0:T(8,128)(2,1)S(1)}, bf16[176,512]{1,0:T(8,128)(2,1)S(1)}, u32[]{:S(2)}, u32[]{:S(2)}) %collective-permute-start.13) | collective-permute-done | bytes 180256 | tf_op jit(solution)/shard_map/ppermute | solution.py:317
  40.5 2.7 %collective-permute-done.10.came = bf16[176,512]{1,0:T(8,128)(2,1)S(1)} collective-permute-done((bf16[176,512]{1,0:T(8,128)(2,1)S(1)}, bf16[176,512]{1,0:T(8,128)(2,1)S(1)}, u32[]{:S(2)}, u32[]{:S(2)}) %collective-permute-start.10) | collective-permute-done | bytes 180256 | tf_op jit(solution)/shard_map/ppermute | solution.py:317
  47.2 2.2 %collective-permute-done.11.refs_0_ = bf16[176,512]{1,0:T(8,128)(2,1)S(1)} collective-permute-done((bf16[176,512]{1,0:T(8,128)(2,1)S(1)}, bf16[176,512]{1,0:T(8,128)(2,1)S(1)}, u32[]{:S(2)}, u32[]{:S(2)}) %collective-permute-start.11) | collective-permute-done | bytes 180256 | tf_op jit(solution)/shard_map/ppermute | solution.py:339
  55.3 2.1 %collective-permute-start.19 = (bf16[176,512]{1,0:T(8,128)(2,1)S(1)}, bf16[176,512]{1,0:T(8,128)(2,1)S(1)}, u32[]{:S(2)}, u32[]{:S(2)}) collective-permute-start(bf16[176,512]{1,0:T(8,128)(2,1)S(1)} %get-tuple-element.114), channel_id=1, source_target_pairs={{0,2},{1,3},{2,4},{3,5},{4,6},{5,7},{6,0},{7,1},{8,10},{9,11},{10,... | collective-permute-start | bytes 540680 | tf_op jit(solution)/shard_map/ppermute | solution.py:317
  57.5 2.0 %collective-permute-done.25.came = bf16[160,512]{1,0:T(8,128)(2,1)S(1)} collective-permute-done((bf16[160,512]{1,0:T(8,128)(2,1)S(1)}, bf16[160,512]{1,0:T(8,128)(2,1)S(1)}, u32[]{:S(2)}, u32[]{:S(2)}) %collective-permute-start.25) | collective-permute-done | bytes 163872 | tf_op jit(solution)/shard_map/ppermute | solution.py:317
  61.1 2.2 %collective-permute-done.22.came = bf16[176,512]{1,0:T(8,128)(2,1)S(1)} collective-permute-done((bf16[176,512]{1,0:T(8,128)(2,1)S(1)}, bf16[176,512]{1,0:T(8,128)(2,1)S(1)}, u32[]{:S(2)}, u32[]{:S(2)}) %collective-permute-start.22) | collective-permute-done | bytes 180256 | tf_op jit(solution)/shard_map/ppermute | solution.py:317
  64.8 2.1 %collective-permute-done.19.came = bf16[176,512]{1,0:T(8,128)(2,1)S(1)} collective-permute-done((bf16[176,512]{1,0:T(8,128)(2,1)S(1)}, bf16[176,512]{1,0:T(8,128)(2,1)S(1)}, u32[]{:S(2)}, u32[]{:S(2)}) %collective-permute-start.19) | collective-permute-done | bytes 180256 | tf_op jit(solution)/shard_map/ppermute | solution.py:317
  69.9 1.7 %shard_map.76 = (f32[512,512]{1,0:T(8,128)S(1)}, f32[512,512]{1,0:T(8,128)S(1)}, f32[512,512]{1,0:T(8,128)S(1)}) custom-call(f32[4,8,512]{2,1,0:T(8,128)S(1)} %get-tuple-element.58.flags, bf16[176,512]{1,0:T(8,128)(2,1)S(1)} %collective-permute-done.23.refs_0_, bf16[1,2,4,1,512,512]{5,4,3,2,1,0:T(8,128)(2,1)S(1)} %copy-done, ...), custom_call_target="tpu_custom_call" | custom-call | flops 738197504 | tf_op jit(solution)/shard_map/pallas_call | solution.py:245
  71.6 1.8 %collective-permute-done.20.refs_0_ = bf16[176,512]{1,0:T(8,128)(2,1)S(1)} collective-permute-done((bf16[176,512]{1,0:T(8,128)(2,1)S(1)}, bf16[176,512]{1,0:T(8,128)(2,1)S(1)}, u32[]{:S(2)}, u32[]{:S(2)}) %collective-permute-start.20) | collective-permute-done | bytes 180256 | tf_op jit(solution)/shard_map/ppermute | solution.py:339
  78.9 5.4 %collective-permute-done.34.came = bf16[160,512]{1,0:T(8,128)(2,1)S(1)} collective-permute-done((bf16[160,512]{1,0:T(8,128)(2,1)S(1)}, bf16[160,512]{1,0:T(8,128)(2,1)S(1)}, u32[]{:S(2)}, u32[]{:S(2)}) %collective-permute-start.34) | collective-permute-done | bytes 163872 | tf_op jit(solution)/shard_map/ppermute | solution.py:317
  84.4 2.4 %collective-permute-start.35 = (bf16[160,512]{1,0:T(8,128)(2,1)S(1)}, bf16[160,512]{1,0:T(8,128)(2,1)S(1)}, u32[]{:S(2)}, u32[]{:S(2)}) collective-permute-start(bf16[160,512]{1,0:T(8,128)(2,1)S(1)} %shard_map.81.refs_0_), channel_id=1, source_target_pairs={{0,8},{1,9},{2,10},{3,11},{4,12},{5,13},{6,14},{7,15},{8,0},{9,1},... | collective-permute-start | bytes 491528 | tf_op jit(solution)/shard_map/ppermute | solution.py:339
  88.3 2.4 %collective-permute-start.32 = (bf16[176,512]{1,0:T(8,128)(2,1)S(1)}, bf16[176,512]{1,0:T(8,128)(2,1)S(1)}, u32[]{:S(2)}, u32[]{:S(2)}) collective-permute-start(bf16[176,512]{1,0:T(8,128)(2,1)S(1)} %shard_map.80.refs_1_), channel_id=1, source_target_pairs={{0,8},{1,9},{2,10},{3,11},{4,12},{5,13},{6,14},{7,15},{8,0},{9,1},... | collective-permute-start | bytes 540680 | tf_op jit(solution)/shard_map/ppermute | solution.py:339
  91.9 2.4 %collective-permute-start.29 = (bf16[176,512]{1,0:T(8,128)(2,1)S(1)}, bf16[176,512]{1,0:T(8,128)(2,1)S(1)}, u32[]{:S(2)}, u32[]{:S(2)}) collective-permute-start(bf16[176,512]{1,0:T(8,128)(2,1)S(1)} %shard_map.79.refs_2_), channel_id=1, source_target_pairs={{0,8},{1,9},{2,10},{3,11},{4,12},{5,13},{6,14},{7,15},{8,0},{9,1},... | collective-permute-start | bytes 540680 | tf_op jit(solution)/shard_map/ppermute | solution.py:339
  101.6 1.9 %collective-permute-start.39 = (bf16[336,512]{1,0:T(8,128)(2,1)S(1)}, bf16[336,512]{1,0:T(8,128)(2,1)S(1)}, u32[]{:S(2)}, u32[]{:S(2)}) collective-permute-start(bf16[336,512]{1,0:T(8,128)(2,1)S(1)} %add_convert_fusion), channel_id=1, source_target_pairs={{24,26},{25,27},{26,28},{27,29},{28,30},{29,31}} | collective-permute-start | bytes 1032200 | tf_op jit(solution)/shard_map/ppermute | solution.py:317
  103.6 2.3 %collective-permute-start.37 = (bf16[176,512]{1,0:T(8,128)(2,1)S(1)}, bf16[176,512]{1,0:T(8,128)(2,1)S(1)}, u32[]{:S(2)}, u32[]{:S(2)}) collective-permute-start(bf16[176,512]{1,0:T(8,128)(2,1)S(1)} %add_convert_fusion.1), channel_id=1, source_target_pairs={{24,26},{25,27},{26,28},{27,29},{28,30},{29,31}} | collective-permute-start | bytes 540680 | tf_op jit(solution)/shard_map/ppermute | solution.py:317
  106.9 7.5 %collective-permute-done.39.came = bf16[336,512]{1,0:T(8,128)(2,1)S(1)} collective-permute-done((bf16[336,512]{1,0:T(8,128)(2,1)S(1)}, bf16[336,512]{1,0:T(8,128)(2,1)S(1)}, u32[]{:S(2)}, u32[]{:S(2)}) %collective-permute-start.39) | collective-permute-done | bytes 344096 | tf_op jit(solution)/shard_map/ppermute | solution.py:317
  115.4 2.1 %collective-permute-done.37.came = bf16[176,512]{1,0:T(8,128)(2,1)S(1)} collective-permute-done((bf16[176,512]{1,0:T(8,128)(2,1)S(1)}, bf16[176,512]{1,0:T(8,128)(2,1)S(1)}, u32[]{:S(2)}, u32[]{:S(2)}) %collective-permute-start.37) | collective-permute-done | bytes 180256 | tf_op jit(solution)/shard_map/ppermute | solution.py:317
  (111 shorter events, 51.3 us)
Async XLA Ops:
  5.8 7.1 %collective-permute-start.7 = (bf16[160,512]{1,0:T(8,128)(2,1)S(1)}, bf16[160,512]{1,0:T(8,128)(2,1)S(1)}, u32[]{:S(2)}, u32[]{:S(2)}) collective-permute-start(bf16[160,512]{1,0:T(8,128)(2,1)S(1)} %add_convert_fusion.13), channel_id=1, source_target_pairs={{0,2},{1,3},{2,4},{3,5},{4,6},{5,7},{18,16},{19,17},{20,18},{21,19... | collective-permute-start | bytes 491528 | tf_op jit(solution)/shard_map/ppermute | solution.py:317
  6.4 10.4 %collective-permute-start.4 = (bf16[176,512]{1,0:T(8,128)(2,1)S(1)}, bf16[176,512]{1,0:T(8,128)(2,1)S(1)}, u32[]{:S(2)}, u32[]{:S(2)}) collective-permute-start(bf16[176,512]{1,0:T(8,128)(2,1)S(1)} %get-tuple-element.117), channel_id=1, source_target_pairs={{0,2},{1,3},{2,4},{3,5},{4,6},{5,7},{18,16},{19,17},{20,18},{21,19... | collective-permute-start | bytes 540680 | tf_op jit(solution)/shard_map/ppermute | solution.py:317
  7.0 13.1 %collective-permute-start.1 = (bf16[176,512]{1,0:T(8,128)(2,1)S(1)}, bf16[176,512]{1,0:T(8,128)(2,1)S(1)}, u32[]{:S(2)}, u32[]{:S(2)}) collective-permute-start(bf16[176,512]{1,0:T(8,128)(2,1)S(1)} %get-tuple-element.118), channel_id=1, source_target_pairs={{0,2},{1,3},{2,4},{3,5},{4,6},{5,7},{18,16},{19,17},{20,18},{21,19... | collective-permute-start | bytes 540680 | tf_op jit(solution)/shard_map/ppermute | solution.py:317
  13.1 7.8 %collective-permute-start.8 = (bf16[160,512]{1,0:T(8,128)(2,1)S(1)}, bf16[160,512]{1,0:T(8,128)(2,1)S(1)}, u32[]{:S(2)}, u32[]{:S(2)}) collective-permute-start(bf16[160,512]{1,0:T(8,128)(2,1)S(1)} %shard_map.60.refs_0_), channel_id=1, source_target_pairs={{0,8},{1,9},{2,10},{3,11},{4,12},{5,13},{6,14},{7,15},{8,0},{9,1},... | collective-permute-start | bytes 491528 | tf_op jit(solution)/shard_map/ppermute | solution.py:339
  20.3 6.1 %collective-permute-start.2 = (bf16[176,512]{1,0:T(8,128)(2,1)S(1)}, bf16[176,512]{1,0:T(8,128)(2,1)S(1)}, u32[]{:S(2)}, u32[]{:S(2)}) collective-permute-start(bf16[176,512]{1,0:T(8,128)(2,1)S(1)} %shard_map.58.refs_2_), channel_id=1, source_target_pairs={{0,8},{1,9},{2,10},{3,11},{4,12},{5,13},{6,14},{7,15},{8,0},{9,1},... | collective-permute-start | bytes 540680 | tf_op jit(solution)/shard_map/ppermute | solution.py:339
  28.9 7.1 %collective-permute-start.16 = (bf16[160,512]{1,0:T(8,128)(2,1)S(1)}, bf16[160,512]{1,0:T(8,128)(2,1)S(1)}, u32[]{:S(2)}, u32[]{:S(2)}) collective-permute-start(bf16[160,512]{1,0:T(8,128)(2,1)S(1)} %add_convert_fusion.12), channel_id=1, source_target_pairs={{0,2},{1,3},{2,4},{3,5},{4,6},{5,7},{6,0},{7,1},{8,10},{9,11},{10,... | collective-permute-start | bytes 491528 | tf_op jit(solution)/shard_map/ppermute | solution.py:317
  30.6 9.2 %collective-permute-start.13 = (bf16[176,512]{1,0:T(8,128)(2,1)S(1)}, bf16[176,512]{1,0:T(8,128)(2,1)S(1)}, u32[]{:S(2)}, u32[]{:S(2)}) collective-permute-start(bf16[176,512]{1,0:T(8,128)(2,1)S(1)} %get-tuple-element.115), channel_id=1, source_target_pairs={{0,2},{1,3},{2,4},{3,5},{4,6},{5,7},{6,0},{7,1},{8,10},{9,11},{10,... | collective-permute-start | bytes 540680 | tf_op jit(solution)/shard_map/ppermute | solution.py:317
  32.3 10.9 %collective-permute-start.10 = (bf16[176,512]{1,0:T(8,128)(2,1)S(1)}, bf16[176,512]{1,0:T(8,128)(2,1)S(1)}, u32[]{:S(2)}, u32[]{:S(2)}) collective-permute-start(bf16[176,512]{1,0:T(8,128)(2,1)S(1)} %get-tuple-element.116), channel_id=1, source_target_pairs={{0,2},{1,3},{2,4},{3,5},{4,6},{5,7},{6,0},{7,1},{8,10},{9,11},{10,... | collective-permute-start | bytes 540680 | tf_op jit(solution)/shard_map/ppermute | solution.py:317
  36.1 7.7 %collective-permute-start.17 = (bf16[160,512]{1,0:T(8,128)(2,1)S(1)}, bf16[160,512]{1,0:T(8,128)(2,1)S(1)}, u32[]{:S(2)}, u32[]{:S(2)}) collective-permute-start(bf16[160,512]{1,0:T(8,128)(2,1)S(1)} %shard_map.67.refs_0_), channel_id=1, source_target_pairs={{0,8},{1,9},{2,10},{3,11},{4,12},{5,13},{6,14},{7,15},{8,16},{9,17... | collective-permute-start | bytes 491528 | tf_op jit(solution)/shard_map/ppermute | solution.py:339
  43.3 6.1 %collective-permute-start.11 = (bf16[176,512]{1,0:T(8,128)(2,1)S(1)}, bf16[176,512]{1,0:T(8,128)(2,1)S(1)}, u32[]{:S(2)}, u32[]{:S(2)}) collective-permute-start(bf16[176,512]{1,0:T(8,128)(2,1)S(1)} %shard_map.65.refs_2_), channel_id=1, source_target_pairs={{0,8},{1,9},{2,10},{3,11},{4,12},{5,13},{6,14},{7,15},{8,16},{9,17... | collective-permute-start | bytes 540680 | tf_op jit(solution)/shard_map/ppermute | solution.py:339
  52.0 7.5 %collective-permute-start.25 = (bf16[160,512]{1,0:T(8,128)(2,1)S(1)}, bf16[160,512]{1,0:T(8,128)(2,1)S(1)}, u32[]{:S(2)}, u32[]{:S(2)}) collective-permute-start(bf16[160,512]{1,0:T(8,128)(2,1)S(1)} %add_convert_fusion.11), channel_id=1, source_target_pairs={{0,2},{1,3},{2,4},{3,5},{4,6},{5,7},{6,0},{7,1},{8,10},{9,11},{10,... | collective-permute-start | bytes 491528 | tf_op jit(solution)/shard_map/ppermute | solution.py:317
  53.7 9.6 %collective-permute-start.22 = (bf16[176,512]{1,0:T(8,128)(2,1)S(1)}, bf16[176,512]{1,0:T(8,128)(2,1)S(1)}, u32[]{:S(2)}, u32[]{:S(2)}) collective-permute-start(bf16[176,512]{1,0:T(8,128)(2,1)S(1)} %get-tuple-element.113), channel_id=1, source_target_pairs={{0,2},{1,3},{2,4},{3,5},{4,6},{5,7},{6,0},{7,1},{8,10},{9,11},{10,... | collective-permute-start | bytes 540680 | tf_op jit(solution)/shard_map/ppermute | solution.py:317
  55.3 11.6 %collective-permute-start.19 = (bf16[176,512]{1,0:T(8,128)(2,1)S(1)}, bf16[176,512]{1,0:T(8,128)(2,1)S(1)}, u32[]{:S(2)}, u32[]{:S(2)}) collective-permute-start(bf16[176,512]{1,0:T(8,128)(2,1)S(1)} %get-tuple-element.114), channel_id=1, source_target_pairs={{0,2},{1,3},{2,4},{3,5},{4,6},{5,7},{6,0},{7,1},{8,10},{9,11},{10,... | collective-permute-start | bytes 540680 | tf_op jit(solution)/shard_map/ppermute | solution.py:317
  59.5 8.9 %collective-permute-start.26 = (bf16[160,512]{1,0:T(8,128)(2,1)S(1)}, bf16[160,512]{1,0:T(8,128)(2,1)S(1)}, u32[]{:S(2)}, u32[]{:S(2)}) collective-permute-start(bf16[160,512]{1,0:T(8,128)(2,1)S(1)} %shard_map.74.refs_0_), channel_id=1, source_target_pairs={{0,8},{1,9},{2,10},{3,11},{4,12},{5,13},{6,14},{7,15},{8,16},{9,17... | collective-permute-start | bytes 491528 | tf_op jit(solution)/shard_map/ppermute | solution.py:339
  63.4 6.5 %collective-permute-start.23 = (bf16[176,512]{1,0:T(8,128)(2,1)S(1)}, bf16[176,512]{1,0:T(8,128)(2,1)S(1)}, u32[]{:S(2)}, u32[]{:S(2)}) collective-permute-start(bf16[176,512]{1,0:T(8,128)(2,1)S(1)} %shard_map.73.refs_1_), channel_id=1, source_target_pairs={{0,8},{1,9},{2,10},{3,11},{4,12},{5,13},{6,14},{7,15},{8,16},{9,17... | collective-permute-start | bytes 540680 | tf_op jit(solution)/shard_map/ppermute | solution.py:339
  67.0 6.4 %collective-permute-start.20 = (bf16[176,512]{1,0:T(8,128)(2,1)S(1)}, bf16[176,512]{1,0:T(8,128)(2,1)S(1)}, u32[]{:S(2)}, u32[]{:S(2)}) collective-permute-start(bf16[176,512]{1,0:T(8,128)(2,1)S(1)} %shard_map.72.refs_2_), channel_id=1, source_target_pairs={{0,8},{1,9},{2,10},{3,11},{4,12},{5,13},{6,14},{7,15},{8,16},{9,17... | collective-permute-start | bytes 540680 | tf_op jit(solution)/shard_map/ppermute | solution.py:339
  75.9 8.4 %collective-permute-start.34 = (bf16[160,512]{1,0:T(8,128)(2,1)S(1)}, bf16[160,512]{1,0:T(8,128)(2,1)S(1)}, u32[]{:S(2)}, u32[]{:S(2)}) collective-permute-start(bf16[160,512]{1,0:T(8,128)(2,1)S(1)} %add_convert_fusion.10), channel_id=1, source_target_pairs={{16,18},{17,19},{18,20},{19,21},{20,22},{21,23},{2,0},{3,1},{4,2},... | collective-permute-start | bytes 491528 | tf_op jit(solution)/shard_map/ppermute | solution.py:317
  76.8 11.4 %collective-permute-start.31 = (bf16[176,512]{1,0:T(8,128)(2,1)S(1)}, bf16[176,512]{1,0:T(8,128)(2,1)S(1)}, u32[]{:S(2)}, u32[]{:S(2)}) collective-permute-start(bf16[176,512]{1,0:T(8,128)(2,1)S(1)} %get-tuple-element.111), channel_id=1, source_target_pairs={{16,18},{17,19},{18,20},{19,21},{20,22},{21,23},{2,0},{3,1},{4,2},... | collective-permute-start | bytes 540680 | tf_op jit(solution)/shard_map/ppermute | solution.py:317
  78.4 13.4 %collective-permute-start.28 = (bf16[176,512]{1,0:T(8,128)(2,1)S(1)}, bf16[176,512]{1,0:T(8,128)(2,1)S(1)}, u32[]{:S(2)}, u32[]{:S(2)}) collective-permute-start(bf16[176,512]{1,0:T(8,128)(2,1)S(1)} %get-tuple-element.112), channel_id=1, source_target_pairs={{16,18},{17,19},{18,20},{19,21},{20,22},{21,23},{2,0},{3,1},{4,2},... | collective-permute-start | bytes 540680 | tf_op jit(solution)/shard_map/ppermute | solution.py:317
  84.4 9.9 %collective-permute-start.35 = (bf16[160,512]{1,0:T(8,128)(2,1)S(1)}, bf16[160,512]{1,0:T(8,128)(2,1)S(1)}, u32[]{:S(2)}, u32[]{:S(2)}) collective-permute-start(bf16[160,512]{1,0:T(8,128)(2,1)S(1)} %shard_map.81.refs_0_), channel_id=1, source_target_pairs={{0,8},{1,9},{2,10},{3,11},{4,12},{5,13},{6,14},{7,15},{8,0},{9,1},... | collective-permute-start | bytes 491528 | tf_op jit(solution)/shard_map/ppermute | solution.py:339
  88.3 7.5 %collective-permute-start.32 = (bf16[176,512]{1,0:T(8,128)(2,1)S(1)}, bf16[176,512]{1,0:T(8,128)(2,1)S(1)}, u32[]{:S(2)}, u32[]{:S(2)}) collective-permute-start(bf16[176,512]{1,0:T(8,128)(2,1)S(1)} %shard_map.80.refs_1_), channel_id=1, source_target_pairs={{0,8},{1,9},{2,10},{3,11},{4,12},{5,13},{6,14},{7,15},{8,0},{9,1},... | collective-permute-start | bytes 540680 | tf_op jit(solution)/shard_map/ppermute | solution.py:339
  91.9 7.0 %collective-permute-start.29 = (bf16[176,512]{1,0:T(8,128)(2,1)S(1)}, bf16[176,512]{1,0:T(8,128)(2,1)S(1)}, u32[]{:S(2)}, u32[]{:S(2)}) collective-permute-start(bf16[176,512]{1,0:T(8,128)(2,1)S(1)} %shard_map.79.refs_2_), channel_id=1, source_target_pairs={{0,8},{1,9},{2,10},{3,11},{4,12},{5,13},{6,14},{7,15},{8,0},{9,1},... | collective-permute-start | bytes 540680 | tf_op jit(solution)/shard_map/ppermute | solution.py:339
  101.6 12.8 %collective-permute-start.39 = (bf16[336,512]{1,0:T(8,128)(2,1)S(1)}, bf16[336,512]{1,0:T(8,128)(2,1)S(1)}, u32[]{:S(2)}, u32[]{:S(2)}) collective-permute-start(bf16[336,512]{1,0:T(8,128)(2,1)S(1)} %add_convert_fusion), channel_id=1, source_target_pairs={{24,26},{25,27},{26,28},{27,29},{28,30},{29,31}} | collective-permute-start | bytes 1032200 | tf_op jit(solution)/shard_map/ppermute | solution.py:317
  103.6 13.9 %collective-permute-start.37 = (bf16[176,512]{1,0:T(8,128)(2,1)S(1)}, bf16[176,512]{1,0:T(8,128)(2,1)S(1)}, u32[]{:S(2)}, u32[]{:S(2)}) collective-permute-start(bf16[176,512]{1,0:T(8,128)(2,1)S(1)} %add_convert_fusion.1), channel_id=1, source_target_pairs={{24,26},{25,27},{26,28},{27,29},{28,30},{29,31}} | collective-permute-start | bytes 540680 | tf_op jit(solution)/shard_map/ppermute | solution.py:317
  (20 other events, 72.4 us)

commit v5 on v4

--- a/solution.py
+++ b/solution.py
@@ -7,7 +7,7 @@
 from jax.experimental.pallas import tpu as pltpu
 from jax.sharding import PartitionSpec as P
 
-PARTS = (10, 11, 11)
+PARTS = (8, 8, 8, 8)
 CHUNKS = len(PARTS)
 LAST_PARTS = (21, 11)
 AXES = ("site", "sector")
@@ -54,10 +54,10 @@
 
 def group(states, e, row, ket, bra, flags, pair, total):
     rows = slice(row, row + e.shape[0])
-    for s in states:
-        part = product(e, ket[0, pair, s, 0], bra[0, s, 0, rows], flags[s, :1])
-        total = part if total is None else total + part
-    return total
+    moved = [(across(e, ket[0, pair, s, 0]) * flags[s, :1]).astype(jnp.bfloat16) for s in states]
+    blocks = [bra[0, s, 0, rows] for s in states]
+    part = down(jnp.concatenate(blocks, axis=0), jnp.concatenate(moved, axis=0))
+    return part if total is None else total + part
 
 
 def parted(total, cuts, outs):

time: 119 us -> 117 us (0.983)
  waiting for transfers between devices: 50.5 us -> 35 us
  starting transfers between devices: 36.9 us -> 49.4 us
  Pallas kernels: 29.7 us -> 31.2 us
    ppermute x14 -> x18, waiting for transfers between devices: 42.1 us -> 31.6 us  [per_device(): came = lax.ppermute(up, AXES, up_pairs(step))]
    ppermute x12 -> x16, starting transfers between devices: 15 us -> 20.9 us  [per_device(): held = [lax.ppermute(rows, AXES, next_pairs(step)) for rows in fresh]]
    ppermute x12 -> x16, waiting for transfers between devices: 8.05 us -> 2.6 us  [per_device(): held = [lax.ppermute(rows, AXES, next_pairs(step)) for rows in fresh]]
    ppermute x14 -> x18, starting transfers between devices: 18.7 us -> 23.6 us  [per_device(): came = lax.ppermute(up, AXES, up_pairs(step))]
    ppermute x14 -> x18, starting transfers between devices: 3.15 us -> 4.88 us  [swapped(): return [lax.ppermute(part, AXES, swap_pairs) for part in parts]]
    pallas_call x16 -> x20, Pallas kernels: 19.7 us -> 21 us  [chunk(): call(functools.partial(step_kernel, step, cuts[k], fresh, len(before) > 0...]
  transfers between devices with their start and end apart: 40 -> 52, of which waited for: 21 -> 25; matrix products, arithmetic and copies ran while one was open for 1% -> 0% of each run, Pallas kernels for 18% -> 21%
where the time goes in v5:
time: 117 us
  starting transfers between devices  49.4 us (42%)
  waiting for transfers between devices  35 us (30%)
  Pallas kernels  31.2 us (27%)
    ppermute x18, waiting for transfers between devices, per_device(): came = lax.ppermute(up, AXES, up_pairs(step))  31.6 us
    ppermute x18, starting transfers between devices, per_device(): came = lax.ppermute(up, AXES, up_pairs(step))  23.6 us
    pallas_call x20, Pallas kernels, chunk(): call(functools.partial(step_kernel, step, cuts[k], fresh, len(before) > 0...  21 us
    ppermute x16, starting transfers between devices, per_device(): held = [lax.ppermute(rows, AXES, next_pairs(step)) for rows in fresh]  20.9 us
    ppermute x18, starting transfers between devices, swapped(): return [lax.ppermute(part, AXES, swap_pairs) for part in parts]  4.88 us
    pallas_call x1, Pallas kernels, per_device(): call(functools.partial(open_kernel, first, later, cuts), [pl.BlockSpec(me...  3.7 us
    ppermute x16, waiting for transfers between devices, per_device(): held = [lax.ppermute(rows, AXES, next_pairs(step)) for rows in fresh]  2.6 us
  transfers between devices with their start and end apart: 52, of which 25 were waited for; matrix products, arithmetic and copies ran while one was open for 0% of the time, Pallas kernels for 21%

profile of v5, /device:TPU:14, one launch (start us, length us, event | category | flops | bytes accessed | tf_op | source)
XLA Modules:
  0.0 117.0 jit_solution(2710553325829065607)
XLA Ops:
  0.0 3.7 %shard_map.55 = (bf16[128,512]{1,0:T(8,128)(2,1)S(1)}, bf16[128,512]{1,0:T(8,128)(2,1)S(1)}, bf16[128,512]{1,0:T(8,128)(2,1)}, bf16[128,512]{1,0:T(8,128)(2,1)},...) custom-call(s32[5,8]{1,0:T(8,128)} %dims.1, s32[4]{0:T(128)} %bitcast.1, ...), custom_call_target="tpu_custom_call" | custom-call | flops 1073741824 | tf_op jit(solution)/shard_map/pallas_call | solution.py:262
  7.4 1.6 %collective-permute-start.4 = (bf16[128,512]{1,0:T(8,128)(2,1)S(1)}, bf16[128,512]{1,0:T(8,128)(2,1)S(1)}, u32[]{:S(2)}, u32[]{:S(2)}) collective-permute-start(bf16[128,512]{1,0:T(8,128)(2,1)S(1)} %get-tuple-element.157), channel_id=1, source_target_pairs={{0,2},{1,3},{2,4},{3,5},{4,6},{5,7},{18,16},{19,17},{20,18},{21,19... | collective-permute-start | bytes 393224 | tf_op jit(solution)/shard_map/ppermute | solution.py:317
  9.8 1.6 %collective-permute-start.1 = (bf16[128,512]{1,0:T(8,128)(2,1)S(1)}, bf16[128,512]{1,0:T(8,128)(2,1)S(1)}, u32[]{:S(2)}, u32[]{:S(2)}) collective-permute-start(bf16[128,512]{1,0:T(8,128)(2,1)S(1)} %get-tuple-element.158), channel_id=1, source_target_pairs={{0,2},{1,3},{2,4},{3,5},{4,6},{5,7},{18,16},{19,17},{20,18},{21,19... | collective-permute-start | bytes 393224 | tf_op jit(solution)/shard_map/ppermute | solution.py:317
  13.6 2.1 %collective-permute-done.7.came = bf16[128,512]{1,0:T(8,128)(2,1)S(1)} collective-permute-done((bf16[128,512]{1,0:T(8,128)(2,1)S(1)}, bf16[128,512]{1,0:T(8,128)(2,1)S(1)}, u32[]{:S(2)}, u32[]{:S(2)}) %collective-permute-start.7) | collective-permute-done | bytes 131104 | tf_op jit(solution)/shard_map/ppermute | solution.py:317
  16.4 2.1 %collective-permute-done.4.came = bf16[128,512]{1,0:T(8,128)(2,1)S(1)} collective-permute-done((bf16[128,512]{1,0:T(8,128)(2,1)S(1)}, bf16[128,512]{1,0:T(8,128)(2,1)S(1)}, u32[]{:S(2)}, u32[]{:S(2)}) %collective-permute-start.4) | collective-permute-done | bytes 131104 | tf_op jit(solution)/shard_map/ppermute | solution.py:317
  29.3 1.6 %collective-permute-start.22 = (bf16[128,512]{1,0:T(8,128)(2,1)S(1)}, bf16[128,512]{1,0:T(8,128)(2,1)S(1)}, u32[]{:S(2)}, u32[]{:S(2)}) collective-permute-start(bf16[128,512]{1,0:T(8,128)(2,1)S(1)} %get-tuple-element.151), channel_id=1, source_target_pairs={{0,2},{1,3},{2,4},{3,5},{4,6},{5,7},{6,0},{7,1},{8,10},{9,11},{10,... | collective-permute-start | bytes 393224 | tf_op jit(solution)/shard_map/ppermute | solution.py:317
  30.9 1.6 %collective-permute-start.19 = (bf16[128,512]{1,0:T(8,128)(2,1)S(1)}, bf16[128,512]{1,0:T(8,128)(2,1)S(1)}, u32[]{:S(2)}, u32[]{:S(2)}) collective-permute-start(bf16[128,512]{1,0:T(8,128)(2,1)S(1)} %get-tuple-element.152), channel_id=1, source_target_pairs={{0,2},{1,3},{2,4},{3,5},{4,6},{5,7},{6,0},{7,1},{8,10},{9,11},{10,... | collective-permute-start | bytes 393224 | tf_op jit(solution)/shard_map/ppermute | solution.py:317
  36.3 2.2 %collective-permute-done.19.came = bf16[128,512]{1,0:T(8,128)(2,1)S(1)} collective-permute-done((bf16[128,512]{1,0:T(8,128)(2,1)S(1)}, bf16[128,512]{1,0:T(8,128)(2,1)S(1)}, u32[]{:S(2)}, u32[]{:S(2)}) %collective-permute-start.19) | collective-permute-done | bytes 131104 | tf_op jit(solution)/shard_map/ppermute | solution.py:317
  39.1 2.2 %collective-permute-done.16.came = bf16[128,512]{1,0:T(8,128)(2,1)S(1)} collective-permute-done((bf16[128,512]{1,0:T(8,128)(2,1)S(1)}, bf16[128,512]{1,0:T(8,128)(2,1)S(1)}, u32[]{:S(2)}, u32[]{:S(2)}) %collective-permute-start.16) | collective-permute-done | bytes 131104 | tf_op jit(solution)/shard_map/ppermute | solution.py:317
  52.1 1.6 %collective-permute-start.34 = (bf16[128,512]{1,0:T(8,128)(2,1)S(1)}, bf16[128,512]{1,0:T(8,128)(2,1)S(1)}, u32[]{:S(2)}, u32[]{:S(2)}) collective-permute-start(bf16[128,512]{1,0:T(8,128)(2,1)S(1)} %get-tuple-element.147), channel_id=1, source_target_pairs={{0,2},{1,3},{2,4},{3,5},{4,6},{5,7},{6,0},{7,1},{8,10},{9,11},{10,... | collective-permute-start | bytes 393224 | tf_op jit(solution)/shard_map/ppermute | solution.py:317
  55.3 2.0 %collective-permute-start.28 = (bf16[128,512]{1,0:T(8,128)(2,1)S(1)}, bf16[128,512]{1,0:T(8,128)(2,1)S(1)}, u32[]{:S(2)}, u32[]{:S(2)}) collective-permute-start(bf16[128,512]{1,0:T(8,128)(2,1)S(1)} %get-tuple-element.149), channel_id=1, source_target_pairs={{0,2},{1,3},{2,4},{3,5},{4,6},{5,7},{6,0},{7,1},{8,10},{9,11},{10,... | collective-permute-start | bytes 393224 | tf_op jit(solution)/shard_map/ppermute | solution.py:317
  58.8 1.7 %collective-permute-start.35 = (bf16[128,512]{1,0:T(8,128)(2,1)S(1)}, bf16[128,512]{1,0:T(8,128)(2,1)S(1)}, u32[]{:S(2)}, u32[]{:S(2)}) collective-permute-start(bf16[128,512]{1,0:T(8,128)(2,1)S(1)} %shard_map.79.refs_0_), channel_id=1, source_target_pairs={{0,8},{1,9},{2,10},{3,11},{4,12},{5,13},{6,14},{7,15},{8,16},{9,17... | collective-permute-start | bytes 393224 | tf_op jit(solution)/shard_map/ppermute | solution.py:339
  61.6 1.7 %collective-permute-start.32 = (bf16[128,512]{1,0:T(8,128)(2,1)S(1)}, bf16[128,512]{1,0:T(8,128)(2,1)S(1)}, u32[]{:S(2)}, u32[]{:S(2)}) collective-permute-start(bf16[128,512]{1,0:T(8,128)(2,1)S(1)} %shard_map.78.refs_1_), channel_id=1, source_target_pairs={{0,8},{1,9},{2,10},{3,11},{4,12},{5,13},{6,14},{7,15},{8,16},{9,17... | collective-permute-start | bytes 393224 | tf_op jit(solution)/shard_map/ppermute | solution.py:339
  64.4 1.7 %collective-permute-start.29 = (bf16[128,512]{1,0:T(8,128)(2,1)S(1)}, bf16[128,512]{1,0:T(8,128)(2,1)S(1)}, u32[]{:S(2)}, u32[]{:S(2)}) collective-permute-start(bf16[128,512]{1,0:T(8,128)(2,1)S(1)} %shard_map.77.refs_2_), channel_id=1, source_target_pairs={{0,8},{1,9},{2,10},{3,11},{4,12},{5,13},{6,14},{7,15},{8,16},{9,17... | collective-permute-start | bytes 393224 | tf_op jit(solution)/shard_map/ppermute | solution.py:339
  66.9 1.7 %collective-permute-start.26 = (bf16[128,512]{1,0:T(8,128)(2,1)S(1)}, bf16[128,512]{1,0:T(8,128)(2,1)S(1)}, u32[]{:S(2)}, u32[]{:S(2)}) collective-permute-start(bf16[128,512]{1,0:T(8,128)(2,1)S(1)} %shard_map.76.refs_3_), channel_id=1, source_target_pairs={{0,8},{1,9},{2,10},{3,11},{4,12},{5,13},{6,14},{7,15},{8,16},{9,17... | collective-permute-start | bytes 393224 | tf_op jit(solution)/shard_map/ppermute | solution.py:339
  79.7 3.6 %collective-permute-done.46.came = bf16[128,512]{1,0:T(8,128)(2,1)S(1)} collective-permute-done((bf16[128,512]{1,0:T(8,128)(2,1)S(1)}, bf16[128,512]{1,0:T(8,128)(2,1)S(1)}, u32[]{:S(2)}, u32[]{:S(2)}) %collective-permute-start.46) | collective-permute-done | bytes 131104 | tf_op jit(solution)/shard_map/ppermute | solution.py:317
  83.4 2.4 %collective-permute-start.47 = (bf16[128,512]{1,0:T(8,128)(2,1)S(1)}, bf16[128,512]{1,0:T(8,128)(2,1)S(1)}, u32[]{:S(2)}, u32[]{:S(2)}) collective-permute-start(bf16[128,512]{1,0:T(8,128)(2,1)S(1)} %shard_map.88.refs_0_), channel_id=1, source_target_pairs={{0,8},{1,9},{2,10},{3,11},{4,12},{5,13},{6,14},{7,15},{8,0},{9,1},... | collective-permute-start | bytes 393224 | tf_op jit(solution)/shard_map/ppermute | solution.py:339
  86.3 2.4 %collective-permute-start.44 = (bf16[128,512]{1,0:T(8,128)(2,1)S(1)}, bf16[128,512]{1,0:T(8,128)(2,1)S(1)}, u32[]{:S(2)}, u32[]{:S(2)}) collective-permute-start(bf16[128,512]{1,0:T(8,128)(2,1)S(1)} %shard_map.87.refs_1_), channel_id=1, source_target_pairs={{0,8},{1,9},{2,10},{3,11},{4,12},{5,13},{6,14},{7,15},{8,0},{9,1},... | collective-permute-start | bytes 393224 | tf_op jit(solution)/shard_map/ppermute | solution.py:339
  89.1 2.4 %collective-permute-start.41 = (bf16[128,512]{1,0:T(8,128)(2,1)S(1)}, bf16[128,512]{1,0:T(8,128)(2,1)S(1)}, u32[]{:S(2)}, u32[]{:S(2)}) collective-permute-start(bf16[128,512]{1,0:T(8,128)(2,1)S(1)} %shard_map.86.refs_2_), channel_id=1, source_target_pairs={{0,8},{1,9},{2,10},{3,11},{4,12},{5,13},{6,14},{7,15},{8,0},{9,1},... | collective-permute-start | bytes 393224 | tf_op jit(solution)/shard_map/ppermute | solution.py:339
  91.6 2.3 %collective-permute-start.38 = (bf16[128,512]{1,0:T(8,128)(2,1)S(1)}, bf16[128,512]{1,0:T(8,128)(2,1)S(1)}, u32[]{:S(2)}, u32[]{:S(2)}) collective-permute-start(bf16[128,512]{1,0:T(8,128)(2,1)S(1)} %shard_map.85.refs_3_), channel_id=1, source_target_pairs={{0,8},{1,9},{2,10},{3,11},{4,12},{5,13},{6,14},{7,15},{8,0},{9,1},... | collective-permute-start | bytes 393224 | tf_op jit(solution)/shard_map/ppermute | solution.py:339
  100.2 1.9 %collective-permute-start.51 = (bf16[336,512]{1,0:T(8,128)(2,1)S(1)}, bf16[336,512]{1,0:T(8,128)(2,1)S(1)}, u32[]{:S(2)}, u32[]{:S(2)}) collective-permute-start(bf16[336,512]{1,0:T(8,128)(2,1)S(1)} %add_convert_fusion), channel_id=1, source_target_pairs={{24,26},{25,27},{26,28},{27,29},{28,30},{29,31}} | collective-permute-start | bytes 1032200 | tf_op jit(solution)/shard_map/ppermute | solution.py:317
  102.2 2.7 %collective-permute-start.49 = (bf16[176,512]{1,0:T(8,128)(2,1)S(1)}, bf16[176,512]{1,0:T(8,128)(2,1)S(1)}, u32[]{:S(2)}, u32[]{:S(2)}) collective-permute-start(bf16[176,512]{1,0:T(8,128)(2,1)S(1)} %add_convert_fusion.1), channel_id=1, source_target_pairs={{24,26},{25,27},{26,28},{27,29},{28,30},{29,31}} | collective-permute-start | bytes 540680 | tf_op jit(solution)/shard_map/ppermute | solution.py:317
  106.0 7.0 %collective-permute-done.51.came = bf16[336,512]{1,0:T(8,128)(2,1)S(1)} collective-permute-done((bf16[336,512]{1,0:T(8,128)(2,1)S(1)}, bf16[336,512]{1,0:T(8,128)(2,1)S(1)}, u32[]{:S(2)}, u32[]{:S(2)}) %collective-permute-start.51) | collective-permute-done | bytes 344096 | tf_op jit(solution)/shard_map/ppermute | solution.py:317
  114.0 2.1 %collective-permute-done.49.came = bf16[176,512]{1,0:T(8,128)(2,1)S(1)} collective-permute-done((bf16[176,512]{1,0:T(8,128)(2,1)S(1)}, bf16[176,512]{1,0:T(8,128)(2,1)S(1)}, u32[]{:S(2)}, u32[]{:S(2)}) %collective-permute-start.49) | collective-permute-done | bytes 180256 | tf_op jit(solution)/shard_map/ppermute | solution.py:317
  (139 shorter events, 60.5 us)
Async XLA Ops:
  6.9 8.7 %collective-permute-start.7 = (bf16[128,512]{1,0:T(8,128)(2,1)S(1)}, bf16[128,512]{1,0:T(8,128)(2,1)S(1)}, u32[]{:S(2)}, u32[]{:S(2)}) collective-permute-start(bf16[128,512]{1,0:T(8,128)(2,1)S(1)} %get-tuple-element.156), channel_id=1, source_target_pairs={{0,2},{1,3},{2,4},{3,5},{4,6},{5,7},{18,16},{19,17},{20,18},{21,19... | collective-permute-start | bytes 393224 | tf_op jit(solution)/shard_map/ppermute | solution.py:317
  7.4 11.0 %collective-permute-start.4 = (bf16[128,512]{1,0:T(8,128)(2,1)S(1)}, bf16[128,512]{1,0:T(8,128)(2,1)S(1)}, u32[]{:S(2)}, u32[]{:S(2)}) collective-permute-start(bf16[128,512]{1,0:T(8,128)(2,1)S(1)} %get-tuple-element.157), channel_id=1, source_target_pairs={{0,2},{1,3},{2,4},{3,5},{4,6},{5,7},{18,16},{19,17},{20,18},{21,19... | collective-permute-start | bytes 393224 | tf_op jit(solution)/shard_map/ppermute | solution.py:317
  9.8 10.5 %collective-permute-start.1 = (bf16[128,512]{1,0:T(8,128)(2,1)S(1)}, bf16[128,512]{1,0:T(8,128)(2,1)S(1)}, u32[]{:S(2)}, u32[]{:S(2)}) collective-permute-start(bf16[128,512]{1,0:T(8,128)(2,1)S(1)} %get-tuple-element.158), channel_id=1, source_target_pairs={{0,2},{1,3},{2,4},{3,5},{4,6},{5,7},{18,16},{19,17},{20,18},{21,19... | collective-permute-start | bytes 393224 | tf_op jit(solution)/shard_map/ppermute | solution.py:317
  13.0 8.1 %collective-permute-start.11 = (bf16[128,512]{1,0:T(8,128)(2,1)S(1)}, bf16[128,512]{1,0:T(8,128)(2,1)S(1)}, u32[]{:S(2)}, u32[]{:S(2)}) collective-permute-start(bf16[128,512]{1,0:T(8,128)(2,1)S(1)} %shard_map.61.refs_0_), channel_id=1, source_target_pairs={{0,8},{1,9},{2,10},{3,11},{4,12},{5,13},{6,14},{7,15},{8,0},{9,1},... | collective-permute-start | bytes 393224 | tf_op jit(solution)/shard_map/ppermute | solution.py:339
  30.9 7.6 %collective-permute-start.19 = (bf16[128,512]{1,0:T(8,128)(2,1)S(1)}, bf16[128,512]{1,0:T(8,128)(2,1)S(1)}, u32[]{:S(2)}, u32[]{:S(2)}) collective-permute-start(bf16[128,512]{1,0:T(8,128)(2,1)S(1)} %get-tuple-element.152), channel_id=1, source_target_pairs={{0,2},{1,3},{2,4},{3,5},{4,6},{5,7},{6,0},{7,1},{8,10},{9,11},{10,... | collective-permute-start | bytes 393224 | tf_op jit(solution)/shard_map/ppermute | solution.py:317
  32.5 8.8 %collective-permute-start.16 = (bf16[128,512]{1,0:T(8,128)(2,1)S(1)}, bf16[128,512]{1,0:T(8,128)(2,1)S(1)}, u32[]{:S(2)}, u32[]{:S(2)}) collective-permute-start(bf16[128,512]{1,0:T(8,128)(2,1)S(1)} %get-tuple-element.153), channel_id=1, source_target_pairs={{0,2},{1,3},{2,4},{3,5},{4,6},{5,7},{6,0},{7,1},{8,10},{9,11},{10,... | collective-permute-start | bytes 393224 | tf_op jit(solution)/shard_map/ppermute | solution.py:317
  32.7 10.8 %collective-permute-start.13 = (bf16[128,512]{1,0:T(8,128)(2,1)S(1)}, bf16[128,512]{1,0:T(8,128)(2,1)S(1)}, u32[]{:S(2)}, u32[]{:S(2)}) collective-permute-start(bf16[128,512]{1,0:T(8,128)(2,1)S(1)} %get-tuple-element.154), channel_id=1, source_target_pairs={{0,2},{1,3},{2,4},{3,5},{4,6},{5,7},{6,0},{7,1},{8,10},{9,11},{10,... | collective-permute-start | bytes 393224 | tf_op jit(solution)/shard_map/ppermute | solution.py:317
  35.8 8.5 %collective-permute-start.23 = (bf16[128,512]{1,0:T(8,128)(2,1)S(1)}, bf16[128,512]{1,0:T(8,128)(2,1)S(1)}, u32[]{:S(2)}, u32[]{:S(2)}) collective-permute-start(bf16[128,512]{1,0:T(8,128)(2,1)S(1)} %shard_map.70.refs_0_), channel_id=1, source_target_pairs={{0,8},{1,9},{2,10},{3,11},{4,12},{5,13},{6,14},{7,15},{8,16},{9,17... | collective-permute-start | bytes 393224 | tf_op jit(solution)/shard_map/ppermute | solution.py:339
  38.6 7.0 %collective-permute-start.20 = (bf16[128,512]{1,0:T(8,128)(2,1)S(1)}, bf16[128,512]{1,0:T(8,128)(2,1)S(1)}, u32[]{:S(2)}, u32[]{:S(2)}) collective-permute-start(bf16[128,512]{1,0:T(8,128)(2,1)S(1)} %shard_map.69.refs_1_), channel_id=1, source_target_pairs={{0,8},{1,9},{2,10},{3,11},{4,12},{5,13},{6,14},{7,15},{8,16},{9,17... | collective-permute-start | bytes 393224 | tf_op jit(solution)/shard_map/ppermute | solution.py:339
  53.7 7.8 %collective-permute-start.31 = (bf16[128,512]{1,0:T(8,128)(2,1)S(1)}, bf16[128,512]{1,0:T(8,128)(2,1)S(1)}, u32[]{:S(2)}, u32[]{:S(2)}) collective-permute-start(bf16[128,512]{1,0:T(8,128)(2,1)S(1)} %get-tuple-element.148), channel_id=1, source_target_pairs={{0,2},{1,3},{2,4},{3,5},{4,6},{5,7},{6,0},{7,1},{8,10},{9,11},{10,... | collective-permute-start | bytes 393224 | tf_op jit(solution)/shard_map/ppermute | solution.py:317
  55.3 9.1 %collective-permute-start.28 = (bf16[128,512]{1,0:T(8,128)(2,1)S(1)}, bf16[128,512]{1,0:T(8,128)(2,1)S(1)}, u32[]{:S(2)}, u32[]{:S(2)}) collective-permute-start(bf16[128,512]{1,0:T(8,128)(2,1)S(1)} %get-tuple-element.149), channel_id=1, source_target_pairs={{0,2},{1,3},{2,4},{3,5},{4,6},{5,7},{6,0},{7,1},{8,10},{9,11},{10,... | collective-permute-start | bytes 393224 | tf_op jit(solution)/shard_map/ppermute | solution.py:317
  57.3 9.5 %collective-permute-start.25 = (bf16[128,512]{1,0:T(8,128)(2,1)S(1)}, bf16[128,512]{1,0:T(8,128)(2,1)S(1)}, u32[]{:S(2)}, u32[]{:S(2)}) collective-permute-start(bf16[128,512]{1,0:T(8,128)(2,1)S(1)} %get-tuple-element.150), channel_id=1, source_target_pairs={{0,2},{1,3},{2,4},{3,5},{4,6},{5,7},{6,0},{7,1},{8,10},{9,11},{10,... | collective-permute-start | bytes 393224 | tf_op jit(solution)/shard_map/ppermute | solution.py:317
  58.8 9.7 %collective-permute-start.35 = (bf16[128,512]{1,0:T(8,128)(2,1)S(1)}, bf16[128,512]{1,0:T(8,128)(2,1)S(1)}, u32[]{:S(2)}, u32[]{:S(2)}) collective-permute-start(bf16[128,512]{1,0:T(8,128)(2,1)S(1)} %shard_map.79.refs_0_), channel_id=1, source_target_pairs={{0,8},{1,9},{2,10},{3,11},{4,12},{5,13},{6,14},{7,15},{8,16},{9,17... | collective-permute-start | bytes 393224 | tf_op jit(solution)/shard_map/ppermute | solution.py:339
  61.6 8.2 %collective-permute-start.32 = (bf16[128,512]{1,0:T(8,128)(2,1)S(1)}, bf16[128,512]{1,0:T(8,128)(2,1)S(1)}, u32[]{:S(2)}, u32[]{:S(2)}) collective-permute-start(bf16[128,512]{1,0:T(8,128)(2,1)S(1)} %shard_map.78.refs_1_), channel_id=1, source_target_pairs={{0,8},{1,9},{2,10},{3,11},{4,12},{5,13},{6,14},{7,15},{8,16},{9,17... | collective-permute-start | bytes 393224 | tf_op jit(solution)/shard_map/ppermute | solution.py:339
  64.4 6.7 %collective-permute-start.29 = (bf16[128,512]{1,0:T(8,128)(2,1)S(1)}, bf16[128,512]{1,0:T(8,128)(2,1)S(1)}, u32[]{:S(2)}, u32[]{:S(2)}) collective-permute-start(bf16[128,512]{1,0:T(8,128)(2,1)S(1)} %shard_map.77.refs_2_), channel_id=1, source_target_pairs={{0,8},{1,9},{2,10},{3,11},{4,12},{5,13},{6,14},{7,15},{8,16},{9,17... | collective-permute-start | bytes 393224 | tf_op jit(solution)/shard_map/ppermute | solution.py:339
  75.3 8.1 %collective-permute-start.46 = (bf16[128,512]{1,0:T(8,128)(2,1)S(1)}, bf16[128,512]{1,0:T(8,128)(2,1)S(1)}, u32[]{:S(2)}, u32[]{:S(2)}) collective-permute-start(bf16[128,512]{1,0:T(8,128)(2,1)S(1)} %get-tuple-element.143), channel_id=1, source_target_pairs={{16,18},{17,19},{18,20},{19,21},{20,22},{21,23},{2,0},{3,1},{4,2},... | collective-permute-start | bytes 393224 | tf_op jit(solution)/shard_map/ppermute | solution.py:317
  76.5 9.6 %collective-permute-start.43 = (bf16[128,512]{1,0:T(8,128)(2,1)S(1)}, bf16[128,512]{1,0:T(8,128)(2,1)S(1)}, u32[]{:S(2)}, u32[]{:S(2)}) collective-permute-start(bf16[128,512]{1,0:T(8,128)(2,1)S(1)} %get-tuple-element.144), channel_id=1, source_target_pairs={{16,18},{17,19},{18,20},{19,21},{20,22},{21,23},{2,0},{3,1},{4,2},... | collective-permute-start | bytes 393224 | tf_op jit(solution)/shard_map/ppermute | solution.py:317
  78.1 10.8 %collective-permute-start.40 = (bf16[128,512]{1,0:T(8,128)(2,1)S(1)}, bf16[128,512]{1,0:T(8,128)(2,1)S(1)}, u32[]{:S(2)}, u32[]{:S(2)}) collective-permute-start(bf16[128,512]{1,0:T(8,128)(2,1)S(1)} %get-tuple-element.145), channel_id=1, source_target_pairs={{16,18},{17,19},{18,20},{19,21},{20,22},{21,23},{2,0},{3,1},{4,2},... | collective-permute-start | bytes 393224 | tf_op jit(solution)/shard_map/ppermute | solution.py:317
  79.3 12.2 %collective-permute-start.37 = (bf16[128,512]{1,0:T(8,128)(2,1)S(1)}, bf16[128,512]{1,0:T(8,128)(2,1)S(1)}, u32[]{:S(2)}, u32[]{:S(2)}) collective-permute-start(bf16[128,512]{1,0:T(8,128)(2,1)S(1)} %get-tuple-element.146), channel_id=1, source_target_pairs={{16,18},{17,19},{18,20},{19,21},{20,22},{21,23},{2,0},{3,1},{4,2},... | collective-permute-start | bytes 393224 | tf_op jit(solution)/shard_map/ppermute | solution.py:317
  83.4 10.5 %collective-permute-start.47 = (bf16[128,512]{1,0:T(8,128)(2,1)S(1)}, bf16[128,512]{1,0:T(8,128)(2,1)S(1)}, u32[]{:S(2)}, u32[]{:S(2)}) collective-permute-start(bf16[128,512]{1,0:T(8,128)(2,1)S(1)} %shard_map.88.refs_0_), channel_id=1, source_target_pairs={{0,8},{1,9},{2,10},{3,11},{4,12},{5,13},{6,14},{7,15},{8,0},{9,1},... | collective-permute-start | bytes 393224 | tf_op jit(solution)/shard_map/ppermute | solution.py:339
  86.3 8.9 %collective-permute-start.44 = (bf16[128,512]{1,0:T(8,128)(2,1)S(1)}, bf16[128,512]{1,0:T(8,128)(2,1)S(1)}, u32[]{:S(2)}, u32[]{:S(2)}) collective-permute-start(bf16[128,512]{1,0:T(8,128)(2,1)S(1)} %shard_map.87.refs_1_), channel_id=1, source_target_pairs={{0,8},{1,9},{2,10},{3,11},{4,12},{5,13},{6,14},{7,15},{8,0},{9,1},... | collective-permute-start | bytes 393224 | tf_op jit(solution)/shard_map/ppermute | solution.py:339
  89.1 7.4 %collective-permute-start.41 = (bf16[128,512]{1,0:T(8,128)(2,1)S(1)}, bf16[128,512]{1,0:T(8,128)(2,1)S(1)}, u32[]{:S(2)}, u32[]{:S(2)}) collective-permute-start(bf16[128,512]{1,0:T(8,128)(2,1)S(1)} %shard_map.86.refs_2_), channel_id=1, source_target_pairs={{0,8},{1,9},{2,10},{3,11},{4,12},{5,13},{6,14},{7,15},{8,0},{9,1},... | collective-permute-start | bytes 393224 | tf_op jit(solution)/shard_map/ppermute | solution.py:339
  100.2 12.8 %collective-permute-start.51 = (bf16[336,512]{1,0:T(8,128)(2,1)S(1)}, bf16[336,512]{1,0:T(8,128)(2,1)S(1)}, u32[]{:S(2)}, u32[]{:S(2)}) collective-permute-start(bf16[336,512]{1,0:T(8,128)(2,1)S(1)} %add_convert_fusion), channel_id=1, source_target_pairs={{24,26},{25,27},{26,28},{27,29},{28,30},{29,31}} | collective-permute-start | bytes 1032200 | tf_op jit(solution)/shard_map/ppermute | solution.py:317
  102.2 13.9 %collective-permute-start.49 = (bf16[176,512]{1,0:T(8,128)(2,1)S(1)}, bf16[176,512]{1,0:T(8,128)(2,1)S(1)}, u32[]{:S(2)}, u32[]{:S(2)}) collective-permute-start(bf16[176,512]{1,0:T(8,128)(2,1)S(1)} %add_convert_fusion.1), channel_id=1, source_target_pairs={{24,26},{25,27},{26,28},{27,29},{28,30},{29,31}} | collective-permute-start | bytes 540680 | tf_op jit(solution)/shard_map/ppermute | solution.py:317
  (32 other events, 124.1 us)

commit v6 on v5

--- a/solution.py
+++ b/solution.py
@@ -9,6 +9,7 @@
 
 PARTS = (8, 8, 8, 8)
 CHUNKS = len(PARTS)
+JOINED = (0, 2, 3)
 LAST_PARTS = (21, 11)
 AXES = ("site", "sector")
 LIMIT = 20 << 20
@@ -116,14 +117,15 @@
         entering[p] = cut(env[p + 1, 0], 0, dims)
 
 
-def step_kernel(step, row, fresh, added, groups, cuts, flags, *refs):
+def step_kernel(step, row, count, fresh, added, groups, cuts, flags, *refs):
     refs = list(refs)
     entering = refs.pop(0) if fresh else None
-    held, ket, bra = refs[:3]
-    before = refs[3 : 3 + len(groups)] if added else [None] * len(groups)
-    outs = refs[3 + len(groups) * added :]
+    held, (ket, bra) = refs[:count], refs[count : count + 2]
+    refs = refs[count + 2 :]
+    before = refs[: len(groups)] if added else [None] * len(groups)
+    outs = refs[len(groups) * added :]
     pair = pair_of(step, ket.shape[1])
-    e = held[...]
+    e = jnp.concatenate([rows[...] for rows in held], axis=0)
     if fresh:
         e = jnp.where(lax.axis_index("site") == 0, entering[step - 1, row : row + e.shape[0]], e)
     for states, start, out in zip(groups, before, outs):
@@ -239,14 +241,14 @@
     def blocks_of(parts):
         return [block(end - start) for start, end in zip(parts, parts[1:])]
 
-    def chunk(step, k, groups, held, before, dtype, parts=None):
+    def chunk(step, start, end, groups, held, before, dtype, parts=None):
         fresh = step < pairs
-        operands = [flag_rows] + ([entering] if fresh else []) + [held, ket, bra] + before
+        operands = [flag_rows] + ([entering] if fresh else []) + held[start:end] + [ket, bra] + before
         return call(
-            functools.partial(step_kernel, step, cuts[k], fresh, len(before) > 0, groups, parts),
+            functools.partial(step_kernel, step, cuts[start], end - start, fresh, len(before) > 0, groups, parts),
             [VMEM] * len(operands),
             [block(width, dtype)] * len(groups) if parts is None else blocks_of(parts),
-            4 * sum(len(states) for states in groups) * (cuts[k + 1] - cuts[k]) * width**2,
+            4 * sum(len(states) for states in groups) * (cuts[end] - cuts[start]) * width**2,
             out_specs=[VMEM] * (len(groups) if parts is None else len(parts) - 1),
         )(*operands)
 
@@ -300,13 +302,13 @@
             )(sector_dims, env_in, double)
         else:
             total = []
-            for k in range(CHUNKS - 1):
-                total = chunk(step, k, [(1, 2), (3,), (0,)], held[k], list(total), jnp.float32)
+            for start, end in zip(JOINED, JOINED[1:]):
+                total = chunk(step, start, end, [(1, 2), (3,), (0,)], held, list(total), jnp.float32)
             total = list(total)
             parts = cuts if step + 1 < steps else last_cuts
-            single = chunk(step, CHUNKS - 1, [(1, 2)], held[-1], total[:1], jnp.bfloat16, parts)
+            single = chunk(step, CHUNKS - 1, CHUNKS, [(1, 2)], held, total[:1], jnp.bfloat16, parts)
             other = swapped(single)
-            double, none = chunk(step, CHUNKS - 1, [(3,), (0,)], held[-1], total[1:], jnp.bfloat16)
+            double, none = chunk(step, CHUNKS - 1, CHUNKS, [(3,), (0,)], held, total[1:], jnp.bfloat16)
         fresh = []
         if step + 1 == steps:
             cuts = last_cuts

time: 117 us -> 117 us (level)
  waiting for transfers between devices: 35 us -> 39.3 us
  Pallas kernels: 31.2 us -> 27 us
    pallas_call x20 -> x16, Pallas kernels: 21 us -> 16.8 us  [chunk(): call(functools.partial(step_kernel, step, cuts[start], end - start, fresh...]
    ppermute x16, waiting for transfers between devices: 2.6 us -> 6.41 us  [per_device(): held = [lax.ppermute(rows, AXES, next_pairs(step)) for rows in fresh]]
  transfers between devices with their start and end apart: 52 -> 52, of which waited for: 25 -> 29; matrix products, arithmetic and copies ran while one was open for 0% -> 0% of each run, Pallas kernels for 21% -> 17%
where the time goes in v6:
time: 117 us
  starting transfers between devices  48.9 us (42%)
  waiting for transfers between devices  39.3 us (34%)
  Pallas kernels  27 us (23%)
    ppermute x18, waiting for transfers between devices, per_device(): came = lax.ppermute(up, AXES, up_pairs(step))  32.1 us
    ppermute x18, starting transfers between devices, per_device(): came = lax.ppermute(up, AXES, up_pairs(step))  23.3 us
    ppermute x16, starting transfers between devices, per_device(): held = [lax.ppermute(rows, AXES, next_pairs(step)) for rows in fresh]  20.7 us
    pallas_call x16, Pallas kernels, chunk(): call(functools.partial(step_kernel, step, cuts[start], end - start, fresh...  16.8 us
    ppermute x16, waiting for transfers between devices, per_device(): held = [lax.ppermute(rows, AXES, next_pairs(step)) for rows in fresh]  6.41 us
    ppermute x18, starting transfers between devices, swapped(): return [lax.ppermute(part, AXES, swap_pairs) for part in parts]  4.88 us
    pallas_call x1, Pallas kernels, per_device(): call(functools.partial(open_kernel, first, later, cuts), [pl.BlockSpec(me...  3.69 us
  transfers between devices with their start and end apart: 52, of which 29 were waited for; matrix products, arithmetic and copies ran while one was open for 0% of the time, Pallas kernels for 17%

profile of v6, /device:TPU:14, one launch (start us, length us, event | category | flops | bytes accessed | tf_op | source)
XLA Modules:
  0.0 116.6 jit_solution(9198684895929804209)
XLA Ops:
  0.0 3.7 %shard_map.55 = (bf16[128,512]{1,0:T(8,128)(2,1)S(1)}, bf16[128,512]{1,0:T(8,128)(2,1)S(1)}, bf16[128,512]{1,0:T(8,128)(2,1)}, bf16[128,512]{1,0:T(8,128)(2,1)},...) custom-call(s32[5,8]{1,0:T(8,128)} %dims.1, s32[4]{0:T(128)} %bitcast.1, ...), custom_call_target="tpu_custom_call" | custom-call | flops 1073741824 | tf_op jit(solution)/shard_map/pallas_call | solution.py:264
  7.4 1.6 %collective-permute-start.4 = (bf16[128,512]{1,0:T(8,128)(2,1)S(1)}, bf16[128,512]{1,0:T(8,128)(2,1)S(1)}, u32[]{:S(2)}, u32[]{:S(2)}) collective-permute-start(bf16[128,512]{1,0:T(8,128)(2,1)S(1)} %get-tuple-element.133), channel_id=1, source_target_pairs={{0,2},{1,3},{2,4},{3,5},{4,6},{5,7},{18,16},{19,17},{20,18},{21,19... | collective-permute-start | bytes 393224 | tf_op jit(solution)/shard_map/ppermute | solution.py:319
  9.8 1.6 %collective-permute-start.1 = (bf16[128,512]{1,0:T(8,128)(2,1)S(1)}, bf16[128,512]{1,0:T(8,128)(2,1)S(1)}, u32[]{:S(2)}, u32[]{:S(2)}) collective-permute-start(bf16[128,512]{1,0:T(8,128)(2,1)S(1)} %get-tuple-element.134), channel_id=1, source_target_pairs={{0,2},{1,3},{2,4},{3,5},{4,6},{5,7},{18,16},{19,17},{20,18},{21,19... | collective-permute-start | bytes 393224 | tf_op jit(solution)/shard_map/ppermute | solution.py:319
  13.5 2.1 %collective-permute-done.10.came = bf16[128,512]{1,0:T(8,128)(2,1)S(1)} collective-permute-done((bf16[128,512]{1,0:T(8,128)(2,1)S(1)}, bf16[128,512]{1,0:T(8,128)(2,1)S(1)}, u32[]{:S(2)}, u32[]{:S(2)}) %collective-permute-start.10) | collective-permute-done | bytes 131104 | tf_op jit(solution)/shard_map/ppermute | solution.py:319
  16.3 2.1 %collective-permute-done.4.came = bf16[128,512]{1,0:T(8,128)(2,1)S(1)} collective-permute-done((bf16[128,512]{1,0:T(8,128)(2,1)S(1)}, bf16[128,512]{1,0:T(8,128)(2,1)S(1)}, u32[]{:S(2)}, u32[]{:S(2)}) %collective-permute-start.4) | collective-permute-done | bytes 131104 | tf_op jit(solution)/shard_map/ppermute | solution.py:319
  29.3 1.6 %collective-permute-start.22 = (bf16[128,512]{1,0:T(8,128)(2,1)S(1)}, bf16[128,512]{1,0:T(8,128)(2,1)S(1)}, u32[]{:S(2)}, u32[]{:S(2)}) collective-permute-start(bf16[128,512]{1,0:T(8,128)(2,1)S(1)} %get-tuple-element.127), channel_id=1, source_target_pairs={{0,2},{1,3},{2,4},{3,5},{4,6},{5,7},{6,0},{7,1},{8,10},{9,11},{10,... | collective-permute-start | bytes 393224 | tf_op jit(solution)/shard_map/ppermute | solution.py:319
  32.7 1.6 %collective-permute-start.13 = (bf16[128,512]{1,0:T(8,128)(2,1)S(1)}, bf16[128,512]{1,0:T(8,128)(2,1)S(1)}, u32[]{:S(2)}, u32[]{:S(2)}) collective-permute-start(bf16[128,512]{1,0:T(8,128)(2,1)S(1)} %get-tuple-element.130), channel_id=1, source_target_pairs={{0,2},{1,3},{2,4},{3,5},{4,6},{5,7},{6,0},{7,1},{8,10},{9,11},{10,... | collective-permute-start | bytes 393224 | tf_op jit(solution)/shard_map/ppermute | solution.py:319
  36.3 2.2 %collective-permute-done.19.came = bf16[128,512]{1,0:T(8,128)(2,1)S(1)} collective-permute-done((bf16[128,512]{1,0:T(8,128)(2,1)S(1)}, bf16[128,512]{1,0:T(8,128)(2,1)S(1)}, u32[]{:S(2)}, u32[]{:S(2)}) %collective-permute-start.19) | collective-permute-done | bytes 131104 | tf_op jit(solution)/shard_map/ppermute | solution.py:319
  39.1 2.2 %collective-permute-done.16.came = bf16[128,512]{1,0:T(8,128)(2,1)S(1)} collective-permute-done((bf16[128,512]{1,0:T(8,128)(2,1)S(1)}, bf16[128,512]{1,0:T(8,128)(2,1)S(1)}, u32[]{:S(2)}, u32[]{:S(2)}) %collective-permute-start.16) | collective-permute-done | bytes 131104 | tf_op jit(solution)/shard_map/ppermute | solution.py:319
  52.1 1.6 %collective-permute-start.34 = (bf16[128,512]{1,0:T(8,128)(2,1)S(1)}, bf16[128,512]{1,0:T(8,128)(2,1)S(1)}, u32[]{:S(2)}, u32[]{:S(2)}) collective-permute-start(bf16[128,512]{1,0:T(8,128)(2,1)S(1)} %get-tuple-element.123), channel_id=1, source_target_pairs={{0,2},{1,3},{2,4},{3,5},{4,6},{5,7},{6,0},{7,1},{8,10},{9,11},{10,... | collective-permute-start | bytes 393224 | tf_op jit(solution)/shard_map/ppermute | solution.py:319
  55.3 2.0 %collective-permute-start.28 = (bf16[128,512]{1,0:T(8,128)(2,1)S(1)}, bf16[128,512]{1,0:T(8,128)(2,1)S(1)}, u32[]{:S(2)}, u32[]{:S(2)}) collective-permute-start(bf16[128,512]{1,0:T(8,128)(2,1)S(1)} %get-tuple-element.125), channel_id=1, source_target_pairs={{0,2},{1,3},{2,4},{3,5},{4,6},{5,7},{6,0},{7,1},{8,10},{9,11},{10,... | collective-permute-start | bytes 393224 | tf_op jit(solution)/shard_map/ppermute | solution.py:319
  58.8 1.6 %collective-permute-start.35 = (bf16[128,512]{1,0:T(8,128)(2,1)S(1)}, bf16[128,512]{1,0:T(8,128)(2,1)S(1)}, u32[]{:S(2)}, u32[]{:S(2)}) collective-permute-start(bf16[128,512]{1,0:T(8,128)(2,1)S(1)} %shard_map.77.refs_1_), channel_id=1, source_target_pairs={{0,8},{1,9},{2,10},{3,11},{4,12},{5,13},{6,14},{7,15},{8,16},{9,17... | collective-permute-start | bytes 393224 | tf_op jit(solution)/shard_map/ppermute | solution.py:341
  61.6 1.6 %collective-permute-start.32 = (bf16[128,512]{1,0:T(8,128)(2,1)S(1)}, bf16[128,512]{1,0:T(8,128)(2,1)S(1)}, u32[]{:S(2)}, u32[]{:S(2)}) collective-permute-start(bf16[128,512]{1,0:T(8,128)(2,1)S(1)} %shard_map.76.refs_0_), channel_id=1, source_target_pairs={{0,8},{1,9},{2,10},{3,11},{4,12},{5,13},{6,14},{7,15},{8,16},{9,17... | collective-permute-start | bytes 393224 | tf_op jit(solution)/shard_map/ppermute | solution.py:341
  64.4 1.6 %collective-permute-start.29 = (bf16[128,512]{1,0:T(8,128)(2,1)S(1)}, bf16[128,512]{1,0:T(8,128)(2,1)S(1)}, u32[]{:S(2)}, u32[]{:S(2)}) collective-permute-start(bf16[128,512]{1,0:T(8,128)(2,1)S(1)} %shard_map.75.refs_2_), channel_id=1, source_target_pairs={{0,8},{1,9},{2,10},{3,11},{4,12},{5,13},{6,14},{7,15},{8,16},{9,17... | collective-permute-start | bytes 393224 | tf_op jit(solution)/shard_map/ppermute | solution.py:341
  66.9 1.6 %collective-permute-start.26 = (bf16[128,512]{1,0:T(8,128)(2,1)S(1)}, bf16[128,512]{1,0:T(8,128)(2,1)S(1)}, u32[]{:S(2)}, u32[]{:S(2)}) collective-permute-start(bf16[128,512]{1,0:T(8,128)(2,1)S(1)} %shard_map.74.refs_3_), channel_id=1, source_target_pairs={{0,8},{1,9},{2,10},{3,11},{4,12},{5,13},{6,14},{7,15},{8,16},{9,17... | collective-permute-start | bytes 393224 | tf_op jit(solution)/shard_map/ppermute | solution.py:341
  79.1 4.3 %collective-permute-done.46.came = bf16[128,512]{1,0:T(8,128)(2,1)S(1)} collective-permute-done((bf16[128,512]{1,0:T(8,128)(2,1)S(1)}, bf16[128,512]{1,0:T(8,128)(2,1)S(1)}, u32[]{:S(2)}, u32[]{:S(2)}) %collective-permute-start.46) | collective-permute-done | bytes 131104 | tf_op jit(solution)/shard_map/ppermute | solution.py:319
  83.4 2.4 %collective-permute-start.47 = (bf16[128,512]{1,0:T(8,128)(2,1)S(1)}, bf16[128,512]{1,0:T(8,128)(2,1)S(1)}, u32[]{:S(2)}, u32[]{:S(2)}) collective-permute-start(bf16[128,512]{1,0:T(8,128)(2,1)S(1)} %shard_map.85.refs_1_), channel_id=1, source_target_pairs={{0,8},{1,9},{2,10},{3,11},{4,12},{5,13},{6,14},{7,15},{8,0},{9,1},... | collective-permute-start | bytes 393224 | tf_op jit(solution)/shard_map/ppermute | solution.py:341
  86.2 2.4 %collective-permute-start.44 = (bf16[128,512]{1,0:T(8,128)(2,1)S(1)}, bf16[128,512]{1,0:T(8,128)(2,1)S(1)}, u32[]{:S(2)}, u32[]{:S(2)}) collective-permute-start(bf16[128,512]{1,0:T(8,128)(2,1)S(1)} %shard_map.84.refs_0_), channel_id=1, source_target_pairs={{0,8},{1,9},{2,10},{3,11},{4,12},{5,13},{6,14},{7,15},{8,0},{9,1},... | collective-permute-start | bytes 393224 | tf_op jit(solution)/shard_map/ppermute | solution.py:341
  89.1 2.4 %collective-permute-start.41 = (bf16[128,512]{1,0:T(8,128)(2,1)S(1)}, bf16[128,512]{1,0:T(8,128)(2,1)S(1)}, u32[]{:S(2)}, u32[]{:S(2)}) collective-permute-start(bf16[128,512]{1,0:T(8,128)(2,1)S(1)} %shard_map.83.refs_2_), channel_id=1, source_target_pairs={{0,8},{1,9},{2,10},{3,11},{4,12},{5,13},{6,14},{7,15},{8,0},{9,1},... | collective-permute-start | bytes 393224 | tf_op jit(solution)/shard_map/ppermute | solution.py:341
  91.6 2.3 %collective-permute-start.38 = (bf16[128,512]{1,0:T(8,128)(2,1)S(1)}, bf16[128,512]{1,0:T(8,128)(2,1)S(1)}, u32[]{:S(2)}, u32[]{:S(2)}) collective-permute-start(bf16[128,512]{1,0:T(8,128)(2,1)S(1)} %shard_map.82.refs_3_), channel_id=1, source_target_pairs={{0,8},{1,9},{2,10},{3,11},{4,12},{5,13},{6,14},{7,15},{8,0},{9,1},... | collective-permute-start | bytes 393224 | tf_op jit(solution)/shard_map/ppermute | solution.py:341
  99.7 1.9 %collective-permute-start.51 = (bf16[336,512]{1,0:T(8,128)(2,1)S(1)}, bf16[336,512]{1,0:T(8,128)(2,1)S(1)}, u32[]{:S(2)}, u32[]{:S(2)}) collective-permute-start(bf16[336,512]{1,0:T(8,128)(2,1)S(1)} %add_convert_fusion), channel_id=1, source_target_pairs={{24,26},{25,27},{26,28},{27,29},{28,30},{29,31}} | collective-permute-start | bytes 1032200 | tf_op jit(solution)/shard_map/ppermute | solution.py:319
  101.7 2.9 %collective-permute-start.49 = (bf16[176,512]{1,0:T(8,128)(2,1)S(1)}, bf16[176,512]{1,0:T(8,128)(2,1)S(1)}, u32[]{:S(2)}, u32[]{:S(2)}) collective-permute-start(bf16[176,512]{1,0:T(8,128)(2,1)S(1)} %add_convert_fusion.1), channel_id=1, source_target_pairs={{24,26},{25,27},{26,28},{27,29},{28,30},{29,31}} | collective-permute-start | bytes 540680 | tf_op jit(solution)/shard_map/ppermute | solution.py:319
  105.7 6.9 %collective-permute-done.51.came = bf16[336,512]{1,0:T(8,128)(2,1)S(1)} collective-permute-done((bf16[336,512]{1,0:T(8,128)(2,1)S(1)}, bf16[336,512]{1,0:T(8,128)(2,1)S(1)}, u32[]{:S(2)}, u32[]{:S(2)}) %collective-permute-start.51) | collective-permute-done | bytes 344096 | tf_op jit(solution)/shard_map/ppermute | solution.py:319
  113.5 2.1 %collective-permute-done.49.came = bf16[176,512]{1,0:T(8,128)(2,1)S(1)} collective-permute-done((bf16[176,512]{1,0:T(8,128)(2,1)S(1)}, bf16[176,512]{1,0:T(8,128)(2,1)S(1)}, u32[]{:S(2)}, u32[]{:S(2)}) %collective-permute-start.49) | collective-permute-done | bytes 180256 | tf_op jit(solution)/shard_map/ppermute | solution.py:319
  (135 shorter events, 59.4 us)
Async XLA Ops:
  6.4 6.4 %collective-permute-start.7 = (bf16[128,512]{1,0:T(8,128)(2,1)S(1)}, bf16[128,512]{1,0:T(8,128)(2,1)S(1)}, u32[]{:S(2)}, u32[]{:S(2)}) collective-permute-start(bf16[128,512]{1,0:T(8,128)(2,1)S(1)} %get-tuple-element.132), channel_id=1, source_target_pairs={{0,2},{1,3},{2,4},{3,5},{4,6},{5,7},{18,16},{19,17},{20,18},{21,19... | collective-permute-start | bytes 393224 | tf_op jit(solution)/shard_map/ppermute | solution.py:319
  6.9 8.7 %collective-permute-start.10 = (bf16[128,512]{1,0:T(8,128)(2,1)S(1)}, bf16[128,512]{1,0:T(8,128)(2,1)S(1)}, u32[]{:S(2)}, u32[]{:S(2)}) collective-permute-start(bf16[128,512]{1,0:T(8,128)(2,1)S(1)} %get-tuple-element.131), channel_id=1, source_target_pairs={{0,2},{1,3},{2,4},{3,5},{4,6},{5,7},{18,16},{19,17},{20,18},{21,19... | collective-permute-start | bytes 393224 | tf_op jit(solution)/shard_map/ppermute | solution.py:319
  7.4 11.0 %collective-permute-start.4 = (bf16[128,512]{1,0:T(8,128)(2,1)S(1)}, bf16[128,512]{1,0:T(8,128)(2,1)S(1)}, u32[]{:S(2)}, u32[]{:S(2)}) collective-permute-start(bf16[128,512]{1,0:T(8,128)(2,1)S(1)} %get-tuple-element.133), channel_id=1, source_target_pairs={{0,2},{1,3},{2,4},{3,5},{4,6},{5,7},{18,16},{19,17},{20,18},{21,19... | collective-permute-start | bytes 393224 | tf_op jit(solution)/shard_map/ppermute | solution.py:319
  9.8 10.5 %collective-permute-start.1 = (bf16[128,512]{1,0:T(8,128)(2,1)S(1)}, bf16[128,512]{1,0:T(8,128)(2,1)S(1)}, u32[]{:S(2)}, u32[]{:S(2)}) collective-permute-start(bf16[128,512]{1,0:T(8,128)(2,1)S(1)} %get-tuple-element.134), channel_id=1, source_target_pairs={{0,2},{1,3},{2,4},{3,5},{4,6},{5,7},{18,16},{19,17},{20,18},{21,19... | collective-permute-start | bytes 393224 | tf_op jit(solution)/shard_map/ppermute | solution.py:319
  12.9 8.1 %collective-permute-start.8 = (bf16[128,512]{1,0:T(8,128)(2,1)S(1)}, bf16[128,512]{1,0:T(8,128)(2,1)S(1)}, u32[]{:S(2)}, u32[]{:S(2)}) collective-permute-start(bf16[128,512]{1,0:T(8,128)(2,1)S(1)} %shard_map.60.refs_0_), channel_id=1, source_target_pairs={{0,8},{1,9},{2,10},{3,11},{4,12},{5,13},{6,14},{7,15},{8,0},{9,1},... | collective-permute-start | bytes 393224 | tf_op jit(solution)/shard_map/ppermute | solution.py:341
  29.3 6.4 %collective-permute-start.22 = (bf16[128,512]{1,0:T(8,128)(2,1)S(1)}, bf16[128,512]{1,0:T(8,128)(2,1)S(1)}, u32[]{:S(2)}, u32[]{:S(2)}) collective-permute-start(bf16[128,512]{1,0:T(8,128)(2,1)S(1)} %get-tuple-element.127), channel_id=1, source_target_pairs={{0,2},{1,3},{2,4},{3,5},{4,6},{5,7},{6,0},{7,1},{8,10},{9,11},{10,... | collective-permute-start | bytes 393224 | tf_op jit(solution)/shard_map/ppermute | solution.py:319
  30.9 7.6 %collective-permute-start.19 = (bf16[128,512]{1,0:T(8,128)(2,1)S(1)}, bf16[128,512]{1,0:T(8,128)(2,1)S(1)}, u32[]{:S(2)}, u32[]{:S(2)}) collective-permute-start(bf16[128,512]{1,0:T(8,128)(2,1)S(1)} %get-tuple-element.128), channel_id=1, source_target_pairs={{0,2},{1,3},{2,4},{3,5},{4,6},{5,7},{6,0},{7,1},{8,10},{9,11},{10,... | collective-permute-start | bytes 393224 | tf_op jit(solution)/shard_map/ppermute | solution.py:319
  32.5 8.8 %collective-permute-start.16 = (bf16[128,512]{1,0:T(8,128)(2,1)S(1)}, bf16[128,512]{1,0:T(8,128)(2,1)S(1)}, u32[]{:S(2)}, u32[]{:S(2)}) collective-permute-start(bf16[128,512]{1,0:T(8,128)(2,1)S(1)} %get-tuple-element.129), channel_id=1, source_target_pairs={{0,2},{1,3},{2,4},{3,5},{4,6},{5,7},{6,0},{7,1},{8,10},{9,11},{10,... | collective-permute-start | bytes 393224 | tf_op jit(solution)/shard_map/ppermute | solution.py:319
  32.7 10.8 %collective-permute-start.13 = (bf16[128,512]{1,0:T(8,128)(2,1)S(1)}, bf16[128,512]{1,0:T(8,128)(2,1)S(1)}, u32[]{:S(2)}, u32[]{:S(2)}) collective-permute-start(bf16[128,512]{1,0:T(8,128)(2,1)S(1)} %get-tuple-element.130), channel_id=1, source_target_pairs={{0,2},{1,3},{2,4},{3,5},{4,6},{5,7},{6,0},{7,1},{8,10},{9,11},{10,... | collective-permute-start | bytes 393224 | tf_op jit(solution)/shard_map/ppermute | solution.py:319
  35.8 8.3 %collective-permute-start.23 = (bf16[128,512]{1,0:T(8,128)(2,1)S(1)}, bf16[128,512]{1,0:T(8,128)(2,1)S(1)}, u32[]{:S(2)}, u32[]{:S(2)}) collective-permute-start(bf16[128,512]{1,0:T(8,128)(2,1)S(1)} %shard_map.69.refs_1_), channel_id=1, source_target_pairs={{0,8},{1,9},{2,10},{3,11},{4,12},{5,13},{6,14},{7,15},{8,16},{9,17... | collective-permute-start | bytes 393224 | tf_op jit(solution)/shard_map/ppermute | solution.py:341
  52.1 6.7 %collective-permute-start.34 = (bf16[128,512]{1,0:T(8,128)(2,1)S(1)}, bf16[128,512]{1,0:T(8,128)(2,1)S(1)}, u32[]{:S(2)}, u32[]{:S(2)}) collective-permute-start(bf16[128,512]{1,0:T(8,128)(2,1)S(1)} %get-tuple-element.123), channel_id=1, source_target_pairs={{0,2},{1,3},{2,4},{3,5},{4,6},{5,7},{6,0},{7,1},{8,10},{9,11},{10,... | collective-permute-start | bytes 393224 | tf_op jit(solution)/shard_map/ppermute | solution.py:319
  53.7 7.8 %collective-permute-start.31 = (bf16[128,512]{1,0:T(8,128)(2,1)S(1)}, bf16[128,512]{1,0:T(8,128)(2,1)S(1)}, u32[]{:S(2)}, u32[]{:S(2)}) collective-permute-start(bf16[128,512]{1,0:T(8,128)(2,1)S(1)} %get-tuple-element.124), channel_id=1, source_target_pairs={{0,2},{1,3},{2,4},{3,5},{4,6},{5,7},{6,0},{7,1},{8,10},{9,11},{10,... | collective-permute-start | bytes 393224 | tf_op jit(solution)/shard_map/ppermute | solution.py:319
  55.3 9.1 %collective-permute-start.28 = (bf16[128,512]{1,0:T(8,128)(2,1)S(1)}, bf16[128,512]{1,0:T(8,128)(2,1)S(1)}, u32[]{:S(2)}, u32[]{:S(2)}) collective-permute-start(bf16[128,512]{1,0:T(8,128)(2,1)S(1)} %get-tuple-element.125), channel_id=1, source_target_pairs={{0,2},{1,3},{2,4},{3,5},{4,6},{5,7},{6,0},{7,1},{8,10},{9,11},{10,... | collective-permute-start | bytes 393224 | tf_op jit(solution)/shard_map/ppermute | solution.py:319
  57.3 9.5 %collective-permute-start.25 = (bf16[128,512]{1,0:T(8,128)(2,1)S(1)}, bf16[128,512]{1,0:T(8,128)(2,1)S(1)}, u32[]{:S(2)}, u32[]{:S(2)}) collective-permute-start(bf16[128,512]{1,0:T(8,128)(2,1)S(1)} %get-tuple-element.126), channel_id=1, source_target_pairs={{0,2},{1,3},{2,4},{3,5},{4,6},{5,7},{6,0},{7,1},{8,10},{9,11},{10,... | collective-permute-start | bytes 393224 | tf_op jit(solution)/shard_map/ppermute | solution.py:319
  58.8 9.7 %collective-permute-start.35 = (bf16[128,512]{1,0:T(8,128)(2,1)S(1)}, bf16[128,512]{1,0:T(8,128)(2,1)S(1)}, u32[]{:S(2)}, u32[]{:S(2)}) collective-permute-start(bf16[128,512]{1,0:T(8,128)(2,1)S(1)} %shard_map.77.refs_1_), channel_id=1, source_target_pairs={{0,8},{1,9},{2,10},{3,11},{4,12},{5,13},{6,14},{7,15},{8,16},{9,17... | collective-permute-start | bytes 393224 | tf_op jit(solution)/shard_map/ppermute | solution.py:341
  61.6 6.9 %collective-permute-start.32 = (bf16[128,512]{1,0:T(8,128)(2,1)S(1)}, bf16[128,512]{1,0:T(8,128)(2,1)S(1)}, u32[]{:S(2)}, u32[]{:S(2)}) collective-permute-start(bf16[128,512]{1,0:T(8,128)(2,1)S(1)} %shard_map.76.refs_0_), channel_id=1, source_target_pairs={{0,8},{1,9},{2,10},{3,11},{4,12},{5,13},{6,14},{7,15},{8,16},{9,17... | collective-permute-start | bytes 393224 | tf_op jit(solution)/shard_map/ppermute | solution.py:341
  75.1 8.2 %collective-permute-start.46 = (bf16[128,512]{1,0:T(8,128)(2,1)S(1)}, bf16[128,512]{1,0:T(8,128)(2,1)S(1)}, u32[]{:S(2)}, u32[]{:S(2)}) collective-permute-start(bf16[128,512]{1,0:T(8,128)(2,1)S(1)} %get-tuple-element.119), channel_id=1, source_target_pairs={{16,18},{17,19},{18,20},{19,21},{20,22},{21,23},{2,0},{3,1},{4,2},... | collective-permute-start | bytes 393224 | tf_op jit(solution)/shard_map/ppermute | solution.py:319
  76.5 9.6 %collective-permute-start.43 = (bf16[128,512]{1,0:T(8,128)(2,1)S(1)}, bf16[128,512]{1,0:T(8,128)(2,1)S(1)}, u32[]{:S(2)}, u32[]{:S(2)}) collective-permute-start(bf16[128,512]{1,0:T(8,128)(2,1)S(1)} %get-tuple-element.120), channel_id=1, source_target_pairs={{16,18},{17,19},{18,20},{19,21},{20,22},{21,23},{2,0},{3,1},{4,2},... | collective-permute-start | bytes 393224 | tf_op jit(solution)/shard_map/ppermute | solution.py:319
  78.1 10.9 %collective-permute-start.40 = (bf16[128,512]{1,0:T(8,128)(2,1)S(1)}, bf16[128,512]{1,0:T(8,128)(2,1)S(1)}, u32[]{:S(2)}, u32[]{:S(2)}) collective-permute-start(bf16[128,512]{1,0:T(8,128)(2,1)S(1)} %get-tuple-element.121), channel_id=1, source_target_pairs={{16,18},{17,19},{18,20},{19,21},{20,22},{21,23},{2,0},{3,1},{4,2},... | collective-permute-start | bytes 393224 | tf_op jit(solution)/shard_map/ppermute | solution.py:319
  78.6 12.9 %collective-permute-start.37 = (bf16[128,512]{1,0:T(8,128)(2,1)S(1)}, bf16[128,512]{1,0:T(8,128)(2,1)S(1)}, u32[]{:S(2)}, u32[]{:S(2)}) collective-permute-start(bf16[128,512]{1,0:T(8,128)(2,1)S(1)} %get-tuple-element.122), channel_id=1, source_target_pairs={{16,18},{17,19},{18,20},{19,21},{20,22},{21,23},{2,0},{3,1},{4,2},... | collective-permute-start | bytes 393224 | tf_op jit(solution)/shard_map/ppermute | solution.py:319
  83.4 10.5 %collective-permute-start.47 = (bf16[128,512]{1,0:T(8,128)(2,1)S(1)}, bf16[128,512]{1,0:T(8,128)(2,1)S(1)}, u32[]{:S(2)}, u32[]{:S(2)}) collective-permute-start(bf16[128,512]{1,0:T(8,128)(2,1)S(1)} %shard_map.85.refs_1_), channel_id=1, source_target_pairs={{0,8},{1,9},{2,10},{3,11},{4,12},{5,13},{6,14},{7,15},{8,0},{9,1},... | collective-permute-start | bytes 393224 | tf_op jit(solution)/shard_map/ppermute | solution.py:341
  86.2 7.7 %collective-permute-start.44 = (bf16[128,512]{1,0:T(8,128)(2,1)S(1)}, bf16[128,512]{1,0:T(8,128)(2,1)S(1)}, u32[]{:S(2)}, u32[]{:S(2)}) collective-permute-start(bf16[128,512]{1,0:T(8,128)(2,1)S(1)} %shard_map.84.refs_0_), channel_id=1, source_target_pairs={{0,8},{1,9},{2,10},{3,11},{4,12},{5,13},{6,14},{7,15},{8,0},{9,1},... | collective-permute-start | bytes 393224 | tf_op jit(solution)/shard_map/ppermute | solution.py:341
  99.7 12.8 %collective-permute-start.51 = (bf16[336,512]{1,0:T(8,128)(2,1)S(1)}, bf16[336,512]{1,0:T(8,128)(2,1)S(1)}, u32[]{:S(2)}, u32[]{:S(2)}) collective-permute-start(bf16[336,512]{1,0:T(8,128)(2,1)S(1)} %add_convert_fusion), channel_id=1, source_target_pairs={{24,26},{25,27},{26,28},{27,29},{28,30},{29,31}} | collective-permute-start | bytes 1032200 | tf_op jit(solution)/shard_map/ppermute | solution.py:319
  101.7 13.9 %collective-permute-start.49 = (bf16[176,512]{1,0:T(8,128)(2,1)S(1)}, bf16[176,512]{1,0:T(8,128)(2,1)S(1)}, u32[]{:S(2)}, u32[]{:S(2)}) collective-permute-start(bf16[176,512]{1,0:T(8,128)(2,1)S(1)} %add_convert_fusion.1), channel_id=1, source_target_pairs={{24,26},{25,27},{26,28},{27,29},{28,30},{29,31}} | collective-permute-start | bytes 540680 | tf_op jit(solution)/shard_map/ppermute | solution.py:319
  (32 other events, 123.6 us)

commit v7 on v6

--- a/solution.py
+++ b/solution.py
@@ -305,9 +305,11 @@
             for start, end in zip(JOINED, JOINED[1:]):
                 total = chunk(step, start, end, [(1, 2), (3,), (0,)], held, list(total), jnp.float32)
             total = list(total)
-            parts = cuts if step + 1 < steps else last_cuts
+            parts = [0, width] if step + 1 < steps else last_cuts
             single = chunk(step, CHUNKS - 1, CHUNKS, [(1, 2)], held, total[:1], jnp.bfloat16, parts)
             other = swapped(single)
+            if step + 1 < steps:
+                other = [other[0][cuts[k] : cuts[k + 1]] for k in range(CHUNKS)]
             double, none = chunk(step, CHUNKS - 1, CHUNKS, [(3,), (0,)], held, total[1:], jnp.bfloat16)
         fresh = []
         if step + 1 == steps:

time: 117 us -> 116 us (level)
  starting transfers between devices: 48.9 us -> 45.9 us
  waiting for transfers between devices: 39.3 us -> 42 us
    ppermute x18 -> x9, starting transfers between devices: 4.88 us -> 1.86 us  [swapped(): return [lax.ppermute(part, AXES, swap_pairs) for part in parts]]
    ppermute x18 -> x9, waiting for transfers between devices: 0.77 us -> 3.43 us  [swapped(): return [lax.ppermute(part, AXES, swap_pairs) for part in parts]]
  transfers between devices with their start and end apart: 52 -> 43, of which waited for: 29 -> 30; matrix products, arithmetic and copies ran while one was open for 0% -> 0% of each run, Pallas kernels for 17% -> 17%
where the time goes in v7:
time: 116 us
  starting transfers between devices  45.9 us (40%)
  waiting for transfers between devices  42 us (36%)
  Pallas kernels  26.9 us (23%)
    ppermute x18, waiting for transfers between devices, per_device(): came = lax.ppermute(up, AXES, up_pairs(step))  31.4 us
    ppermute x18, starting transfers between devices, per_device(): came = lax.ppermute(up, AXES, up_pairs(step))  23.4 us
    ppermute x16, starting transfers between devices, per_device(): held = [lax.ppermute(rows, AXES, next_pairs(step)) for rows in fresh]  20.6 us
    pallas_call x16, Pallas kernels, chunk(): call(functools.partial(step_kernel, step, cuts[start], end - start, fresh...  16.8 us
    ppermute x16, waiting for transfers between devices, per_device(): held = [lax.ppermute(rows, AXES, next_pairs(step)) for rows in fresh]  7.12 us
    pallas_call x1, Pallas kernels, per_device(): call(functools.partial(open_kernel, first, later, cuts), [pl.BlockSpec(me...  3.68 us
    ppermute x9, waiting for transfers between devices, swapped(): return [lax.ppermute(part, AXES, swap_pairs) for part in parts]  3.43 us
  transfers between devices with their start and end apart: 43, of which 30 were waited for; matrix products, arithmetic and copies ran while one was open for 0% of the time, Pallas kernels for 17%

profile of v7, /device:TPU:14, one launch (start us, length us, event | category | flops | bytes accessed | tf_op | source)
XLA Modules:
  0.0 116.2 jit_solution(12699158966602149443)
XLA Ops:
  0.0 3.7 %shard_map.55 = (bf16[128,512]{1,0:T(8,128)(2,1)S(1)}, bf16[128,512]{1,0:T(8,128)(2,1)S(1)}, bf16[128,512]{1,0:T(8,128)(2,1)}, bf16[128,512]{1,0:T(8,128)(2,1)},...) custom-call(s32[5,8]{1,0:T(8,128)} %dims.1, s32[4]{0:T(128)} %bitcast.1, ...), custom_call_target="tpu_custom_call" | custom-call | flops 1073741824 | tf_op jit(solution)/shard_map/pallas_call | solution.py:264
  7.4 1.6 %collective-permute-start.4 = (bf16[128,512]{1,0:T(8,128)(2,1)S(1)}, bf16[128,512]{1,0:T(8,128)(2,1)S(1)}, u32[]{:S(2)}, u32[]{:S(2)}) collective-permute-start(bf16[128,512]{1,0:T(8,128)(2,1)S(1)} %get-tuple-element.121), channel_id=1, source_target_pairs={{0,2},{1,3},{2,4},{3,5},{4,6},{5,7},{18,16},{19,17},{20,18},{21,19... | collective-permute-start | bytes 393224 | tf_op jit(solution)/shard_map/ppermute | solution.py:321
  9.8 1.6 %collective-permute-start.1 = (bf16[128,512]{1,0:T(8,128)(2,1)S(1)}, bf16[128,512]{1,0:T(8,128)(2,1)S(1)}, u32[]{:S(2)}, u32[]{:S(2)}) collective-permute-start(bf16[128,512]{1,0:T(8,128)(2,1)S(1)} %get-tuple-element.122), channel_id=1, source_target_pairs={{0,2},{1,3},{2,4},{3,5},{4,6},{5,7},{18,16},{19,17},{20,18},{21,19... | collective-permute-start | bytes 393224 | tf_op jit(solution)/shard_map/ppermute | solution.py:321
  13.5 2.1 %collective-permute-done.10.came = bf16[128,512]{1,0:T(8,128)(2,1)S(1)} collective-permute-done((bf16[128,512]{1,0:T(8,128)(2,1)S(1)}, bf16[128,512]{1,0:T(8,128)(2,1)S(1)}, u32[]{:S(2)}, u32[]{:S(2)}) %collective-permute-start.10) | collective-permute-done | bytes 131104 | tf_op jit(solution)/shard_map/ppermute | solution.py:321
  16.3 2.1 %collective-permute-done.4.came = bf16[128,512]{1,0:T(8,128)(2,1)S(1)} collective-permute-done((bf16[128,512]{1,0:T(8,128)(2,1)S(1)}, bf16[128,512]{1,0:T(8,128)(2,1)S(1)}, u32[]{:S(2)}, u32[]{:S(2)}) %collective-permute-start.4) | collective-permute-done | bytes 131104 | tf_op jit(solution)/shard_map/ppermute | solution.py:321
  29.1 1.6 %collective-permute-start.19 = (bf16[128,512]{1,0:T(8,128)(2,1)S(1)}, bf16[128,512]{1,0:T(8,128)(2,1)S(1)}, u32[]{:S(2)}, u32[]{:S(2)}) collective-permute-start(bf16[128,512]{1,0:T(8,128)(2,1)S(1)} %get-tuple-element.103), channel_id=1, source_target_pairs={{0,2},{1,3},{2,4},{3,5},{4,6},{5,7},{6,0},{7,1},{8,10},{9,11},{10,... | collective-permute-start | bytes 393224 | tf_op jit(solution)/shard_map/ppermute | solution.py:321
  36.2 2.2 %collective-permute-done.17.came = bf16[128,512]{1,0:T(8,128)(2,1)S(1)} collective-permute-done((bf16[128,512]{1,0:T(8,128)(2,1)S(1)}, bf16[128,512]{1,0:T(8,128)(2,1)S(1)}, u32[]{:S(2)}, u32[]{:S(2)}) %collective-permute-start.17) | collective-permute-done | bytes 131104 | tf_op jit(solution)/shard_map/ppermute | solution.py:321
  39.0 2.2 %collective-permute-done.15.came = bf16[128,512]{1,0:T(8,128)(2,1)S(1)} collective-permute-done((bf16[128,512]{1,0:T(8,128)(2,1)S(1)}, bf16[128,512]{1,0:T(8,128)(2,1)S(1)}, u32[]{:S(2)}, u32[]{:S(2)}) %collective-permute-start.15) | collective-permute-done | bytes 131104 | tf_op jit(solution)/shard_map/ppermute | solution.py:321
  51.8 1.6 %collective-permute-start.28 = (bf16[128,512]{1,0:T(8,128)(2,1)S(1)}, bf16[128,512]{1,0:T(8,128)(2,1)S(1)}, u32[]{:S(2)}, u32[]{:S(2)}) collective-permute-start(bf16[128,512]{1,0:T(8,128)(2,1)S(1)} %get-tuple-element.99), channel_id=1, source_target_pairs={{0,2},{1,3},{2,4},{3,5},{4,6},{5,7},{6,0},{7,1},{8,10},{9,11},{10,... | collective-permute-start | bytes 393224 | tf_op jit(solution)/shard_map/ppermute | solution.py:321
  55.0 2.0 %collective-permute-start.24 = (bf16[128,512]{1,0:T(8,128)(2,1)S(1)}, bf16[128,512]{1,0:T(8,128)(2,1)S(1)}, u32[]{:S(2)}, u32[]{:S(2)}) collective-permute-start(bf16[128,512]{1,0:T(8,128)(2,1)S(1)} %get-tuple-element.101), channel_id=1, source_target_pairs={{0,2},{1,3},{2,4},{3,5},{4,6},{5,7},{6,0},{7,1},{8,10},{9,11},{10,... | collective-permute-start | bytes 393224 | tf_op jit(solution)/shard_map/ppermute | solution.py:321
  58.5 1.8 %collective-permute-start.29 = (bf16[128,512]{1,0:T(8,128)(2,1)S(1)}, bf16[128,512]{1,0:T(8,128)(2,1)S(1)}, u32[]{:S(2)}, u32[]{:S(2)}) collective-permute-start(bf16[128,512]{1,0:T(8,128)(2,1)S(1)} %shard_map.77.refs_1_), channel_id=1, source_target_pairs={{0,8},{1,9},{2,10},{3,11},{4,12},{5,13},{6,14},{7,15},{8,16},{9,17... | collective-permute-start | bytes 393224 | tf_op jit(solution)/shard_map/ppermute | solution.py:343
  61.3 1.6 %collective-permute-start.27 = (bf16[128,512]{1,0:T(8,128)(2,1)S(1)}, bf16[128,512]{1,0:T(8,128)(2,1)S(1)}, u32[]{:S(2)}, u32[]{:S(2)}) collective-permute-start(bf16[128,512]{1,0:T(8,128)(2,1)S(1)} %shard_map.76.refs_0_), channel_id=1, source_target_pairs={{0,8},{1,9},{2,10},{3,11},{4,12},{5,13},{6,14},{7,15},{8,16},{9,17... | collective-permute-start | bytes 393224 | tf_op jit(solution)/shard_map/ppermute | solution.py:343
  64.2 1.6 %collective-permute-start.25 = (bf16[128,512]{1,0:T(8,128)(2,1)S(1)}, bf16[128,512]{1,0:T(8,128)(2,1)S(1)}, u32[]{:S(2)}, u32[]{:S(2)}) collective-permute-start(bf16[128,512]{1,0:T(8,128)(2,1)S(1)} %shard_map.75.refs_2_), channel_id=1, source_target_pairs={{0,8},{1,9},{2,10},{3,11},{4,12},{5,13},{6,14},{7,15},{8,16},{9,17... | collective-permute-start | bytes 393224 | tf_op jit(solution)/shard_map/ppermute | solution.py:343
  66.4 1.6 %collective-permute-start.23 = (bf16[128,512]{1,0:T(8,128)(2,1)S(1)}, bf16[128,512]{1,0:T(8,128)(2,1)S(1)}, u32[]{:S(2)}, u32[]{:S(2)}) collective-permute-start(bf16[128,512]{1,0:T(8,128)(2,1)S(1)} %shard_map.74.refs_3_), channel_id=1, source_target_pairs={{0,8},{1,9},{2,10},{3,11},{4,12},{5,13},{6,14},{7,15},{8,16},{9,17... | collective-permute-start | bytes 393224 | tf_op jit(solution)/shard_map/ppermute | solution.py:343
  76.3 1.6 %collective-permute-start.35 = (bf16[128,512]{1,0:T(8,128)(2,1)S(1)}, bf16[128,512]{1,0:T(8,128)(2,1)S(1)}, u32[]{:S(2)}, u32[]{:S(2)}) collective-permute-start(bf16[128,512]{1,0:T(8,128)(2,1)S(1)} %get-tuple-element.96), channel_id=1, source_target_pairs={{16,18},{17,19},{18,20},{19,21},{20,22},{21,23},{2,0},{3,1},{4,2},... | collective-permute-start | bytes 393224 | tf_op jit(solution)/shard_map/ppermute | solution.py:321
  78.9 4.2 %collective-permute-done.37.came = bf16[128,512]{1,0:T(8,128)(2,1)S(1)} collective-permute-done((bf16[128,512]{1,0:T(8,128)(2,1)S(1)}, bf16[128,512]{1,0:T(8,128)(2,1)S(1)}, u32[]{:S(2)}, u32[]{:S(2)}) %collective-permute-start.37) | collective-permute-done | bytes 131104 | tf_op jit(solution)/shard_map/ppermute | solution.py:321
  83.2 2.4 %collective-permute-start.38 = (bf16[128,512]{1,0:T(8,128)(2,1)S(1)}, bf16[128,512]{1,0:T(8,128)(2,1)S(1)}, u32[]{:S(2)}, u32[]{:S(2)}) collective-permute-start(bf16[128,512]{1,0:T(8,128)(2,1)S(1)} %shard_map.85.refs_1_), channel_id=1, source_target_pairs={{0,8},{1,9},{2,10},{3,11},{4,12},{5,13},{6,14},{7,15},{8,0},{9,1},... | collective-permute-start | bytes 393224 | tf_op jit(solution)/shard_map/ppermute | solution.py:343
  86.0 2.4 %collective-permute-start.36 = (bf16[128,512]{1,0:T(8,128)(2,1)S(1)}, bf16[128,512]{1,0:T(8,128)(2,1)S(1)}, u32[]{:S(2)}, u32[]{:S(2)}) collective-permute-start(bf16[128,512]{1,0:T(8,128)(2,1)S(1)} %shard_map.84.refs_0_), channel_id=1, source_target_pairs={{0,8},{1,9},{2,10},{3,11},{4,12},{5,13},{6,14},{7,15},{8,0},{9,1},... | collective-permute-start | bytes 393224 | tf_op jit(solution)/shard_map/ppermute | solution.py:343
  88.8 2.4 %collective-permute-start.34 = (bf16[128,512]{1,0:T(8,128)(2,1)S(1)}, bf16[128,512]{1,0:T(8,128)(2,1)S(1)}, u32[]{:S(2)}, u32[]{:S(2)}) collective-permute-start(bf16[128,512]{1,0:T(8,128)(2,1)S(1)} %shard_map.83.refs_2_), channel_id=1, source_target_pairs={{0,8},{1,9},{2,10},{3,11},{4,12},{5,13},{6,14},{7,15},{8,0},{9,1},... | collective-permute-start | bytes 393224 | tf_op jit(solution)/shard_map/ppermute | solution.py:343
  91.3 2.2 %collective-permute-start.32 = (bf16[128,512]{1,0:T(8,128)(2,1)S(1)}, bf16[128,512]{1,0:T(8,128)(2,1)S(1)}, u32[]{:S(2)}, u32[]{:S(2)}) collective-permute-start(bf16[128,512]{1,0:T(8,128)(2,1)S(1)} %shard_map.82.refs_3_), channel_id=1, source_target_pairs={{0,8},{1,9},{2,10},{3,11},{4,12},{5,13},{6,14},{7,15},{8,0},{9,1},... | collective-permute-start | bytes 393224 | tf_op jit(solution)/shard_map/ppermute | solution.py:343
  99.4 1.9 %collective-permute-start.42 = (bf16[336,512]{1,0:T(8,128)(2,1)S(1)}, bf16[336,512]{1,0:T(8,128)(2,1)S(1)}, u32[]{:S(2)}, u32[]{:S(2)}) collective-permute-start(bf16[336,512]{1,0:T(8,128)(2,1)S(1)} %add_convert_fusion), channel_id=1, source_target_pairs={{24,26},{25,27},{26,28},{27,29},{28,30},{29,31}} | collective-permute-start | bytes 1032200 | tf_op jit(solution)/shard_map/ppermute | solution.py:321
  101.4 3.0 %collective-permute-start.40 = (bf16[176,512]{1,0:T(8,128)(2,1)S(1)}, bf16[176,512]{1,0:T(8,128)(2,1)S(1)}, u32[]{:S(2)}, u32[]{:S(2)}) collective-permute-start(bf16[176,512]{1,0:T(8,128)(2,1)S(1)} %add_convert_fusion.1), channel_id=1, source_target_pairs={{24,26},{25,27},{26,28},{27,29},{28,30},{29,31}} | collective-permute-start | bytes 540680 | tf_op jit(solution)/shard_map/ppermute | solution.py:321
  105.5 6.8 %collective-permute-done.42.came = bf16[336,512]{1,0:T(8,128)(2,1)S(1)} collective-permute-done((bf16[336,512]{1,0:T(8,128)(2,1)S(1)}, bf16[336,512]{1,0:T(8,128)(2,1)S(1)}, u32[]{:S(2)}, u32[]{:S(2)}) %collective-permute-start.42) | collective-permute-done | bytes 344096 | tf_op jit(solution)/shard_map/ppermute | solution.py:321
  113.2 2.1 %collective-permute-done.40.came = bf16[176,512]{1,0:T(8,128)(2,1)S(1)} collective-permute-done((bf16[176,512]{1,0:T(8,128)(2,1)S(1)}, bf16[176,512]{1,0:T(8,128)(2,1)S(1)}, u32[]{:S(2)}, u32[]{:S(2)}) %collective-permute-start.40) | collective-permute-done | bytes 180256 | tf_op jit(solution)/shard_map/ppermute | solution.py:321
  (120 shorter events, 59.3 us)
Async XLA Ops:
  6.4 6.4 %collective-permute-start.7 = (bf16[128,512]{1,0:T(8,128)(2,1)S(1)}, bf16[128,512]{1,0:T(8,128)(2,1)S(1)}, u32[]{:S(2)}, u32[]{:S(2)}) collective-permute-start(bf16[128,512]{1,0:T(8,128)(2,1)S(1)} %get-tuple-element.120), channel_id=1, source_target_pairs={{0,2},{1,3},{2,4},{3,5},{4,6},{5,7},{18,16},{19,17},{20,18},{21,19... | collective-permute-start | bytes 393224 | tf_op jit(solution)/shard_map/ppermute | solution.py:321
  6.9 8.7 %collective-permute-start.10 = (bf16[128,512]{1,0:T(8,128)(2,1)S(1)}, bf16[128,512]{1,0:T(8,128)(2,1)S(1)}, u32[]{:S(2)}, u32[]{:S(2)}) collective-permute-start(bf16[128,512]{1,0:T(8,128)(2,1)S(1)} %get-tuple-element.119), channel_id=1, source_target_pairs={{0,2},{1,3},{2,4},{3,5},{4,6},{5,7},{18,16},{19,17},{20,18},{21,19... | collective-permute-start | bytes 393224 | tf_op jit(solution)/shard_map/ppermute | solution.py:321
  7.4 11.0 %collective-permute-start.4 = (bf16[128,512]{1,0:T(8,128)(2,1)S(1)}, bf16[128,512]{1,0:T(8,128)(2,1)S(1)}, u32[]{:S(2)}, u32[]{:S(2)}) collective-permute-start(bf16[128,512]{1,0:T(8,128)(2,1)S(1)} %get-tuple-element.121), channel_id=1, source_target_pairs={{0,2},{1,3},{2,4},{3,5},{4,6},{5,7},{18,16},{19,17},{20,18},{21,19... | collective-permute-start | bytes 393224 | tf_op jit(solution)/shard_map/ppermute | solution.py:321
  9.8 10.5 %collective-permute-start.1 = (bf16[128,512]{1,0:T(8,128)(2,1)S(1)}, bf16[128,512]{1,0:T(8,128)(2,1)S(1)}, u32[]{:S(2)}, u32[]{:S(2)}) collective-permute-start(bf16[128,512]{1,0:T(8,128)(2,1)S(1)} %get-tuple-element.122), channel_id=1, source_target_pairs={{0,2},{1,3},{2,4},{3,5},{4,6},{5,7},{18,16},{19,17},{20,18},{21,19... | collective-permute-start | bytes 393224 | tf_op jit(solution)/shard_map/ppermute | solution.py:321
  12.9 8.1 %collective-permute-start.8 = (bf16[128,512]{1,0:T(8,128)(2,1)S(1)}, bf16[128,512]{1,0:T(8,128)(2,1)S(1)}, u32[]{:S(2)}, u32[]{:S(2)}) collective-permute-start(bf16[128,512]{1,0:T(8,128)(2,1)S(1)} %shard_map.60.refs_0_), channel_id=1, source_target_pairs={{0,8},{1,9},{2,10},{3,11},{4,12},{5,13},{6,14},{7,15},{8,0},{9,1},... | collective-permute-start | bytes 393224 | tf_op jit(solution)/shard_map/ppermute | solution.py:343
  29.1 6.4 %collective-permute-start.19 = (bf16[128,512]{1,0:T(8,128)(2,1)S(1)}, bf16[128,512]{1,0:T(8,128)(2,1)S(1)}, u32[]{:S(2)}, u32[]{:S(2)}) collective-permute-start(bf16[128,512]{1,0:T(8,128)(2,1)S(1)} %get-tuple-element.103), channel_id=1, source_target_pairs={{0,2},{1,3},{2,4},{3,5},{4,6},{5,7},{6,0},{7,1},{8,10},{9,11},{10,... | collective-permute-start | bytes 393224 | tf_op jit(solution)/shard_map/ppermute | solution.py:321
  30.7 7.6 %collective-permute-start.17 = (bf16[128,512]{1,0:T(8,128)(2,1)S(1)}, bf16[128,512]{1,0:T(8,128)(2,1)S(1)}, u32[]{:S(2)}, u32[]{:S(2)}) collective-permute-start(bf16[128,512]{1,0:T(8,128)(2,1)S(1)} %get-tuple-element.104), channel_id=1, source_target_pairs={{0,2},{1,3},{2,4},{3,5},{4,6},{5,7},{6,0},{7,1},{8,10},{9,11},{10,... | collective-permute-start | bytes 393224 | tf_op jit(solution)/shard_map/ppermute | solution.py:321
  32.3 8.8 %collective-permute-start.15 = (bf16[128,512]{1,0:T(8,128)(2,1)S(1)}, bf16[128,512]{1,0:T(8,128)(2,1)S(1)}, u32[]{:S(2)}, u32[]{:S(2)}) collective-permute-start(bf16[128,512]{1,0:T(8,128)(2,1)S(1)} %get-tuple-element.105), channel_id=1, source_target_pairs={{0,2},{1,3},{2,4},{3,5},{4,6},{5,7},{6,0},{7,1},{8,10},{9,11},{10,... | collective-permute-start | bytes 393224 | tf_op jit(solution)/shard_map/ppermute | solution.py:321
  32.5 10.6 %collective-permute-start.13 = (bf16[128,512]{1,0:T(8,128)(2,1)S(1)}, bf16[128,512]{1,0:T(8,128)(2,1)S(1)}, u32[]{:S(2)}, u32[]{:S(2)}) collective-permute-start(bf16[128,512]{1,0:T(8,128)(2,1)S(1)} %get-tuple-element.106), channel_id=1, source_target_pairs={{0,2},{1,3},{2,4},{3,5},{4,6},{5,7},{6,0},{7,1},{8,10},{9,11},{10,... | collective-permute-start | bytes 393224 | tf_op jit(solution)/shard_map/ppermute | solution.py:321
  35.6 8.1 %collective-permute-start.20 = (bf16[128,512]{1,0:T(8,128)(2,1)S(1)}, bf16[128,512]{1,0:T(8,128)(2,1)S(1)}, u32[]{:S(2)}, u32[]{:S(2)}) collective-permute-start(bf16[128,512]{1,0:T(8,128)(2,1)S(1)} %shard_map.69.refs_1_), channel_id=1, source_target_pairs={{0,8},{1,9},{2,10},{3,11},{4,12},{5,13},{6,14},{7,15},{8,16},{9,17... | collective-permute-start | bytes 393224 | tf_op jit(solution)/shard_map/ppermute | solution.py:343
  51.8 6.7 %collective-permute-start.28 = (bf16[128,512]{1,0:T(8,128)(2,1)S(1)}, bf16[128,512]{1,0:T(8,128)(2,1)S(1)}, u32[]{:S(2)}, u32[]{:S(2)}) collective-permute-start(bf16[128,512]{1,0:T(8,128)(2,1)S(1)} %get-tuple-element.99), channel_id=1, source_target_pairs={{0,2},{1,3},{2,4},{3,5},{4,6},{5,7},{6,0},{7,1},{8,10},{9,11},{10,... | collective-permute-start | bytes 393224 | tf_op jit(solution)/shard_map/ppermute | solution.py:321
  53.4 7.8 %collective-permute-start.26 = (bf16[128,512]{1,0:T(8,128)(2,1)S(1)}, bf16[128,512]{1,0:T(8,128)(2,1)S(1)}, u32[]{:S(2)}, u32[]{:S(2)}) collective-permute-start(bf16[128,512]{1,0:T(8,128)(2,1)S(1)} %get-tuple-element.100), channel_id=1, source_target_pairs={{0,2},{1,3},{2,4},{3,5},{4,6},{5,7},{6,0},{7,1},{8,10},{9,11},{10,... | collective-permute-start | bytes 393224 | tf_op jit(solution)/shard_map/ppermute | solution.py:321
  55.0 9.1 %collective-permute-start.24 = (bf16[128,512]{1,0:T(8,128)(2,1)S(1)}, bf16[128,512]{1,0:T(8,128)(2,1)S(1)}, u32[]{:S(2)}, u32[]{:S(2)}) collective-permute-start(bf16[128,512]{1,0:T(8,128)(2,1)S(1)} %get-tuple-element.101), channel_id=1, source_target_pairs={{0,2},{1,3},{2,4},{3,5},{4,6},{5,7},{6,0},{7,1},{8,10},{9,11},{10,... | collective-permute-start | bytes 393224 | tf_op jit(solution)/shard_map/ppermute | solution.py:321
  57.0 9.3 %collective-permute-start.22 = (bf16[128,512]{1,0:T(8,128)(2,1)S(1)}, bf16[128,512]{1,0:T(8,128)(2,1)S(1)}, u32[]{:S(2)}, u32[]{:S(2)}) collective-permute-start(bf16[128,512]{1,0:T(8,128)(2,1)S(1)} %get-tuple-element.102), channel_id=1, source_target_pairs={{0,2},{1,3},{2,4},{3,5},{4,6},{5,7},{6,0},{7,1},{8,10},{9,11},{10,... | collective-permute-start | bytes 393224 | tf_op jit(solution)/shard_map/ppermute | solution.py:321
  58.5 9.5 %collective-permute-start.29 = (bf16[128,512]{1,0:T(8,128)(2,1)S(1)}, bf16[128,512]{1,0:T(8,128)(2,1)S(1)}, u32[]{:S(2)}, u32[]{:S(2)}) collective-permute-start(bf16[128,512]{1,0:T(8,128)(2,1)S(1)} %shard_map.77.refs_1_), channel_id=1, source_target_pairs={{0,8},{1,9},{2,10},{3,11},{4,12},{5,13},{6,14},{7,15},{8,16},{9,17... | collective-permute-start | bytes 393224 | tf_op jit(solution)/shard_map/ppermute | solution.py:343
  61.3 6.7 %collective-permute-start.27 = (bf16[128,512]{1,0:T(8,128)(2,1)S(1)}, bf16[128,512]{1,0:T(8,128)(2,1)S(1)}, u32[]{:S(2)}, u32[]{:S(2)}) collective-permute-start(bf16[128,512]{1,0:T(8,128)(2,1)S(1)} %shard_map.76.refs_0_), channel_id=1, source_target_pairs={{0,8},{1,9},{2,10},{3,11},{4,12},{5,13},{6,14},{7,15},{8,16},{9,17... | collective-permute-start | bytes 393224 | tf_op jit(solution)/shard_map/ppermute | solution.py:343
  74.9 8.2 %collective-permute-start.37 = (bf16[128,512]{1,0:T(8,128)(2,1)S(1)}, bf16[128,512]{1,0:T(8,128)(2,1)S(1)}, u32[]{:S(2)}, u32[]{:S(2)}) collective-permute-start(bf16[128,512]{1,0:T(8,128)(2,1)S(1)} %get-tuple-element.95), channel_id=1, source_target_pairs={{16,18},{17,19},{18,20},{19,21},{20,22},{21,23},{2,0},{3,1},{4,2},... | collective-permute-start | bytes 393224 | tf_op jit(solution)/shard_map/ppermute | solution.py:321
  76.3 9.6 %collective-permute-start.35 = (bf16[128,512]{1,0:T(8,128)(2,1)S(1)}, bf16[128,512]{1,0:T(8,128)(2,1)S(1)}, u32[]{:S(2)}, u32[]{:S(2)}) collective-permute-start(bf16[128,512]{1,0:T(8,128)(2,1)S(1)} %get-tuple-element.96), channel_id=1, source_target_pairs={{16,18},{17,19},{18,20},{19,21},{20,22},{21,23},{2,0},{3,1},{4,2},... | collective-permute-start | bytes 393224 | tf_op jit(solution)/shard_map/ppermute | solution.py:321
  77.9 10.9 %collective-permute-start.33 = (bf16[128,512]{1,0:T(8,128)(2,1)S(1)}, bf16[128,512]{1,0:T(8,128)(2,1)S(1)}, u32[]{:S(2)}, u32[]{:S(2)}) collective-permute-start(bf16[128,512]{1,0:T(8,128)(2,1)S(1)} %get-tuple-element.97), channel_id=1, source_target_pairs={{16,18},{17,19},{18,20},{19,21},{20,22},{21,23},{2,0},{3,1},{4,2},... | collective-permute-start | bytes 393224 | tf_op jit(solution)/shard_map/ppermute | solution.py:321
  78.4 12.9 %collective-permute-start.31 = (bf16[128,512]{1,0:T(8,128)(2,1)S(1)}, bf16[128,512]{1,0:T(8,128)(2,1)S(1)}, u32[]{:S(2)}, u32[]{:S(2)}) collective-permute-start(bf16[128,512]{1,0:T(8,128)(2,1)S(1)} %get-tuple-element.98), channel_id=1, source_target_pairs={{16,18},{17,19},{18,20},{19,21},{20,22},{21,23},{2,0},{3,1},{4,2},... | collective-permute-start | bytes 393224 | tf_op jit(solution)/shard_map/ppermute | solution.py:321
  83.2 10.3 %collective-permute-start.38 = (bf16[128,512]{1,0:T(8,128)(2,1)S(1)}, bf16[128,512]{1,0:T(8,128)(2,1)S(1)}, u32[]{:S(2)}, u32[]{:S(2)}) collective-permute-start(bf16[128,512]{1,0:T(8,128)(2,1)S(1)} %shard_map.85.refs_1_), channel_id=1, source_target_pairs={{0,8},{1,9},{2,10},{3,11},{4,12},{5,13},{6,14},{7,15},{8,0},{9,1},... | collective-permute-start | bytes 393224 | tf_op jit(solution)/shard_map/ppermute | solution.py:343
  86.0 7.5 %collective-permute-start.36 = (bf16[128,512]{1,0:T(8,128)(2,1)S(1)}, bf16[128,512]{1,0:T(8,128)(2,1)S(1)}, u32[]{:S(2)}, u32[]{:S(2)}) collective-permute-start(bf16[128,512]{1,0:T(8,128)(2,1)S(1)} %shard_map.84.refs_0_), channel_id=1, source_target_pairs={{0,8},{1,9},{2,10},{3,11},{4,12},{5,13},{6,14},{7,15},{8,0},{9,1},... | collective-permute-start | bytes 393224 | tf_op jit(solution)/shard_map/ppermute | solution.py:343
  99.4 12.8 %collective-permute-start.42 = (bf16[336,512]{1,0:T(8,128)(2,1)S(1)}, bf16[336,512]{1,0:T(8,128)(2,1)S(1)}, u32[]{:S(2)}, u32[]{:S(2)}) collective-permute-start(bf16[336,512]{1,0:T(8,128)(2,1)S(1)} %add_convert_fusion), channel_id=1, source_target_pairs={{24,26},{25,27},{26,28},{27,29},{28,30},{29,31}} | collective-permute-start | bytes 1032200 | tf_op jit(solution)/shard_map/ppermute | solution.py:321
  101.4 13.9 %collective-permute-start.40 = (bf16[176,512]{1,0:T(8,128)(2,1)S(1)}, bf16[176,512]{1,0:T(8,128)(2,1)S(1)}, u32[]{:S(2)}, u32[]{:S(2)}) collective-permute-start(bf16[176,512]{1,0:T(8,128)(2,1)S(1)} %add_convert_fusion.1), channel_id=1, source_target_pairs={{24,26},{25,27},{26,28},{27,29},{28,30},{29,31}} | collective-permute-start | bytes 540680 | tf_op jit(solution)/shard_map/ppermute | solution.py:321
  (23 other events, 110.8 us)

commit v8 on v6

--- a/solution.py
+++ b/solution.py
@@ -9,7 +9,7 @@
 
 PARTS = (8, 8, 8, 8)
 CHUNKS = len(PARTS)
-JOINED = (0, 2, 3)
+JOINED = (0, 1, 3)
 LAST_PARTS = (21, 11)
 AXES = ("site", "sector")
 LIMIT = 20 << 20

time: 117 us -> 117 us (level)
  transfers between devices with their start and end apart: 52 -> 52, of which waited for: 29 -> 26; matrix products, arithmetic and copies ran while one was open for 0% -> 0% of each run, Pallas kernels for 17% -> 17%
where the time goes in v8:
time: 117 us
  starting transfers between devices  49.4 us (42%)
  waiting for transfers between devices  38.7 us (33%)
  Pallas kernels  27 us (23%)
    ppermute x18, waiting for transfers between devices, per_device(): came = lax.ppermute(up, AXES, up_pairs(step))  31.7 us
    ppermute x18, starting transfers between devices, per_device(): came = lax.ppermute(up, AXES, up_pairs(step))  23.3 us
    ppermute x16, starting transfers between devices, per_device(): held = [lax.ppermute(rows, AXES, next_pairs(step)) for rows in fresh]  21.2 us
    pallas_call x16, Pallas kernels, chunk(): call(functools.partial(step_kernel, step, cuts[start], end - start, fresh...  16.8 us
    ppermute x16, waiting for transfers between devices, per_device(): held = [lax.ppermute(rows, AXES, next_pairs(step)) for rows in fresh]  6.22 us
    ppermute x18, starting transfers between devices, swapped(): return [lax.ppermute(part, AXES, swap_pairs) for part in parts]  4.88 us
    pallas_call x1, Pallas kernels, per_device(): call(functools.partial(open_kernel, first, later, cuts), [pl.BlockSpec(me...  3.69 us
  transfers between devices with their start and end apart: 52, of which 26 were waited for; matrix products, arithmetic and copies ran while one was open for 0% of the time, Pallas kernels for 17%

profile of v8, /device:TPU:14, one launch (start us, length us, event | category | flops | bytes accessed | tf_op | source)
XLA Modules:
  0.0 116.5 jit_solution(5619854827224344592)
XLA Ops:
  0.0 3.7 %shard_map.55 = (bf16[128,512]{1,0:T(8,128)(2,1)S(1)}, bf16[128,512]{1,0:T(8,128)(2,1)}, bf16[128,512]{1,0:T(8,128)(2,1)S(1)}, bf16[128,512]{1,0:T(8,128)(2,1)},...) custom-call(s32[5,8]{1,0:T(8,128)} %dims.1, s32[4]{0:T(128)} %bitcast.1, ...), custom_call_target="tpu_custom_call" | custom-call | flops 1073741824 | tf_op jit(solution)/shard_map/pallas_call | solution.py:264
  9.8 1.6 %collective-permute-start.1 = (bf16[128,512]{1,0:T(8,128)(2,1)S(1)}, bf16[128,512]{1,0:T(8,128)(2,1)S(1)}, u32[]{:S(2)}, u32[]{:S(2)}) collective-permute-start(bf16[128,512]{1,0:T(8,128)(2,1)S(1)} %get-tuple-element.134), channel_id=1, source_target_pairs={{0,2},{1,3},{2,4},{3,5},{4,6},{5,7},{18,16},{19,17},{20,18},{21,19... | collective-permute-start | bytes 393224 | tf_op jit(solution)/shard_map/ppermute | solution.py:319
  13.5 2.1 %collective-permute-done.4.came = bf16[128,512]{1,0:T(8,128)(2,1)S(1)} collective-permute-done((bf16[128,512]{1,0:T(8,128)(2,1)S(1)}, bf16[128,512]{1,0:T(8,128)(2,1)S(1)}, u32[]{:S(2)}, u32[]{:S(2)}) %collective-permute-start.4) | collective-permute-done | bytes 131104 | tf_op jit(solution)/shard_map/ppermute | solution.py:319
  16.3 2.1 %collective-permute-done.7.came = bf16[128,512]{1,0:T(8,128)(2,1)S(1)} collective-permute-done((bf16[128,512]{1,0:T(8,128)(2,1)S(1)}, bf16[128,512]{1,0:T(8,128)(2,1)S(1)}, u32[]{:S(2)}, u32[]{:S(2)}) %collective-permute-start.7) | collective-permute-done | bytes 131104 | tf_op jit(solution)/shard_map/ppermute | solution.py:319
  22.4 2.5 %collective-permute-done.8.refs_2_ = bf16[128,512]{1,0:T(8,128)(2,1)S(1)} collective-permute-done((bf16[128,512]{1,0:T(8,128)(2,1)S(1)}, bf16[128,512]{1,0:T(8,128)(2,1)S(1)}, u32[]{:S(2)}, u32[]{:S(2)}) %collective-permute-start.8) | collective-permute-done | bytes 131104 | tf_op jit(solution)/shard_map/ppermute | solution.py:341
  29.3 1.6 %collective-permute-start.22 = (bf16[128,512]{1,0:T(8,128)(2,1)S(1)}, bf16[128,512]{1,0:T(8,128)(2,1)S(1)}, u32[]{:S(2)}, u32[]{:S(2)}) collective-permute-start(bf16[128,512]{1,0:T(8,128)(2,1)S(1)} %get-tuple-element.127), channel_id=1, source_target_pairs={{0,2},{1,3},{2,4},{3,5},{4,6},{5,7},{6,0},{7,1},{8,10},{9,11},{10,... | collective-permute-start | bytes 393224 | tf_op jit(solution)/shard_map/ppermute | solution.py:319
  36.3 2.2 %collective-permute-done.19.came = bf16[128,512]{1,0:T(8,128)(2,1)S(1)} collective-permute-done((bf16[128,512]{1,0:T(8,128)(2,1)S(1)}, bf16[128,512]{1,0:T(8,128)(2,1)S(1)}, u32[]{:S(2)}, u32[]{:S(2)}) %collective-permute-start.19) | collective-permute-done | bytes 131104 | tf_op jit(solution)/shard_map/ppermute | solution.py:319
  39.1 2.2 %collective-permute-done.16.came = bf16[128,512]{1,0:T(8,128)(2,1)S(1)} collective-permute-done((bf16[128,512]{1,0:T(8,128)(2,1)S(1)}, bf16[128,512]{1,0:T(8,128)(2,1)S(1)}, u32[]{:S(2)}, u32[]{:S(2)}) %collective-permute-start.16) | collective-permute-done | bytes 131104 | tf_op jit(solution)/shard_map/ppermute | solution.py:319
  45.4 1.8 %collective-permute-done.17.refs_0_ = bf16[128,512]{1,0:T(8,128)(2,1)S(1)} collective-permute-done((bf16[128,512]{1,0:T(8,128)(2,1)S(1)}, bf16[128,512]{1,0:T(8,128)(2,1)S(1)}, u32[]{:S(2)}, u32[]{:S(2)}) %collective-permute-start.17) | collective-permute-done | bytes 131104 | tf_op jit(solution)/shard_map/ppermute | solution.py:341
  52.1 1.6 %collective-permute-start.34 = (bf16[128,512]{1,0:T(8,128)(2,1)S(1)}, bf16[128,512]{1,0:T(8,128)(2,1)S(1)}, u32[]{:S(2)}, u32[]{:S(2)}) collective-permute-start(bf16[128,512]{1,0:T(8,128)(2,1)S(1)} %get-tuple-element.123), channel_id=1, source_target_pairs={{0,2},{1,3},{2,4},{3,5},{4,6},{5,7},{6,0},{7,1},{8,10},{9,11},{10,... | collective-permute-start | bytes 393224 | tf_op jit(solution)/shard_map/ppermute | solution.py:319
  55.3 2.0 %collective-permute-start.28 = (bf16[128,512]{1,0:T(8,128)(2,1)S(1)}, bf16[128,512]{1,0:T(8,128)(2,1)S(1)}, u32[]{:S(2)}, u32[]{:S(2)}) collective-permute-start(bf16[128,512]{1,0:T(8,128)(2,1)S(1)} %get-tuple-element.125), channel_id=1, source_target_pairs={{0,2},{1,3},{2,4},{3,5},{4,6},{5,7},{6,0},{7,1},{8,10},{9,11},{10,... | collective-permute-start | bytes 393224 | tf_op jit(solution)/shard_map/ppermute | solution.py:319
  58.8 1.8 %collective-permute-start.35 = (bf16[128,512]{1,0:T(8,128)(2,1)S(1)}, bf16[128,512]{1,0:T(8,128)(2,1)S(1)}, u32[]{:S(2)}, u32[]{:S(2)}) collective-permute-start(bf16[128,512]{1,0:T(8,128)(2,1)S(1)} %shard_map.77.refs_0_), channel_id=1, source_target_pairs={{0,8},{1,9},{2,10},{3,11},{4,12},{5,13},{6,14},{7,15},{8,16},{9,17... | collective-permute-start | bytes 393224 | tf_op jit(solution)/shard_map/ppermute | solution.py:341
  61.6 1.8 %collective-permute-start.32 = (bf16[128,512]{1,0:T(8,128)(2,1)S(1)}, bf16[128,512]{1,0:T(8,128)(2,1)S(1)}, u32[]{:S(2)}, u32[]{:S(2)}) collective-permute-start(bf16[128,512]{1,0:T(8,128)(2,1)S(1)} %shard_map.76.refs_2_), channel_id=1, source_target_pairs={{0,8},{1,9},{2,10},{3,11},{4,12},{5,13},{6,14},{7,15},{8,16},{9,17... | collective-permute-start | bytes 393224 | tf_op jit(solution)/shard_map/ppermute | solution.py:341
  64.5 1.8 %collective-permute-start.29 = (bf16[128,512]{1,0:T(8,128)(2,1)S(1)}, bf16[128,512]{1,0:T(8,128)(2,1)S(1)}, u32[]{:S(2)}, u32[]{:S(2)}) collective-permute-start(bf16[128,512]{1,0:T(8,128)(2,1)S(1)} %shard_map.75.refs_1_), channel_id=1, source_target_pairs={{0,8},{1,9},{2,10},{3,11},{4,12},{5,13},{6,14},{7,15},{8,16},{9,17... | collective-permute-start | bytes 393224 | tf_op jit(solution)/shard_map/ppermute | solution.py:341
  66.9 1.8 %collective-permute-start.26 = (bf16[128,512]{1,0:T(8,128)(2,1)S(1)}, bf16[128,512]{1,0:T(8,128)(2,1)S(1)}, u32[]{:S(2)}, u32[]{:S(2)}) collective-permute-start(bf16[128,512]{1,0:T(8,128)(2,1)S(1)} %shard_map.74.refs_3_), channel_id=1, source_target_pairs={{0,8},{1,9},{2,10},{3,11},{4,12},{5,13},{6,14},{7,15},{8,16},{9,17... | collective-permute-start | bytes 393224 | tf_op jit(solution)/shard_map/ppermute | solution.py:341
  79.1 4.3 %collective-permute-done.46.came = bf16[128,512]{1,0:T(8,128)(2,1)S(1)} collective-permute-done((bf16[128,512]{1,0:T(8,128)(2,1)S(1)}, bf16[128,512]{1,0:T(8,128)(2,1)S(1)}, u32[]{:S(2)}, u32[]{:S(2)}) %collective-permute-start.46) | collective-permute-done | bytes 131104 | tf_op jit(solution)/shard_map/ppermute | solution.py:319
  83.5 2.4 %collective-permute-start.47 = (bf16[128,512]{1,0:T(8,128)(2,1)S(1)}, bf16[128,512]{1,0:T(8,128)(2,1)S(1)}, u32[]{:S(2)}, u32[]{:S(2)}) collective-permute-start(bf16[128,512]{1,0:T(8,128)(2,1)S(1)} %shard_map.85.refs_0_), channel_id=1, source_target_pairs={{0,8},{1,9},{2,10},{3,11},{4,12},{5,13},{6,14},{7,15},{8,0},{9,1},... | collective-permute-start | bytes 393224 | tf_op jit(solution)/shard_map/ppermute | solution.py:341
  86.3 2.4 %collective-permute-start.44 = (bf16[128,512]{1,0:T(8,128)(2,1)S(1)}, bf16[128,512]{1,0:T(8,128)(2,1)S(1)}, u32[]{:S(2)}, u32[]{:S(2)}) collective-permute-start(bf16[128,512]{1,0:T(8,128)(2,1)S(1)} %shard_map.84.refs_2_), channel_id=1, source_target_pairs={{0,8},{1,9},{2,10},{3,11},{4,12},{5,13},{6,14},{7,15},{8,0},{9,1},... | collective-permute-start | bytes 393224 | tf_op jit(solution)/shard_map/ppermute | solution.py:341
  89.1 2.4 %collective-permute-start.41 = (bf16[128,512]{1,0:T(8,128)(2,1)S(1)}, bf16[128,512]{1,0:T(8,128)(2,1)S(1)}, u32[]{:S(2)}, u32[]{:S(2)}) collective-permute-start(bf16[128,512]{1,0:T(8,128)(2,1)S(1)} %shard_map.83.refs_1_), channel_id=1, source_target_pairs={{0,8},{1,9},{2,10},{3,11},{4,12},{5,13},{6,14},{7,15},{8,0},{9,1},... | collective-permute-start | bytes 393224 | tf_op jit(solution)/shard_map/ppermute | solution.py:341
  91.6 2.3 %collective-permute-start.38 = (bf16[128,512]{1,0:T(8,128)(2,1)S(1)}, bf16[128,512]{1,0:T(8,128)(2,1)S(1)}, u32[]{:S(2)}, u32[]{:S(2)}) collective-permute-start(bf16[128,512]{1,0:T(8,128)(2,1)S(1)} %shard_map.82.refs_3_), channel_id=1, source_target_pairs={{0,8},{1,9},{2,10},{3,11},{4,12},{5,13},{6,14},{7,15},{8,0},{9,1},... | collective-permute-start | bytes 393224 | tf_op jit(solution)/shard_map/ppermute | solution.py:341
  99.7 1.9 %collective-permute-start.51 = (bf16[336,512]{1,0:T(8,128)(2,1)S(1)}, bf16[336,512]{1,0:T(8,128)(2,1)S(1)}, u32[]{:S(2)}, u32[]{:S(2)}) collective-permute-start(bf16[336,512]{1,0:T(8,128)(2,1)S(1)} %add_convert_fusion), channel_id=1, source_target_pairs={{24,26},{25,27},{26,28},{27,29},{28,30},{29,31}} | collective-permute-start | bytes 1032200 | tf_op jit(solution)/shard_map/ppermute | solution.py:319
  101.7 2.9 %collective-permute-start.49 = (bf16[176,512]{1,0:T(8,128)(2,1)S(1)}, bf16[176,512]{1,0:T(8,128)(2,1)S(1)}, u32[]{:S(2)}, u32[]{:S(2)}) collective-permute-start(bf16[176,512]{1,0:T(8,128)(2,1)S(1)} %add_convert_fusion.1), channel_id=1, source_target_pairs={{24,26},{25,27},{26,28},{27,29},{28,30},{29,31}} | collective-permute-start | bytes 540680 | tf_op jit(solution)/shard_map/ppermute | solution.py:319
  105.7 6.8 %collective-permute-done.51.came = bf16[336,512]{1,0:T(8,128)(2,1)S(1)} collective-permute-done((bf16[336,512]{1,0:T(8,128)(2,1)S(1)}, bf16[336,512]{1,0:T(8,128)(2,1)S(1)}, u32[]{:S(2)}, u32[]{:S(2)}) %collective-permute-start.51) | collective-permute-done | bytes 344096 | tf_op jit(solution)/shard_map/ppermute | solution.py:319
  113.5 2.1 %collective-permute-done.49.came = bf16[176,512]{1,0:T(8,128)(2,1)S(1)} collective-permute-done((bf16[176,512]{1,0:T(8,128)(2,1)S(1)}, bf16[176,512]{1,0:T(8,128)(2,1)S(1)}, u32[]{:S(2)}, u32[]{:S(2)}) %collective-permute-start.49) | collective-permute-done | bytes 180256 | tf_op jit(solution)/shard_map/ppermute | solution.py:319
  (135 shorter events, 57.7 us)
Async XLA Ops:
  6.9 8.7 %collective-permute-start.4 = (bf16[128,512]{1,0:T(8,128)(2,1)S(1)}, bf16[128,512]{1,0:T(8,128)(2,1)S(1)}, u32[]{:S(2)}, u32[]{:S(2)}) collective-permute-start(bf16[128,512]{1,0:T(8,128)(2,1)S(1)} %get-tuple-element.133), channel_id=1, source_target_pairs={{0,2},{1,3},{2,4},{3,5},{4,6},{5,7},{18,16},{19,17},{20,18},{21,19... | collective-permute-start | bytes 393224 | tf_op jit(solution)/shard_map/ppermute | solution.py:319
  7.4 11.0 %collective-permute-start.7 = (bf16[128,512]{1,0:T(8,128)(2,1)S(1)}, bf16[128,512]{1,0:T(8,128)(2,1)S(1)}, u32[]{:S(2)}, u32[]{:S(2)}) collective-permute-start(bf16[128,512]{1,0:T(8,128)(2,1)S(1)} %get-tuple-element.132), channel_id=1, source_target_pairs={{0,2},{1,3},{2,4},{3,5},{4,6},{5,7},{18,16},{19,17},{20,18},{21,19... | collective-permute-start | bytes 393224 | tf_op jit(solution)/shard_map/ppermute | solution.py:319
  9.8 10.5 %collective-permute-start.1 = (bf16[128,512]{1,0:T(8,128)(2,1)S(1)}, bf16[128,512]{1,0:T(8,128)(2,1)S(1)}, u32[]{:S(2)}, u32[]{:S(2)}) collective-permute-start(bf16[128,512]{1,0:T(8,128)(2,1)S(1)} %get-tuple-element.134), channel_id=1, source_target_pairs={{0,2},{1,3},{2,4},{3,5},{4,6},{5,7},{18,16},{19,17},{20,18},{21,19... | collective-permute-start | bytes 393224 | tf_op jit(solution)/shard_map/ppermute | solution.py:319
  12.9 8.1 %collective-permute-start.11 = (bf16[128,512]{1,0:T(8,128)(2,1)S(1)}, bf16[128,512]{1,0:T(8,128)(2,1)S(1)}, u32[]{:S(2)}, u32[]{:S(2)}) collective-permute-start(bf16[128,512]{1,0:T(8,128)(2,1)S(1)} %shard_map.61.refs_0_), channel_id=1, source_target_pairs={{0,8},{1,9},{2,10},{3,11},{4,12},{5,13},{6,14},{7,15},{8,0},{9,1},... | collective-permute-start | bytes 393224 | tf_op jit(solution)/shard_map/ppermute | solution.py:341
  15.7 6.6 %collective-permute-start.5 = (bf16[128,512]{1,0:T(8,128)(2,1)S(1)}, bf16[128,512]{1,0:T(8,128)(2,1)S(1)}, u32[]{:S(2)}, u32[]{:S(2)}) collective-permute-start(bf16[128,512]{1,0:T(8,128)(2,1)S(1)} %shard_map.59.refs_1_), channel_id=1, source_target_pairs={{0,8},{1,9},{2,10},{3,11},{4,12},{5,13},{6,14},{7,15},{8,0},{9,1},... | collective-permute-start | bytes 393224 | tf_op jit(solution)/shard_map/ppermute | solution.py:341
  30.9 7.6 %collective-permute-start.19 = (bf16[128,512]{1,0:T(8,128)(2,1)S(1)}, bf16[128,512]{1,0:T(8,128)(2,1)S(1)}, u32[]{:S(2)}, u32[]{:S(2)}) collective-permute-start(bf16[128,512]{1,0:T(8,128)(2,1)S(1)} %get-tuple-element.128), channel_id=1, source_target_pairs={{0,2},{1,3},{2,4},{3,5},{4,6},{5,7},{6,0},{7,1},{8,10},{9,11},{10,... | collective-permute-start | bytes 393224 | tf_op jit(solution)/shard_map/ppermute | solution.py:319
  32.5 8.8 %collective-permute-start.16 = (bf16[128,512]{1,0:T(8,128)(2,1)S(1)}, bf16[128,512]{1,0:T(8,128)(2,1)S(1)}, u32[]{:S(2)}, u32[]{:S(2)}) collective-permute-start(bf16[128,512]{1,0:T(8,128)(2,1)S(1)} %get-tuple-element.129), channel_id=1, source_target_pairs={{0,2},{1,3},{2,4},{3,5},{4,6},{5,7},{6,0},{7,1},{8,10},{9,11},{10,... | collective-permute-start | bytes 393224 | tf_op jit(solution)/shard_map/ppermute | solution.py:319
  32.7 10.8 %collective-permute-start.13 = (bf16[128,512]{1,0:T(8,128)(2,1)S(1)}, bf16[128,512]{1,0:T(8,128)(2,1)S(1)}, u32[]{:S(2)}, u32[]{:S(2)}) collective-permute-start(bf16[128,512]{1,0:T(8,128)(2,1)S(1)} %get-tuple-element.130), channel_id=1, source_target_pairs={{0,2},{1,3},{2,4},{3,5},{4,6},{5,7},{6,0},{7,1},{8,10},{9,11},{10,... | collective-permute-start | bytes 393224 | tf_op jit(solution)/shard_map/ppermute | solution.py:319
  35.8 8.3 %collective-permute-start.23 = (bf16[128,512]{1,0:T(8,128)(2,1)S(1)}, bf16[128,512]{1,0:T(8,128)(2,1)S(1)}, u32[]{:S(2)}, u32[]{:S(2)}) collective-permute-start(bf16[128,512]{1,0:T(8,128)(2,1)S(1)} %shard_map.69.refs_0_), channel_id=1, source_target_pairs={{0,8},{1,9},{2,10},{3,11},{4,12},{5,13},{6,14},{7,15},{8,16},{9,17... | collective-permute-start | bytes 393224 | tf_op jit(solution)/shard_map/ppermute | solution.py:341
  38.6 6.8 %collective-permute-start.20 = (bf16[128,512]{1,0:T(8,128)(2,1)S(1)}, bf16[128,512]{1,0:T(8,128)(2,1)S(1)}, u32[]{:S(2)}, u32[]{:S(2)}) collective-permute-start(bf16[128,512]{1,0:T(8,128)(2,1)S(1)} %shard_map.68.refs_2_), channel_id=1, source_target_pairs={{0,8},{1,9},{2,10},{3,11},{4,12},{5,13},{6,14},{7,15},{8,16},{9,17... | collective-permute-start | bytes 393224 | tf_op jit(solution)/shard_map/ppermute | solution.py:341
  52.1 6.6 %collective-permute-start.34 = (bf16[128,512]{1,0:T(8,128)(2,1)S(1)}, bf16[128,512]{1,0:T(8,128)(2,1)S(1)}, u32[]{:S(2)}, u32[]{:S(2)}) collective-permute-start(bf16[128,512]{1,0:T(8,128)(2,1)S(1)} %get-tuple-element.123), channel_id=1, source_target_pairs={{0,2},{1,3},{2,4},{3,5},{4,6},{5,7},{6,0},{7,1},{8,10},{9,11},{10,... | collective-permute-start | bytes 393224 | tf_op jit(solution)/shard_map/ppermute | solution.py:319
  53.7 7.8 %collective-permute-start.31 = (bf16[128,512]{1,0:T(8,128)(2,1)S(1)}, bf16[128,512]{1,0:T(8,128)(2,1)S(1)}, u32[]{:S(2)}, u32[]{:S(2)}) collective-permute-start(bf16[128,512]{1,0:T(8,128)(2,1)S(1)} %get-tuple-element.124), channel_id=1, source_target_pairs={{0,2},{1,3},{2,4},{3,5},{4,6},{5,7},{6,0},{7,1},{8,10},{9,11},{10,... | collective-permute-start | bytes 393224 | tf_op jit(solution)/shard_map/ppermute | solution.py:319
  55.3 9.1 %collective-permute-start.28 = (bf16[128,512]{1,0:T(8,128)(2,1)S(1)}, bf16[128,512]{1,0:T(8,128)(2,1)S(1)}, u32[]{:S(2)}, u32[]{:S(2)}) collective-permute-start(bf16[128,512]{1,0:T(8,128)(2,1)S(1)} %get-tuple-element.125), channel_id=1, source_target_pairs={{0,2},{1,3},{2,4},{3,5},{4,6},{5,7},{6,0},{7,1},{8,10},{9,11},{10,... | collective-permute-start | bytes 393224 | tf_op jit(solution)/shard_map/ppermute | solution.py:319
  57.3 9.5 %collective-permute-start.25 = (bf16[128,512]{1,0:T(8,128)(2,1)S(1)}, bf16[128,512]{1,0:T(8,128)(2,1)S(1)}, u32[]{:S(2)}, u32[]{:S(2)}) collective-permute-start(bf16[128,512]{1,0:T(8,128)(2,1)S(1)} %get-tuple-element.126), channel_id=1, source_target_pairs={{0,2},{1,3},{2,4},{3,5},{4,6},{5,7},{6,0},{7,1},{8,10},{9,11},{10,... | collective-permute-start | bytes 393224 | tf_op jit(solution)/shard_map/ppermute | solution.py:319
  58.8 9.9 %collective-permute-start.35 = (bf16[128,512]{1,0:T(8,128)(2,1)S(1)}, bf16[128,512]{1,0:T(8,128)(2,1)S(1)}, u32[]{:S(2)}, u32[]{:S(2)}) collective-permute-start(bf16[128,512]{1,0:T(8,128)(2,1)S(1)} %shard_map.77.refs_0_), channel_id=1, source_target_pairs={{0,8},{1,9},{2,10},{3,11},{4,12},{5,13},{6,14},{7,15},{8,16},{9,17... | collective-permute-start | bytes 393224 | tf_op jit(solution)/shard_map/ppermute | solution.py:341
  61.6 8.3 %collective-permute-start.32 = (bf16[128,512]{1,0:T(8,128)(2,1)S(1)}, bf16[128,512]{1,0:T(8,128)(2,1)S(1)}, u32[]{:S(2)}, u32[]{:S(2)}) collective-permute-start(bf16[128,512]{1,0:T(8,128)(2,1)S(1)} %shard_map.76.refs_2_), channel_id=1, source_target_pairs={{0,8},{1,9},{2,10},{3,11},{4,12},{5,13},{6,14},{7,15},{8,16},{9,17... | collective-permute-start | bytes 393224 | tf_op jit(solution)/shard_map/ppermute | solution.py:341
  75.1 8.2 %collective-permute-start.46 = (bf16[128,512]{1,0:T(8,128)(2,1)S(1)}, bf16[128,512]{1,0:T(8,128)(2,1)S(1)}, u32[]{:S(2)}, u32[]{:S(2)}) collective-permute-start(bf16[128,512]{1,0:T(8,128)(2,1)S(1)} %get-tuple-element.119), channel_id=1, source_target_pairs={{16,18},{17,19},{18,20},{19,21},{20,22},{21,23},{2,0},{3,1},{4,2},... | collective-permute-start | bytes 393224 | tf_op jit(solution)/shard_map/ppermute | solution.py:319
  76.5 9.6 %collective-permute-start.43 = (bf16[128,512]{1,0:T(8,128)(2,1)S(1)}, bf16[128,512]{1,0:T(8,128)(2,1)S(1)}, u32[]{:S(2)}, u32[]{:S(2)}) collective-permute-start(bf16[128,512]{1,0:T(8,128)(2,1)S(1)} %get-tuple-element.120), channel_id=1, source_target_pairs={{16,18},{17,19},{18,20},{19,21},{20,22},{21,23},{2,0},{3,1},{4,2},... | collective-permute-start | bytes 393224 | tf_op jit(solution)/shard_map/ppermute | solution.py:319
  78.1 10.9 %collective-permute-start.40 = (bf16[128,512]{1,0:T(8,128)(2,1)S(1)}, bf16[128,512]{1,0:T(8,128)(2,1)S(1)}, u32[]{:S(2)}, u32[]{:S(2)}) collective-permute-start(bf16[128,512]{1,0:T(8,128)(2,1)S(1)} %get-tuple-element.121), channel_id=1, source_target_pairs={{16,18},{17,19},{18,20},{19,21},{20,22},{21,23},{2,0},{3,1},{4,2},... | collective-permute-start | bytes 393224 | tf_op jit(solution)/shard_map/ppermute | solution.py:319
  78.6 12.8 %collective-permute-start.37 = (bf16[128,512]{1,0:T(8,128)(2,1)S(1)}, bf16[128,512]{1,0:T(8,128)(2,1)S(1)}, u32[]{:S(2)}, u32[]{:S(2)}) collective-permute-start(bf16[128,512]{1,0:T(8,128)(2,1)S(1)} %get-tuple-element.122), channel_id=1, source_target_pairs={{16,18},{17,19},{18,20},{19,21},{20,22},{21,23},{2,0},{3,1},{4,2},... | collective-permute-start | bytes 393224 | tf_op jit(solution)/shard_map/ppermute | solution.py:319
  83.5 10.5 %collective-permute-start.47 = (bf16[128,512]{1,0:T(8,128)(2,1)S(1)}, bf16[128,512]{1,0:T(8,128)(2,1)S(1)}, u32[]{:S(2)}, u32[]{:S(2)}) collective-permute-start(bf16[128,512]{1,0:T(8,128)(2,1)S(1)} %shard_map.85.refs_0_), channel_id=1, source_target_pairs={{0,8},{1,9},{2,10},{3,11},{4,12},{5,13},{6,14},{7,15},{8,0},{9,1},... | collective-permute-start | bytes 393224 | tf_op jit(solution)/shard_map/ppermute | solution.py:341
  86.3 8.9 %collective-permute-start.44 = (bf16[128,512]{1,0:T(8,128)(2,1)S(1)}, bf16[128,512]{1,0:T(8,128)(2,1)S(1)}, u32[]{:S(2)}, u32[]{:S(2)}) collective-permute-start(bf16[128,512]{1,0:T(8,128)(2,1)S(1)} %shard_map.84.refs_2_), channel_id=1, source_target_pairs={{0,8},{1,9},{2,10},{3,11},{4,12},{5,13},{6,14},{7,15},{8,0},{9,1},... | collective-permute-start | bytes 393224 | tf_op jit(solution)/shard_map/ppermute | solution.py:341
  99.7 12.8 %collective-permute-start.51 = (bf16[336,512]{1,0:T(8,128)(2,1)S(1)}, bf16[336,512]{1,0:T(8,128)(2,1)S(1)}, u32[]{:S(2)}, u32[]{:S(2)}) collective-permute-start(bf16[336,512]{1,0:T(8,128)(2,1)S(1)} %add_convert_fusion), channel_id=1, source_target_pairs={{24,26},{25,27},{26,28},{27,29},{28,30},{29,31}} | collective-permute-start | bytes 1032200 | tf_op jit(solution)/shard_map/ppermute | solution.py:319
  101.7 13.9 %collective-permute-start.49 = (bf16[176,512]{1,0:T(8,128)(2,1)S(1)}, bf16[176,512]{1,0:T(8,128)(2,1)S(1)}, u32[]{:S(2)}, u32[]{:S(2)}) collective-permute-start(bf16[176,512]{1,0:T(8,128)(2,1)S(1)} %add_convert_fusion.1), channel_id=1, source_target_pairs={{24,26},{25,27},{26,28},{27,29},{28,30},{29,31}} | collective-permute-start | bytes 540680 | tf_op jit(solution)/shard_map/ppermute | solution.py:319
  (32 other events, 122.0 us)
